TPU v7x, 256 devices: a whole 4x4x8 slice. The times are simulated.
256 devices in a mesh: blk: 32 (over y, x, core), col: 8 (over z).
Axes of the slice: x: 4, y: 4, z: 8, core: 2. Of those that a mesh axis runs over, the one named last changes fastest.
Arguments:
- src_feat: bfloat16 [64, 1024, 256], P('blk', 'col'), may hold values from -40 to 40
- tgt_feat: bfloat16 [64, 1024, 256], P('blk', 'col'), may hold values from -40 to 40
- src_mass: bfloat16 [64, 1024], P('blk', 'col'), may hold values from 0.5 to 2
- tgt_mass: bfloat16 [64, 1024], P('blk', 'col'), may hold values from 0.5 to 2
- candidates: int32 [64, 8], P('blk'), may hold values from 0 to 63, as said below
- counts: int32 [64], P('blk'), may hold values from 1 to 8, as said below
- tgt_home: int32 [64], replicated, may hold values from 0 to 63, each once
Outputs:
- src_aligned: bfloat16 [64, 1024, 256], P('blk', 'col')
- tgt_aligned: bfloat16 [64, 1024, 256], P('blk', 'col')
Inputs may be any that keep to these rules, and one draw needn't show every extreme that they name: `candidates`: each row's 8 entries are distinct; the first counts[i] of row i are live, the others are not used; every target block number is among the live entries of some row. `counts`: the 2 blocks of one index of blk hold at most 12 live slots together, and the blocks of some index hold exactly 12. A permutation: target block number j is stored as block tgt_home[j] of tgt_feat and tgt_mass.
All inputs are finite; a program needn't handle non-finite values.
Results may differ from a plain program's by a relative error of at most 0.017.
Values may be sent and summed in bfloat16 or wider, within the bound.
No kernel may reach another device: no remote copies, remote signals or barrier semaphores. Data moves between devices by JAX's collectives and lax.ppermute only.
A program may use at most 64 MiB of HBM per device.

v0:
```python
import functools
import math

import jax
import jax.numpy as jnp
from jax import lax
from jax.experimental import pallas as pl
from jax.experimental.pallas import tpu as pltpu
from jax.sharding import PartitionSpec as P


PAIRS = 12
TEMP = 0.02
OFFSET = 0.3
EPS = 1e-06
F32 = jnp.float32
BF16 = jnp.bfloat16
SMEM = pl.BlockSpec(memory_space=pltpu.SMEM)
VMEM = pl.BlockSpec(memory_space=pltpu.VMEM)
ANY = pl.BlockSpec(memory_space=pl.ANY)
LIMIT = 16 * 1024 * 1024


def blk_perm(fn):
    pairs = []
    for i in range(32):
        y, x, k = fn(i // 8, (i // 2) % 4, i % 2)
        pairs.append((i, (y * 4 + x) * 2 + k))
    return pairs


def swap(v):
    return lax.ppermute(v, "blk", blk_perm(lambda y, x, k: (y, x, 1 - k)))


def over_x(v, d):
    return lax.ppermute(v, "blk", blk_perm(lambda y, x, k: (y, x ^ d, k)))


def over_y(v, d):
    return lax.ppermute(v, "blk", blk_perm(lambda y, x, k: (y ^ d, x, k)))


def over_first(v, d):
    return lax.ppermute(
        v, "blk", blk_perm(lambda y, x, k: (y, x ^ d, k) if k == 0 else (y ^ d, x, k))
    )


def over_second(v, d):
    return lax.ppermute(
        v, "blk", blk_perm(lambda y, x, k: (y ^ d, x, k) if k == 0 else (y, x ^ d, k))
    )


def over_z(v, d):
    return lax.ppermute(v, "col", [(i, i ^ d) for i in range(8)])


def ring(v):
    pairs = []
    for i in range(256):
        z = i % 8
        pairs.append((i, i - z + (z + (1 if (i // 8) % 2 == 0 else -1)) % 8))
    return lax.ppermute(v, ("blk", "col"), pairs)


def pick(core, zero, one):
    return jnp.where(core == 0, zero, one)


def gather_targets(tgt_feat, core):
    came = swap(tgt_feat)
    pair = pick(core, jnp.stack([tgt_feat[0], came[0]]), jnp.stack([came[1], tgt_feat[1]]))
    near = jnp.concatenate([pair] + [over_first(pair, d) for d in (1, 2, 3)])
    parts = [near] + [over_second(near, d) for d in (1, 2, 3)]
    return parts + [swap(p) for p in parts]


def gather_sources(src_feat, core):
    came = swap(src_feat)
    chunk = pick(core, jnp.concatenate([src_feat, came]), jnp.concatenate([came, src_feat]))
    one = ring(chunk)
    two = ring(one)
    three = ring(two)
    four = ring(pick(core, three[:2], three[2:]))
    give = jnp.concatenate([pick(core, c[2:], c[:2]) for c in (one, two)])
    return [src_feat, one, two, three, four, swap(give), swap(pick(core, three[2:], three[:2]))]


def col_sum_parts(v):
    v = v + over_z(v, 1)
    return (v,) + tuple(over_z(v, d) for d in (2, 6, 4))


def blk_sum_parts(v):
    v = v + swap(v.astype(BF16)).astype(F32)
    low = v.astype(BF16)
    v = v + sum(over_x(low, d).astype(F32) for d in (1, 3, 2))
    low = v.astype(BF16)
    parts = [v]
    for d in (1, 3, 2):
        parts.append(over_y(low, d))
    return parts


def reduce_targets(mine, came, core):
    q = (mine.astype(F32) + came.astype(F32)).astype(BF16).reshape(4, 8, 128, 256)
    s = q[0].astype(F32)
    for d in (1, 3, 2):
        s = s + over_first(q[d], d).astype(F32)
    s = s.astype(BF16).reshape(4, 2, 128, 256)
    t = s[0].astype(F32) + sum(over_second(s[d], d).astype(F32) for d in (1, 3, 2))
    keep = pick(core, t[0], t[1])
    came = swap(pick(core, t[1], t[0]).astype(BF16)).astype(F32)
    return pick(core, jnp.stack([keep, came]), jnp.stack([came, keep]))


def reduce_sources(own, keep, give, far, core):
    got = swap(give)

    def add(m, d):
        k, g = keep[d - 1].astype(F32), got[d - 1].astype(F32)
        m = m.astype(F32)
        return (pick(core, jnp.concatenate([k, g]), jnp.concatenate([g, k])) + m).astype(BF16)

    last = ring(far)
    none = jnp.zeros_like(last)
    moving = pick(core, jnp.concatenate([last, none]), jnp.concatenate([none, last]))
    for d in (3, 2, 1):
        moving = ring(add(moving, d))
    came = swap(pick(core, moving[2:], moving[:2]))
    return own.astype(F32) + pick(core, moving[:2], moving[2:]).astype(F32) + came.astype(F32)


def slot_of(meta, s):
    counts, candidates, home = meta
    first = counts[0]
    p = jnp.where(s >= first, 1, 0)
    return p, home[candidates[p, s - first * p]]


def live(meta):
    return meta[0][0] + meta[0][1]


def place():
    b = lax.axis_index("blk")
    return b, lax.axis_index("col"), b // 8, (b // 2) % 4, b % 2


def unit(rows):
    x = rows.astype(F32)
    return (x * lax.rsqrt(jnp.mean(x * x, axis=-1, keepdims=True) + EPS)).astype(BF16)


def two_rows(v):
    high = v.astype(BF16).astype(F32)
    row = lax.broadcasted_iota(jnp.int32, (16, v.shape[1]), 0)
    return jnp.where(row == 0, high, jnp.where(row == 1, v - high, 0.0)).astype(BF16)


def build_kernel(*refs):
    meta, refs = refs[:3], refs[3:]
    own, one, two, three, four, far12, far3 = refs[:7]
    tgt = refs[7:15]
    mass, kt, tiles, raw, rows, unit_src, acc, sems, row_sems = refs[15:]
    n = live(meta)
    _, z, my_y, my_x, my_k = place()
    sign = 2 * my_k - 1
    chunks = []
    for p in range(2):
        chunks.append((own.at[p], z, p))
        for d, ref in ((1, one), (2, two), (3, three)):
            chunks.append((ref.at[2 * my_k + p], z + sign * d, p))
        chunks.append((four.at[p], z + 4, p))
        chunks.append((far12.at[p], z - sign, p))
        chunks.append((far12.at[2 + p], z - sign * 2, p))
        chunks.append((far3.at[p], z - sign * 3, p))
    copies = []
    for c, (ref, at, p) in enumerate(chunks):
        at = pl.multiple_of((at & 7) * 128, 128)
        copies.append((pltpu.make_async_copy(ref, raw.at[p, pl.ds(at, 128), :], row_sems.at[c]), at, p))
        copies[-1][0].start()

    def fetch(s, _):
        _, j = slot_of(meta, s)
        i, owner = j % 2, j // 2
        dy, dx = (owner // 8) ^ my_y, ((owner // 2) % 4) ^ my_x
        first, second = jnp.where(i == 0, dx, dy), jnp.where(i == 0, dy, dx)
        array = second + jnp.where(i == my_k, 0, 4)
        at = first * 2 + owner % 2
        for a in range(8):

            @pl.when(array == a)
            def _():
                pltpu.make_async_copy(tgt[a].at[at], tiles.at[s], sems.at[s]).start()

        return 0

    lax.fori_loop(0, n, fetch, 0)
    for copy, at, p in copies:
        copy.wait()
        unit_src[p, pl.ds(at, 128), :] = unit(raw[p, pl.ds(at, 128), :])
    acc[...] = jnp.zeros_like(acc)
    scale = math.log2(math.e) / (256 * TEMP)
    shift = OFFSET / TEMP * math.log2(math.e)

    def step(s, _):
        p, _ = slot_of(meta, s)
        pltpu.make_async_copy(tgt[0].at[0], tiles.at[s], sems.at[s]).wait()
        tile = unit(tiles[s])
        for c in range(4):
            cols = slice(c * 256, (c + 1) * 256)
            score = lax.dot_general(
                tile, unit_src[p, cols, :], (((1,), (1,)), ((), ())), preferred_element_type=F32
            )
            k = jnp.exp2(score * scale - shift)
            kt[s, :, cols] = k.astype(BF16)
            acc[p, :, cols] += k.reshape(16, 8, 256).sum(axis=0)
        return 0

    lax.fori_loop(0, n, step, 0)
    lane = lax.broadcasted_iota(jnp.int32, (1, 1024), 1) // 128
    for p in range(2):
        rows[p : p + 1, :] = jnp.sum(acc[p], axis=0, keepdims=True)
        own = jnp.concatenate([mass[p : p + 1, :].astype(F32)] * 8, axis=1)
        rows[2 + p : 3 + p, :] = jnp.where(lane == z, own, 0.0)


def col_kernel(first, *refs):
    meta, refs = refs[:3], refs[3:]
    if first:
        kt, r0, r1, r2, r3, tgt_mass, out, mass_out, u_rows = refs
        total = (r0[...] + r1[...]) + (r2[...] + r3[...])
        mass = total[2:4]
        mass_out[...] = mass
    else:
        kt, r0, r1, r2, r3, mass_in, out, u_out, u_rows = refs
        total = (r0[...] + r1[...]) + (r2[...] + r3[...])
        mass = mass_in[...]
    u = mass / total[0:2]
    if not first:
        u_out[...] = u
    for p in range(2):
        u_rows[p] = two_rows(u[p : p + 1])
    out[...] = jnp.zeros_like(out)

    def step(s, _):
        p, j = slot_of(meta, s)
        part = lax.dot_general(
            u_rows[p], kt[s], (((1,), (1,)), ((), ())), preferred_element_type=F32
        )
        out[pl.ds(j, 1), :] += part[0:1] + part[1:2]
        return 0

    lax.fori_loop(0, live(meta), step, 0)
    if first:
        b = place()[0]
        out[pl.ds(64 + 2 * b, 1), :] = tgt_mass[0:1, :].astype(F32)
        out[pl.ds(65 + 2 * b, 1), :] = tgt_mass[1:2, :].astype(F32)


def row_kernel(*refs):
    meta, refs = refs[:3], refs[3:]
    kt, c0, c1, c2, c3, out, mass_out, v_all, acc = refs
    total = c0[...] + c1[...].astype(F32) + c2[...].astype(F32) + c3[...].astype(F32)
    mass_out[...] = total[64:]
    v_all[...] = total[64:] / total[:64]
    acc[...] = jnp.zeros_like(acc)

    def step(s, _):
        p, j = slot_of(meta, s)
        v = two_rows(v_all[pl.ds(j, 1), :])
        acc[p] += jnp.dot(v, kt[s], preferred_element_type=F32)[:8]
        return 0

    lax.fori_loop(0, live(meta), step, 0)
    for p in range(2):
        out[p : p + 1, :] = acc[p, 0:1, :] + acc[p, 1:2, :]


def back_kernel(*refs):
    meta, refs = refs[:3], refs[3:]
    kt, u, raw, mine, other = refs
    _, _, my_y, my_x, my_k = place()
    mine[...] = jnp.zeros_like(mine)
    other[...] = jnp.zeros_like(other)

    def step(s, _):
        p, j = slot_of(meta, s)
        row = jnp.where(p == 0, u[0:1, :], u[1:2, :])
        plan = (kt[s].astype(F32) * row).astype(BF16)
        back = jnp.dot(plan, raw[p], preferred_element_type=F32)
        i, owner = j % 2, j // 2
        dy, dx = (owner // 8) ^ my_y, ((owner // 2) % 4) ^ my_x
        at = jnp.where(i == 0, dx * 8 + dy * 2, dy * 8 + dx * 2) + owner % 2

        @pl.when(i == my_k)
        def _():
            mine[at] = (mine[at].astype(F32) + back).astype(BF16)

        @pl.when(i != my_k)
        def _():
            other[at] = (other[at].astype(F32) + back).astype(BF16)

        return 0

    lax.fori_loop(0, live(meta), step, 0)


def toward_kernel(*refs):
    meta, refs = refs[:3], refs[3:]
    kt, u, tiles, c0, c1, c2, c3, mass, own, keep, give, far, v_out, v_all, acc = refs
    total = c0[...] + c1[...].astype(F32) + c2[...].astype(F32) + c3[...].astype(F32)
    v_all[...] = mass[...] / total
    b, z = place()[:2]
    v_out[0:1, :] = v_all[pl.ds(2 * b, 1), :]
    v_out[1:2, :] = v_all[pl.ds(2 * b + 1, 1), :]
    acc[...] = jnp.zeros_like(acc)

    def step(s, _):
        p, j = slot_of(meta, s)
        v = jnp.broadcast_to(v_all[pl.ds(j, 1), :], (128, 128)).T
        row = jnp.where(p == 0, u[0:1, :], u[1:2, :])
        plan = []
        for c in range(8):
            cols = slice(c * 128, (c + 1) * 128)
            plan.append((kt[s, :, cols].astype(F32) * row[:, cols] * v).astype(BF16))
        plan = jnp.concatenate(plan, axis=1)
        acc[p] += lax.dot_general(
            plan, tiles[s], (((0,), (0,)), ((), ())), preferred_element_type=F32
        )
        return 0

    lax.fori_loop(0, live(meta), step, 0)
    sign = 1 - 2 * (b % 2)
    for p in range(2):
        for ref, d in ((own, 0), (far, 4)):
            at = pl.multiple_of(((z + d) & 7) * 128, 128)
            ref[p] = acc[p, pl.ds(at, 128), :].astype(BF16)
        for ref, way in ((keep, sign), (give, -sign)):
            for d in (1, 2, 3):
                at = pl.multiple_of(((z + way * d) & 7) * 128, 128)
                ref[d - 1, p] = acc[p, pl.ds(at, 128), :].astype(BF16)


def call(kernel, out_shape, in_specs, scratch, args, flops, nbytes):
    return pl.pallas_call(
        kernel,
        out_shape=out_shape,
        in_specs=in_specs,
        out_specs=[VMEM] * len(out_shape),
        scratch_shapes=scratch,
        compiler_params=pltpu.CompilerParams(vmem_limit_bytes=LIMIT),
        cost_estimate=pl.CostEstimate(flops=flops, bytes_accessed=nbytes, transcendentals=0),
    )(*args)


def program(src_feat, tgt_feat, src_mass, tgt_mass, candidates, counts, tgt_home):
    core = lax.axis_index("blk") % 2
    meta = (counts, candidates, tgt_home)
    sources = gather_sources(src_feat, core)
    targets = gather_targets(tgt_feat, core)
    S = jax.ShapeDtypeStruct
    kt, tiles, raw, rows = call(
        build_kernel,
        [
            S((PAIRS, 128, 1024), BF16),
            S((PAIRS, 128, 256), BF16),
            S((2, 1024, 256), BF16),
            S((4, 1024), F32),
        ],
        [SMEM] * 3 + [ANY] * 15 + [VMEM],
        [
            pltpu.VMEM((2, 1024, 256), BF16),
            pltpu.VMEM((2, 8, 1024), F32),
            pltpu.SemaphoreType.DMA((PAIRS,)),
            pltpu.SemaphoreType.DMA((16,)),
        ],
        (*meta, *sources, *targets, src_mass),
        800_000_000,
        7_000_000,
    )
    sums, mass_src = call(
        functools.partial(col_kernel, True),
        [S((128, 128), F32), S((2, 1024), F32)],
        [SMEM] * 3 + [VMEM] * 6,
        [pltpu.VMEM((2, 16, 1024), BF16)],
        (*meta, kt, *col_sum_parts(rows), tgt_mass),
        100_000_000,
        3_000_000,
    )
    rows, mass_tgt = call(
        row_kernel,
        [S((2, 1024), F32), S((64, 128), F32)],
        [SMEM] * 3 + [VMEM] * 5,
        [pltpu.VMEM((64, 128), F32), pltpu.VMEM((2, 8, 1024), F32)],
        (*meta, kt, *blk_sum_parts(sums)),
        100_000_000,
        3_000_000,
    )
    sums, u = call(
        functools.partial(col_kernel, False),
        [S((64, 128), F32), S((2, 1024), F32)],
        [SMEM] * 3 + [VMEM] * 6,
        [pltpu.VMEM((2, 16, 1024), BF16)],
        (*meta, kt, *col_sum_parts(rows), mass_src),
        100_000_000,
        3_000_000,
    )
    mine, other = call(
        back_kernel,
        [S((32, 128, 256), BF16)] * 2,
        [SMEM] * 3 + [VMEM] * 3,
        [],
        (*meta, kt, u, raw),
        800_000_000,
        8_000_000,
    )
    came = swap(other)
    parts = blk_sum_parts(sums)
    tgt_own = reduce_targets(mine, came, core)
    own, keep, give, far, v = call(
        toward_kernel,
        [S((2, 128, 256), BF16)]
        + [S((3, 2, 128, 256), BF16)] * 2
        + [S((2, 128, 256), BF16), S((2, 128), F32)],
        [SMEM] * 3 + [VMEM] * 8,
        [pltpu.VMEM((64, 128), F32), pltpu.VMEM((2, 1024, 256), F32)],
        (*meta, kt, u, tiles, *parts, mass_tgt),
        800_000_000,
        6_000_000,
    )
    src_own = reduce_sources(own, keep, give, far, core)
    src_aligned = (src_own / src_mass.astype(F32)[:, :, None]).astype(BF16)
    tgt_aligned = (tgt_own * v[:, :, None] / tgt_mass.astype(F32)[:, :, None]).astype(BF16)
    return (src_aligned, tgt_aligned)


def solution(mesh):
    in_specs = (
        P("blk", "col", None),
        P("blk", "col", None),
        P("blk", "col"),
        P("blk", "col"),
        P("blk", None),
        P("blk"),
        P(),
    )
    out_specs = (P("blk", "col", None), P("blk", "col", None))
    return jax.shard_map(program, mesh=mesh, in_specs=in_specs, out_specs=out_specs, check_vma=False)
```

profile of v0, /device:TPU:97, one launch (start us, length us, event | category | flops | bytes accessed | tf_op | source)
XLA Modules:
  0.0 171.3 jit_solution(8281356854875091131)
XLA Ops:
  2.6 2.8 %collective-permute-start.10 = (bf16[2,128,256]{2,1,0:T(8,128)(2,1)S(1)}, bf16[2,128,256]{2,1,0:T(8,128)(2,1)S(1)}, u32[]{:S(2)}, u32[]{:S(2)}) collective-permute-start(bf16[2,128,256]{2,1,0:T(8,128)(2,1)S(1)} %maximum_select_fusion.5), channel_id=1, source_target_pairs={{0,48},{8,200},{16,32},{24,216},{32,16},{40,232},{48,0},{56,248},{... | collective-permute-start | bytes 393224 | tf_op jit(solution)/shard_map/ppermute | solution.py:45
  12.2 2.7 %collective-permute-start.12 = (bf16[8,128,256]{2,1,0:T(8,128)(2,1)S(1)}, bf16[8,128,256]{2,1,0:T(8,128)(2,1)S(1)}, u32[]{:S(2)}, u32[]{:S(2)}) collective-permute-start(bf16[8,128,256]{2,1,0:T(8,128)(2,1)S(1)} %pad_maximum_fusion.refs_10_), channel_id=1, source_target_pairs={{0,128},{8,40},{16,144},{24,56},{32,160},{40,8},{48,176},{56,24},{... | collective-permute-start | bytes 1572872 | tf_op jit(solution)/shard_map/ppermute | solution.py:51
  15.1 5.4 %collective-permute-start.14 = (bf16[8,128,256]{2,1,0:T(8,128)(2,1)S(1)}, bf16[8,128,256]{2,1,0:T(8,128)(2,1)S(1)}, u32[]{:S(2)}, u32[]{:S(2)}) collective-permute-start(bf16[8,128,256]{2,1,0:T(8,128)(2,1)S(1)} %pad_maximum_fusion.refs_10_), channel_id=1, source_target_pairs={{0,8},{8,0},{16,24},{24,16},{32,40},{40,32},{48,56},{56,48},{64,72... | collective-permute-start | bytes 1572872 | tf_op jit(solution)/shard_map/ppermute | solution.py:33
  22.0 6.1 %collective-permute-start.15 = (bf16[8,128,256]{2,1,0:T(8,128)(2,1)S(1)}, bf16[8,128,256]{2,1,0:T(8,128)(2,1)S(1)}, u32[]{:S(2)}, u32[]{:S(2)}) collective-permute-start(bf16[8,128,256]{2,1,0:T(8,128)(2,1)S(1)} %collective-permute-done.11.refs_11_), channel_id=1, source_target_pairs={{0,8},{8,0},{16,24},{24,16},{32,40},{40,32},{48,56},{56,48},{64,72... | collective-permute-start | bytes 1572872 | tf_op jit(solution)/shard_map/ppermute | solution.py:33
  30.1 3.1 %collective-permute-start.17 = (bf16[8,128,256]{2,1,0:T(8,128)(2,1)S(1)}, bf16[8,128,256]{2,1,0:T(8,128)(2,1)S(1)}, u32[]{:S(2)}, u32[]{:S(2)}) collective-permute-start(bf16[8,128,256]{2,1,0:T(8,128)(2,1)S(1)} %collective-permute-done.13.refs_13_), channel_id=1, source_target_pairs={{0,8},{8,0},{16,24},{24,16},{32,40},{40,32},{48,56},{56,48},{64,72... | collective-permute-start | bytes 1572872 | tf_op jit(solution)/shard_map/ppermute | solution.py:33
  38.8 5.2 %shard_map.86 = (bf16[12,128,1024]{2,1,0:T(8,128)(2,1)S(1)}, bf16[12,128,256]{2,1,0:T(8,128)(2,1)S(1)}, bf16[2,1024,256]{2,1,0:T(8,128)(2,1)S(1)}, f32[4,1024]{1,0:T(4,128)S(1)}) custom-call(s32[2]{0:T(128)S(1)} %copy-done.2, s32[2,8]{1,0:T(2,128)S(1)} %copy-done.1, s32[64]{0:T(128)S(1)} %copy-done.3, bf16[2,128,256]{2,1,0:T(8,128)(2,1)S(1)} %copy-done, ...), custom_call_target="tpu_custom_call" | custom-call | flops 800000000 | bytes 7000000 | tf_op jit(solution)/shard_map/pallas_call | solution.py:349
  44.0 2.6 %collective-permute-done.18 = f32[4,1024]{1,0:T(4,128)S(1)} collective-permute-done((f32[4,1024]{1,0:T(4,128)S(1)}, f32[4,1024]{1,0:T(4,128)S(1)}, u32[]{:S(2)}, u32[]{:S(2)}) %collective-permute-start.18) | collective-permute-done | bytes 16416 | tf_op jit(solution)/shard_map/ppermute | solution.py:57
  46.7 4.3 %collective-permute-start.20 = (f32[4,1024]{1,0:T(4,128)S(1)}, f32[4,1024]{1,0:T(4,128)S(1)}, u32[]{:S(2)}, u32[]{:S(2)}) collective-permute-start(f32[4,1024]{1,0:T(4,128)S(1)} %add.75.refs_4_), channel_id=1, source_target_pairs={{0,6},{1,7},{2,4},{3,5},{4,2},{5,3},{6,0},{7,1},{8,14},{9,15},{10,... | collective-permute-start | bytes 49160 | tf_op jit(solution)/shard_map/ppermute | solution.py:57
  52.3 5.1 %collective-permute-done.21.refs_7_ = f32[4,1024]{1,0:T(4,128)S(1)} collective-permute-done((f32[4,1024]{1,0:T(4,128)S(1)}, f32[4,1024]{1,0:T(4,128)S(1)}, u32[]{:S(2)}, u32[]{:S(2)}) %collective-permute-start.21) | collective-permute-done | bytes 16416 | tf_op jit(solution)/shard_map/ppermute | solution.py:57
  58.4 3.4 %collective-permute-start.22 = (bf16[128,128]{1,0:T(8,128)(2,1)S(1)}, bf16[128,128]{1,0:T(8,128)(2,1)S(1)}, u32[]{:S(2)}, u32[]{:S(2)}) collective-permute-start(bf16[128,128]{1,0:T(8,128)(2,1)S(1)} %convert_element_type.160), channel_id=1, source_target_pairs={{0,8},{8,0},{16,24},{24,16},{32,40},{40,32},{48,56},{56,48},{64,72... | collective-permute-start | bytes 98312 | tf_op jit(solution)/shard_map/ppermute | solution.py:33
  62.7 3.0 %collective-permute-start.23 = (bf16[128,128]{1,0:T(8,128)(2,1)S(1)}, bf16[128,128]{1,0:T(8,128)(2,1)S(1)}, u32[]{:S(2)}, u32[]{:S(2)}) collective-permute-start(bf16[128,128]{1,0:T(8,128)(2,1)S(1)} %fusion.13), channel_id=1, source_target_pairs={{0,16},{8,24},{16,0},{24,8},{32,48},{40,56},{48,32},{56,40},{64,80... | collective-permute-start | bytes 98312 | tf_op jit(solution)/shard_map/ppermute | solution.py:37
  80.4 2.5 %collective-permute-start.30 = (f32[2,1024]{1,0:T(2,128)S(1)}, f32[2,1024]{1,0:T(2,128)S(1)}, u32[]{:S(2)}, u32[]{:S(2)}) collective-permute-start(f32[2,1024]{1,0:T(2,128)S(1)} %add.80.refs_4_), channel_id=1, source_target_pairs={{0,2},{1,3},{2,0},{3,1},{4,6},{5,7},{6,4},{7,5},{8,10},{9,11},{10,... | collective-permute-start | bytes 24584 | tf_op jit(solution)/shard_map/ppermute | solution.py:57
  87.5 2.8 %collective-permute-done.32.refs_7_ = f32[2,1024]{1,0:T(2,128)S(1)} collective-permute-done((f32[2,1024]{1,0:T(2,128)S(1)}, f32[2,1024]{1,0:T(2,128)S(1)}, u32[]{:S(2)}, u32[]{:S(2)}) %collective-permute-start.32) | collective-permute-done | bytes 8224 | tf_op jit(solution)/shard_map/ppermute | solution.py:57
  92.6 6.5 %collective-permute-start.46 = (bf16[32,128,256]{2,1,0:T(8,128)(2,1)S(1)}, bf16[32,128,256]{2,1,0:T(8,128)(2,1)S(1)}, u32[]{:S(2)}, u32[]{:S(2)}) collective-permute-start(bf16[32,128,256]{2,1,0:T(8,128)(2,1)S(1)} %get-tuple-element.34), channel_id=1, source_target_pairs={{0,8},{8,0},{16,24},{24,16},{32,40},{40,32},{48,56},{56,48},{64,72... | collective-permute-start | bytes 6291464 | tf_op jit(solution)/shard_map/ppermute | solution.py:33
  99.2 3.7 %collective-permute-done.33 = bf16[64,128]{1,0:T(8,128)(2,1)S(1)} collective-permute-done((bf16[64,128]{1,0:T(8,128)(2,1)S(1)}, bf16[64,128]{1,0:T(8,128)(2,1)S(1)}, u32[]{:S(2)}, u32[]{:S(2)}) %collective-permute-start.33) | collective-permute-done | bytes 16416 | tf_op jit(solution)/shard_map/ppermute | solution.py:33
  109.4 2.9 %collective-permute-start.38 = (bf16[64,128]{1,0:T(8,128)(2,1)S(1)}, bf16[64,128]{1,0:T(8,128)(2,1)S(1)}, u32[]{:S(2)}, u32[]{:S(2)}) collective-permute-start(bf16[64,128]{1,0:T(8,128)(2,1)S(1)} %get-tuple-element.36), channel_id=1, source_target_pairs={{0,192},{8,200},{16,208},{24,216},{32,224},{40,232},{48,240},{56,2... | collective-permute-start | bytes 49160 | tf_op jit(solution)/shard_map/ppermute | solution.py:41
  113.5 3.0 %collective-permute-done.39.refs_9_ = bf16[64,128]{1,0:T(8,128)(2,1)S(1)} collective-permute-done((bf16[64,128]{1,0:T(8,128)(2,1)S(1)}, bf16[64,128]{1,0:T(8,128)(2,1)S(1)}, u32[]{:S(2)}, u32[]{:S(2)}) %collective-permute-start.39) | collective-permute-done | bytes 16416 | tf_op jit(solution)/shard_map/ppermute | solution.py:41
  118.1 3.7 %collective-permute-start.40 = (bf16[3,2,128,256]{3,2,1,0:T(8,128)(2,1)S(1)}, bf16[3,2,128,256]{3,2,1,0:T(8,128)(2,1)S(1)}, u32[]{:S(2)}, u32[]{:S(2)}) collective-permute-start(bf16[3,2,128,256]{3,2,1,0:T(8,128)(2,1)S(1)} %get-tuple-element.30), channel_id=1, source_target_pairs={{0,8},{8,0},{16,24},{24,16},{32,40},{40,32},{48,56},{56,48},{64,72... | collective-permute-start | bytes 1179656 | tf_op jit(solution)/shard_map/ppermute | solution.py:33
  123.2 4.3 %collective-permute-done.41 = bf16[2,128,256]{2,1,0:T(8,128)(2,1)S(1)} collective-permute-done((bf16[2,128,256]{2,1,0:T(8,128)(2,1)S(1)}, bf16[2,128,256]{2,1,0:T(8,128)(2,1)S(1)}, u32[]{:S(2)}, u32[]{:S(2)}) %collective-permute-start.41) | collective-permute-done | bytes 131104 | tf_op jit(solution)/shard_map/ppermute | solution.py:65
  127.7 6.4 %collective-permute-done.42 = bf16[4,128,256]{2,1,0:T(8,128)(2,1)S(1)} collective-permute-done((bf16[4,128,256]{2,1,0:T(8,128)(2,1)S(1)}, bf16[4,128,256]{2,1,0:T(8,128)(2,1)S(1)}, u32[]{:S(2)}, u32[]{:S(2)}) %collective-permute-start.42) | collective-permute-done | bytes 262176 | tf_op jit(solution)/shard_map/ppermute | solution.py:65
  140.9 6.7 %collective-permute-done.44 = bf16[4,128,256]{2,1,0:T(8,128)(2,1)S(1)} collective-permute-done((bf16[4,128,256]{2,1,0:T(8,128)(2,1)S(1)}, bf16[4,128,256]{2,1,0:T(8,128)(2,1)S(1)}, u32[]{:S(2)}, u32[]{:S(2)}) %collective-permute-start.44) | collective-permute-done | bytes 262176 | tf_op jit(solution)/shard_map/ppermute | solution.py:65
  147.6 4.0 %collective-permute-start.45 = (bf16[2,128,256]{2,1,0:T(8,128)(2,1)S(1)}, bf16[2,128,256]{2,1,0:T(8,128)(2,1)S(1)}, u32[]{:S(2)}, u32[]{:S(2)}) collective-permute-start(bf16[2,128,256]{2,1,0:T(8,128)(2,1)S(1)} %broadcast_select_fusion), channel_id=1, source_target_pairs={{0,8},{8,0},{16,24},{24,16},{32,40},{40,32},{48,56},{56,48},{64,72... | collective-permute-start | bytes 393224 | tf_op jit(solution)/shard_map/ppermute | solution.py:33
  156.6 4.3 %collective-permute-done.51 = bf16[2,128,256]{2,1,0:T(8,128)(2,1)S(1)} collective-permute-done((bf16[2,128,256]{2,1,0:T(8,128)(2,1)S(1)}, bf16[2,128,256]{2,1,0:T(8,128)(2,1)S(1)}, u32[]{:S(2)}, u32[]{:S(2)}) %collective-permute-start.51) | collective-permute-done | bytes 131104 | tf_op jit(solution)/shard_map/ppermute | solution.py:51
  161.0 8.6 %collective-permute-start.53 = (bf16[128,256]{1,0:T(8,128)(2,1)S(1)}, bf16[128,256]{1,0:T(8,128)(2,1)S(1)}, u32[]{:S(2)}, u32[]{:S(2)}) collective-permute-start(bf16[128,256]{1,0:T(8,128)(2,1)S(1)} %fusion.12), channel_id=1, source_target_pairs={{0,8},{8,0},{16,24},{24,16},{32,40},{40,32},{48,56},{56,48},{64,72... | collective-permute-start | bytes 196616 | tf_op jit(solution)/shard_map/ppermute | solution.py:33
  (137 shorter events, 67.2 us)
Async XLA Ops:
  7.8 7.3 %collective-permute-start.1 = (bf16[4,128,256]{2,1,0:T(8,128)(2,1)S(1)}, bf16[4,128,256]{2,1,0:T(8,128)(2,1)S(1)}, u32[]{:S(2)}, u32[]{:S(2)}) collective-permute-start(bf16[4,128,256]{2,1,0:T(8,128)(2,1)S(1)} %maximum_select_fusion.3), channel_id=1, source_target_pairs={{0,1},{1,2},{2,3},{3,4},{4,5},{5,6},{6,7},{7,0},{8,15},{9,8},{10,9... | collective-permute-start | bytes 786440 | tf_op jit(solution)/shard_map/ppermute | solution.py:65
  11.1 10.9 %collective-permute-start.11 = (bf16[8,128,256]{2,1,0:T(8,128)(2,1)S(1)}, bf16[8,128,256]{2,1,0:T(8,128)(2,1)S(1)}, u32[]{:S(2)}, u32[]{:S(2)}) collective-permute-start(bf16[8,128,256]{2,1,0:T(8,128)(2,1)S(1)} %pad_maximum_fusion.refs_10_), channel_id=1, source_target_pairs={{0,64},{8,24},{16,80},{24,8},{32,96},{40,56},{48,112},{56,40},{64,... | collective-permute-start | bytes 1572872 | tf_op jit(solution)/shard_map/ppermute | solution.py:51
  12.2 16.0 %collective-permute-start.12 = (bf16[8,128,256]{2,1,0:T(8,128)(2,1)S(1)}, bf16[8,128,256]{2,1,0:T(8,128)(2,1)S(1)}, u32[]{:S(2)}, u32[]{:S(2)}) collective-permute-start(bf16[8,128,256]{2,1,0:T(8,128)(2,1)S(1)} %pad_maximum_fusion.refs_10_), channel_id=1, source_target_pairs={{0,128},{8,40},{16,144},{24,56},{32,160},{40,8},{48,176},{56,24},{... | collective-permute-start | bytes 1572872 | tf_op jit(solution)/shard_map/ppermute | solution.py:51
  14.9 15.2 %collective-permute-start.13 = (bf16[8,128,256]{2,1,0:T(8,128)(2,1)S(1)}, bf16[8,128,256]{2,1,0:T(8,128)(2,1)S(1)}, u32[]{:S(2)}, u32[]{:S(2)}) collective-permute-start(bf16[8,128,256]{2,1,0:T(8,128)(2,1)S(1)} %pad_maximum_fusion.refs_10_), channel_id=1, source_target_pairs={{0,192},{8,56},{16,208},{24,40},{32,224},{40,24},{48,240},{56,8},{... | collective-permute-start | bytes 1572872 | tf_op jit(solution)/shard_map/ppermute | solution.py:51
  15.1 6.9 %collective-permute-start.2 = (bf16[4,128,256]{2,1,0:T(8,128)(2,1)S(1)}, bf16[4,128,256]{2,1,0:T(8,128)(2,1)S(1)}, u32[]{:S(2)}, u32[]{:S(2)}) collective-permute-start(bf16[4,128,256]{2,1,0:T(8,128)(2,1)S(1)} %collective-permute-done.1.refs_4_), channel_id=1, source_target_pairs={{0,1},{1,2},{2,3},{3,4},{4,5},{5,6},{6,7},{7,0},{8,15},{9,8},{10,9... | collective-permute-start | bytes 786440 | tf_op jit(solution)/shard_map/ppermute | solution.py:65
  15.1 18.3 %collective-permute-start.14 = (bf16[8,128,256]{2,1,0:T(8,128)(2,1)S(1)}, bf16[8,128,256]{2,1,0:T(8,128)(2,1)S(1)}, u32[]{:S(2)}, u32[]{:S(2)}) collective-permute-start(bf16[8,128,256]{2,1,0:T(8,128)(2,1)S(1)} %pad_maximum_fusion.refs_10_), channel_id=1, source_target_pairs={{0,8},{8,0},{16,24},{24,16},{32,40},{40,32},{48,56},{56,48},{64,72... | collective-permute-start | bytes 1572872 | tf_op jit(solution)/shard_map/ppermute | solution.py:33
  22.0 11.2 %collective-permute-start.3 = (bf16[4,128,256]{2,1,0:T(8,128)(2,1)S(1)}, bf16[4,128,256]{2,1,0:T(8,128)(2,1)S(1)}, u32[]{:S(2)}, u32[]{:S(2)}) collective-permute-start(bf16[4,128,256]{2,1,0:T(8,128)(2,1)S(1)} %collective-permute-done.2.refs_5_), channel_id=1, source_target_pairs={{0,1},{1,2},{2,3},{3,4},{4,5},{5,6},{6,7},{7,0},{8,15},{9,8},{10,9... | collective-permute-start | bytes 786440 | tf_op jit(solution)/shard_map/ppermute | solution.py:65
  22.0 16.7 %collective-permute-start.15 = (bf16[8,128,256]{2,1,0:T(8,128)(2,1)S(1)}, bf16[8,128,256]{2,1,0:T(8,128)(2,1)S(1)}, u32[]{:S(2)}, u32[]{:S(2)}) collective-permute-start(bf16[8,128,256]{2,1,0:T(8,128)(2,1)S(1)} %collective-permute-done.11.refs_11_), channel_id=1, source_target_pairs={{0,8},{8,0},{16,24},{24,16},{32,40},{40,32},{48,56},{56,48},{64,72... | collective-permute-start | bytes 1572872 | tf_op jit(solution)/shard_map/ppermute | solution.py:33
  28.1 10.6 %collective-permute-start.16 = (bf16[8,128,256]{2,1,0:T(8,128)(2,1)S(1)}, bf16[8,128,256]{2,1,0:T(8,128)(2,1)S(1)}, u32[]{:S(2)}, u32[]{:S(2)}) collective-permute-start(bf16[8,128,256]{2,1,0:T(8,128)(2,1)S(1)} %collective-permute-done.12.refs_12_), channel_id=1, source_target_pairs={{0,8},{8,0},{16,24},{24,16},{32,40},{40,32},{48,56},{56,48},{64,72... | collective-permute-start | bytes 1572872 | tf_op jit(solution)/shard_map/ppermute | solution.py:33
  30.1 8.6 %collective-permute-start.17 = (bf16[8,128,256]{2,1,0:T(8,128)(2,1)S(1)}, bf16[8,128,256]{2,1,0:T(8,128)(2,1)S(1)}, u32[]{:S(2)}, u32[]{:S(2)}) collective-permute-start(bf16[8,128,256]{2,1,0:T(8,128)(2,1)S(1)} %collective-permute-done.13.refs_13_), channel_id=1, source_target_pairs={{0,8},{8,0},{16,24},{24,16},{32,40},{40,32},{48,56},{56,48},{64,72... | collective-permute-start | bytes 1572872 | tf_op jit(solution)/shard_map/ppermute | solution.py:33
  50.9 6.5 %collective-permute-start.21 = (f32[4,1024]{1,0:T(4,128)S(1)}, f32[4,1024]{1,0:T(4,128)S(1)}, u32[]{:S(2)}, u32[]{:S(2)}) collective-permute-start(f32[4,1024]{1,0:T(4,128)S(1)} %add.75.refs_4_), channel_id=1, source_target_pairs={{0,4},{1,5},{2,6},{3,7},{4,0},{5,1},{6,2},{7,3},{8,12},{9,13},{10,... | collective-permute-start | bytes 49160 | tf_op jit(solution)/shard_map/ppermute | solution.py:57
  80.4 5.9 %collective-permute-start.30 = (f32[2,1024]{1,0:T(2,128)S(1)}, f32[2,1024]{1,0:T(2,128)S(1)}, u32[]{:S(2)}, u32[]{:S(2)}) collective-permute-start(f32[2,1024]{1,0:T(2,128)S(1)} %add.80.refs_4_), channel_id=1, source_target_pairs={{0,2},{1,3},{2,0},{3,1},{4,6},{5,7},{6,4},{7,5},{8,10},{9,11},{10,... | collective-permute-start | bytes 24584 | tf_op jit(solution)/shard_map/ppermute | solution.py:57
  83.9 6.4 %collective-permute-start.32 = (f32[2,1024]{1,0:T(2,128)S(1)}, f32[2,1024]{1,0:T(2,128)S(1)}, u32[]{:S(2)}, u32[]{:S(2)}) collective-permute-start(f32[2,1024]{1,0:T(2,128)S(1)} %add.80.refs_4_), channel_id=1, source_target_pairs={{0,4},{1,5},{2,6},{3,7},{4,0},{5,1},{6,2},{7,3},{8,12},{9,13},{10,... | collective-permute-start | bytes 24584 | tf_op jit(solution)/shard_map/ppermute | solution.py:57
  92.6 41.7 %collective-permute-start.46 = (bf16[32,128,256]{2,1,0:T(8,128)(2,1)S(1)}, bf16[32,128,256]{2,1,0:T(8,128)(2,1)S(1)}, u32[]{:S(2)}, u32[]{:S(2)}) collective-permute-start(bf16[32,128,256]{2,1,0:T(8,128)(2,1)S(1)} %get-tuple-element.34), channel_id=1, source_target_pairs={{0,8},{8,0},{16,24},{24,16},{32,40},{40,32},{48,56},{56,48},{64,72... | collective-permute-start | bytes 6291464 | tf_op jit(solution)/shard_map/ppermute | solution.py:33
  127.6 6.5 %collective-permute-start.42 = (bf16[4,128,256]{2,1,0:T(8,128)(2,1)S(1)}, bf16[4,128,256]{2,1,0:T(8,128)(2,1)S(1)}, u32[]{:S(2)}, u32[]{:S(2)}) collective-permute-start(bf16[4,128,256]{2,1,0:T(8,128)(2,1)S(1)} %fusion.5), channel_id=1, source_target_pairs={{0,1},{1,2},{2,3},{3,4},{4,5},{5,6},{6,7},{7,0},{8,15},{9,8},{10,9... | collective-permute-start | bytes 786440 | tf_op jit(solution)/shard_map/ppermute | solution.py:65
  134.2 6.5 %collective-permute-start.43 = (bf16[4,128,256]{2,1,0:T(8,128)(2,1)S(1)}, bf16[4,128,256]{2,1,0:T(8,128)(2,1)S(1)}, u32[]{:S(2)}, u32[]{:S(2)}) collective-permute-start(bf16[4,128,256]{2,1,0:T(8,128)(2,1)S(1)} %fusion.3), channel_id=1, source_target_pairs={{0,1},{1,2},{2,3},{3,4},{4,5},{5,6},{6,7},{7,0},{8,15},{9,8},{10,9... | collective-permute-start | bytes 786440 | tf_op jit(solution)/shard_map/ppermute | solution.py:65
  135.2 16.4 %collective-permute-start.47 = (bf16[8,128,256]{2,1,0:T(8,128)(2,1)S(1)}, bf16[8,128,256]{2,1,0:T(8,128)(2,1)S(1)}, u32[]{:S(2)}, u32[]{:S(2)}) collective-permute-start(bf16[8,128,256]{2,1,0:T(8,128)(2,1)S(1)} %get-tuple-element.40), channel_id=1, source_target_pairs={{0,16},{8,72},{16,0},{24,88},{32,48},{40,104},{48,32},{56,120},{64... | collective-permute-start | bytes 1572872 | tf_op jit(solution)/shard_map/ppermute | solution.py:45
  135.3 16.3 %collective-permute-start.48 = (bf16[8,128,256]{2,1,0:T(8,128)(2,1)S(1)}, bf16[8,128,256]{2,1,0:T(8,128)(2,1)S(1)}, u32[]{:S(2)}, u32[]{:S(2)}) collective-permute-start(bf16[8,128,256]{2,1,0:T(8,128)(2,1)S(1)} %get-tuple-element.42), channel_id=1, source_target_pairs={{0,48},{8,200},{16,32},{24,216},{32,16},{40,232},{48,0},{56,248},{... | collective-permute-start | bytes 1572872 | tf_op jit(solution)/shard_map/ppermute | solution.py:45
  136.1 15.5 %collective-permute-start.49 = (bf16[8,128,256]{2,1,0:T(8,128)(2,1)S(1)}, bf16[8,128,256]{2,1,0:T(8,128)(2,1)S(1)}, u32[]{:S(2)}, u32[]{:S(2)}) collective-permute-start(bf16[8,128,256]{2,1,0:T(8,128)(2,1)S(1)} %get-tuple-element.41), channel_id=1, source_target_pairs={{0,32},{8,136},{16,48},{24,152},{32,0},{40,168},{48,16},{56,184},{... | collective-permute-start | bytes 1572872 | tf_op jit(solution)/shard_map/ppermute | solution.py:45
  140.8 6.8 %collective-permute-start.44 = (bf16[4,128,256]{2,1,0:T(8,128)(2,1)S(1)}, bf16[4,128,256]{2,1,0:T(8,128)(2,1)S(1)}, u32[]{:S(2)}, u32[]{:S(2)}) collective-permute-start(bf16[4,128,256]{2,1,0:T(8,128)(2,1)S(1)} %fusion.1), channel_id=1, source_target_pairs={{0,1},{1,2},{2,3},{3,4},{4,5},{5,6},{6,7},{7,0},{8,15},{9,8},{10,9... | collective-permute-start | bytes 786440 | tf_op jit(solution)/shard_map/ppermute | solution.py:65
  147.6 8.0 %collective-permute-start.45 = (bf16[2,128,256]{2,1,0:T(8,128)(2,1)S(1)}, bf16[2,128,256]{2,1,0:T(8,128)(2,1)S(1)}, u32[]{:S(2)}, u32[]{:S(2)}) collective-permute-start(bf16[2,128,256]{2,1,0:T(8,128)(2,1)S(1)} %broadcast_select_fusion), channel_id=1, source_target_pairs={{0,8},{8,0},{16,24},{24,16},{32,40},{40,32},{48,56},{56,48},{64,72... | collective-permute-start | bytes 393224 | tf_op jit(solution)/shard_map/ppermute | solution.py:33
  153.7 7.3 %collective-permute-start.51 = (bf16[2,128,256]{2,1,0:T(8,128)(2,1)S(1)}, bf16[2,128,256]{2,1,0:T(8,128)(2,1)S(1)}, u32[]{:S(2)}, u32[]{:S(2)}) collective-permute-start(bf16[2,128,256]{2,1,0:T(8,128)(2,1)S(1)} %get-tuple-element.45), channel_id=1, source_target_pairs={{0,192},{8,56},{16,208},{24,40},{32,224},{40,24},{48,240},{56,8},{... | collective-permute-start | bytes 393224 | tf_op jit(solution)/shard_map/ppermute | solution.py:51
  154.0 6.9 %collective-permute-start.52 = (bf16[2,128,256]{2,1,0:T(8,128)(2,1)S(1)}, bf16[2,128,256]{2,1,0:T(8,128)(2,1)S(1)}, u32[]{:S(2)}, u32[]{:S(2)}) collective-permute-start(bf16[2,128,256]{2,1,0:T(8,128)(2,1)S(1)} %get-tuple-element.44), channel_id=1, source_target_pairs={{0,128},{8,40},{16,144},{24,56},{32,160},{40,8},{48,176},{56,24},{... | collective-permute-start | bytes 393224 | tf_op jit(solution)/shard_map/ppermute | solution.py:51
  161.0 9.5 %collective-permute-start.53 = (bf16[128,256]{1,0:T(8,128)(2,1)S(1)}, bf16[128,256]{1,0:T(8,128)(2,1)S(1)}, u32[]{:S(2)}, u32[]{:S(2)}) collective-permute-start(bf16[128,256]{1,0:T(8,128)(2,1)S(1)} %fusion.12), channel_id=1, source_target_pairs={{0,8},{8,0},{16,24},{24,16},{32,40},{40,32},{48,56},{56,48},{64,72... | collective-permute-start | bytes 196616 | tf_op jit(solution)/shard_map/ppermute | solution.py:33
  (36 other events, 330.1 us)
where the time goes:
time: 171 us
  starting transfers between devices  90.8 us (53%)
  waiting for transfers between devices  63 us (37%)
  Pallas kernels  11 us (6%)
  other arithmetic  4.4 us (3%)
    ppermute x14, starting transfers between devices, swap(): return lax.ppermute(v, 'blk', blk_perm(lambda y, x, k: (y, x, 1 - k)))  45.8 us
    ppermute x8, waiting for transfers between devices, ring(): return lax.ppermute(v, ('blk', 'col'), pairs)  22.6 us
    ppermute x8, starting transfers between devices, over_z(): return lax.ppermute(v, 'col', [(i, i ^ d) for i in range(8)])  13.5 us
    ppermute x8, waiting for transfers between devices, over_z(): return lax.ppermute(v, 'col', [(i, i ^ d) for i in range(8)])  12.7 us
    pallas_call x6, Pallas kernels, call(): pl.pallas_call(kernel, out_shape=out_shape, in_specs=in_specs, out_specs=...  11 us
    ppermute x6, starting transfers between devices, over_x(): return lax.ppermute(v, 'blk', blk_perm(lambda y, x, k: (y, x ^ d, k)))  8.46 us
    ppermute x14, waiting for transfers between devices, swap(): return lax.ppermute(v, 'blk', blk_perm(lambda y, x, k: (y, x, 1 - k)))  7.81 us
    ppermute x6, starting transfers between devices, over_second(): lax.ppermute(v, 'blk', blk_perm(lambda y, x, k: (y ^ d, x, k) if k == 0 e...  7.56 us
  transfers between devices with their start and end apart: 54, of which 30 were waited for; matrix products, arithmetic and copies ran while one was open for 3% of the time, Pallas kernels for 1%

commit v1 on v0

--- a/solution.py
+++ b/solution.py
@@ -57,11 +57,11 @@
     return lax.ppermute(v, "col", [(i, i ^ d) for i in range(8)])
 
 
-def ring(v):
+def along_z(v, odd):
     pairs = []
     for i in range(256):
-        z = i % 8
-        pairs.append((i, i - z + (z + (1 if (i // 8) % 2 == 0 else -1)) % 8))
+        z, core = i % 8, (i // 8) % 2
+        pairs.append((i, i - z + (((z + core + odd) ^ 1) - core - odd) % 8))
     return lax.ppermute(v, ("blk", "col"), pairs)
 
 
@@ -72,25 +72,29 @@
 def gather_targets(tgt_feat, core):
     came = swap(tgt_feat)
     pair = pick(core, jnp.stack([tgt_feat[0], came[0]]), jnp.stack([came[1], tgt_feat[1]]))
-    near = jnp.concatenate([pair] + [over_first(pair, d) for d in (1, 2, 3)])
-    parts = [near] + [over_second(near, d) for d in (1, 2, 3)]
-    return parts + [swap(p) for p in parts]
-
-
-def gather_sources(src_feat, core):
-    came = swap(src_feat)
-    chunk = pick(core, jnp.concatenate([src_feat, came]), jnp.concatenate([came, src_feat]))
-    one = ring(chunk)
-    two = ring(one)
-    three = ring(two)
-    four = ring(pick(core, three[:2], three[2:]))
-    give = jnp.concatenate([pick(core, c[2:], c[:2]) for c in (one, two)])
-    return [src_feat, one, two, three, four, swap(give), swap(pick(core, three[2:], three[:2]))]
+    near = [pair]
+    for d in (1, 2, 3):
+        near.append(over_first(pair, d))
+    near = jnp.concatenate(near)
+    parts = [near]
+    for d in (1, 2, 3):
+        parts.append(over_second(near, d))
+    for n in range(4):
+        parts.append(swap(parts[n]))
+    return parts
+
+
+def gather_sources(src_feat, even):
+    came = along_z(src_feat, 0)
+    pairs = [jnp.where(even, jnp.stack([src_feat, came]), jnp.stack([came, src_feat]))]
+    for step in (2, 3, 4):
+        pairs.append(along_z(pairs[-1], (step + 1) % 2))
+    return pairs
 
 
 def col_sum_parts(v):
     v = v + over_z(v, 1)
-    return (v,) + tuple(over_z(v, d) for d in (2, 6, 4))
+    return (v,) + tuple(over_z(v, d) for d in (5, 2, 6))
 
 
 def blk_sum_parts(v):
@@ -110,27 +114,21 @@
     for d in (1, 3, 2):
         s = s + over_first(q[d], d).astype(F32)
     s = s.astype(BF16).reshape(4, 2, 128, 256)
-    t = s[0].astype(F32) + sum(over_second(s[d], d).astype(F32) for d in (1, 3, 2))
+    t = s[0].astype(F32)
+    for d in (1, 3, 2):
+        t = t + over_second(s[d], d).astype(F32)
     keep = pick(core, t[0], t[1])
     came = swap(pick(core, t[1], t[0]).astype(BF16)).astype(F32)
     return pick(core, jnp.stack([keep, came]), jnp.stack([came, keep]))
 
 
-def reduce_sources(own, keep, give, far, core):
-    got = swap(give)
-
-    def add(m, d):
-        k, g = keep[d - 1].astype(F32), got[d - 1].astype(F32)
-        m = m.astype(F32)
-        return (pick(core, jnp.concatenate([k, g]), jnp.concatenate([g, k])) + m).astype(BF16)
-
-    last = ring(far)
-    none = jnp.zeros_like(last)
-    moving = pick(core, jnp.concatenate([last, none]), jnp.concatenate([none, last]))
-    for d in (3, 2, 1):
-        moving = ring(add(moving, d))
-    came = swap(pick(core, moving[2:], moving[:2]))
-    return own.astype(F32) + pick(core, moving[:2], moving[2:]).astype(F32) + came.astype(F32)
+def reduce_sources(parts, even):
+    moving = along_z(parts[3], 1)
+    for step in (2, 1):
+        moving = along_z((parts[step].astype(F32) + moving.astype(F32)).astype(BF16), step % 2)
+    pair = parts[0].astype(F32) + moving.astype(F32)
+    came = along_z(jnp.where(even, pair[1], pair[0]).astype(BF16), 0)
+    return jnp.where(even, pair[0], pair[1]) + came.astype(F32)
 
 
 def slot_of(meta, s):
@@ -149,6 +147,17 @@
     return b, lax.axis_index("col"), b // 8, (b // 2) % 4, b % 2
 
 
+def chunk_places(b, z):
+    core = b % 2
+    half = (z + core) & 7
+    way = 1 - 2 * (half % 2)
+    places = []
+    for off in (0, -way, way, 2):
+        first = 2 * (half // 2 + off)
+        places.append([pl.multiple_of(((first + h - core) & 7) * 128, 128) for h in range(2)])
+    return places
+
+
 def unit(rows):
     x = rows.astype(F32)
     return (x * lax.rsqrt(jnp.mean(x * x, axis=-1, keepdims=True) + EPS)).astype(BF16)
@@ -162,26 +171,11 @@
 
 def build_kernel(*refs):
     meta, refs = refs[:3], refs[3:]
-    own, one, two, three, four, far12, far3 = refs[:7]
-    tgt = refs[7:15]
-    mass, kt, tiles, raw, rows, unit_src, acc, sems, row_sems = refs[15:]
+    src = refs[:4]
+    tgt = refs[4:12]
+    mass, kt, tiles, raw, rows, unit_src, acc, sems = refs[12:]
     n = live(meta)
-    _, z, my_y, my_x, my_k = place()
-    sign = 2 * my_k - 1
-    chunks = []
-    for p in range(2):
-        chunks.append((own.at[p], z, p))
-        for d, ref in ((1, one), (2, two), (3, three)):
-            chunks.append((ref.at[2 * my_k + p], z + sign * d, p))
-        chunks.append((four.at[p], z + 4, p))
-        chunks.append((far12.at[p], z - sign, p))
-        chunks.append((far12.at[2 + p], z - sign * 2, p))
-        chunks.append((far3.at[p], z - sign * 3, p))
-    copies = []
-    for c, (ref, at, p) in enumerate(chunks):
-        at = pl.multiple_of((at & 7) * 128, 128)
-        copies.append((pltpu.make_async_copy(ref, raw.at[p, pl.ds(at, 128), :], row_sems.at[c]), at, p))
-        copies[-1][0].start()
+    b, z, my_y, my_x, my_k = place()
 
     def fetch(s, _):
         _, j = slot_of(meta, s)
@@ -199,9 +193,12 @@
         return 0
 
     lax.fori_loop(0, n, fetch, 0)
-    for copy, at, p in copies:
-        copy.wait()
-        unit_src[p, pl.ds(at, 128), :] = unit(raw[p, pl.ds(at, 128), :])
+    for ref, places in zip(src, chunk_places(b, z)):
+        for h, at in enumerate(places):
+            for p in range(2):
+                chunk = ref[h, p]
+                raw[p, pl.ds(at, 128), :] = chunk
+                unit_src[p, pl.ds(at, 128), :] = unit(chunk)
     acc[...] = jnp.zeros_like(acc)
     scale = math.log2(math.e) / (256 * TEMP)
     shift = OFFSET / TEMP * math.log2(math.e)
@@ -311,7 +308,7 @@
 
 def toward_kernel(*refs):
     meta, refs = refs[:3], refs[3:]
-    kt, u, tiles, c0, c1, c2, c3, mass, own, keep, give, far, v_out, v_all, acc = refs
+    kt, u, tiles, c0, c1, c2, c3, mass, out1, out2, out3, out4, v_out, v_all, acc = refs
     total = c0[...] + c1[...].astype(F32) + c2[...].astype(F32) + c3[...].astype(F32)
     v_all[...] = mass[...] / total
     b, z = place()[:2]
@@ -334,15 +331,10 @@
         return 0
 
     lax.fori_loop(0, live(meta), step, 0)
-    sign = 1 - 2 * (b % 2)
-    for p in range(2):
-        for ref, d in ((own, 0), (far, 4)):
-            at = pl.multiple_of(((z + d) & 7) * 128, 128)
-            ref[p] = acc[p, pl.ds(at, 128), :].astype(BF16)
-        for ref, way in ((keep, sign), (give, -sign)):
-            for d in (1, 2, 3):
-                at = pl.multiple_of(((z + way * d) & 7) * 128, 128)
-                ref[d - 1, p] = acc[p, pl.ds(at, 128), :].astype(BF16)
+    for ref, places in zip((out1, out2, out3, out4), chunk_places(b, z)):
+        for h, at in enumerate(places):
+            for p in range(2):
+                ref[h, p] = acc[p, pl.ds(at, 128), :].astype(BF16)
 
 
 def call(kernel, out_shape, in_specs, scratch, args, flops, nbytes):
@@ -360,7 +352,8 @@
 def program(src_feat, tgt_feat, src_mass, tgt_mass, candidates, counts, tgt_home):
     core = lax.axis_index("blk") % 2
     meta = (counts, candidates, tgt_home)
-    sources = gather_sources(src_feat, core)
+    even = (lax.axis_index("col") + core) % 2 == 0
+    sources = gather_sources(src_feat, even)
     targets = gather_targets(tgt_feat, core)
     S = jax.ShapeDtypeStruct
     kt, tiles, raw, rows = call(
@@ -371,12 +364,11 @@
             S((2, 1024, 256), BF16),
             S((4, 1024), F32),
         ],
-        [SMEM] * 3 + [ANY] * 15 + [VMEM],
+        [SMEM] * 3 + [VMEM] * 4 + [ANY] * 8 + [VMEM],
         [
             pltpu.VMEM((2, 1024, 256), BF16),
             pltpu.VMEM((2, 8, 1024), F32),
             pltpu.SemaphoreType.DMA((PAIRS,)),
-            pltpu.SemaphoreType.DMA((16,)),
         ],
         (*meta, *sources, *targets, src_mass),
         800_000_000,
@@ -421,18 +413,16 @@
     came = swap(other)
     parts = blk_sum_parts(sums)
     tgt_own = reduce_targets(mine, came, core)
-    own, keep, give, far, v = call(
+    *parts, v = call(
         toward_kernel,
-        [S((2, 128, 256), BF16)]
-        + [S((3, 2, 128, 256), BF16)] * 2
-        + [S((2, 128, 256), BF16), S((2, 128), F32)],
+        [S((2, 2, 128, 256), BF16)] * 4 + [S((2, 128), F32)],
         [SMEM] * 3 + [VMEM] * 8,
         [pltpu.VMEM((64, 128), F32), pltpu.VMEM((2, 1024, 256), F32)],
         (*meta, kt, u, tiles, *parts, mass_tgt),
         800_000_000,
         6_000_000,
     )
-    src_own = reduce_sources(own, keep, give, far, core)
+    src_own = reduce_sources(parts, even)
     src_aligned = (src_own / src_mass.astype(F32)[:, :, None]).astype(BF16)
     tgt_aligned = (tgt_own * v[:, :, None] / tgt_mass.astype(F32)[:, :, None]).astype(BF16)
     return (src_aligned, tgt_aligned)

time: 171 us -> 176 us (1.029)
  the two profiles are of different devices: /device:TPU:97 before, /device:TPU:2 now
where the time goes in v1:
time: 176 us; the launch traced here: 175 us
  waiting for transfers between devices  91.6 us (52%)
  starting transfers between devices  66.5 us (38%)
  Pallas kernels  11.5 us (7%)
  other arithmetic  3.18 us (2%)
    ppermute x8, waiting for transfers between devices, along_z(): return lax.ppermute(v, ('blk', 'col'), pairs)  33.7 us
    ppermute x6, waiting for transfers between devices, over_first(): lax.ppermute(v, 'blk', blk_perm(lambda y, x, k: (y, x ^ d, k) if k == 0 e...  20.2 us
    ppermute x8, starting transfers between devices, along_z(): return lax.ppermute(v, ('blk', 'col'), pairs)  17.2 us
    ppermute x8, waiting for transfers between devices, over_z(): return lax.ppermute(v, 'col', [(i, i ^ d) for i in range(8)])  15.8 us
    pallas_call x6, Pallas kernels, call(): pl.pallas_call(kernel, out_shape=out_shape, in_specs=in_specs, out_specs=...  11.5 us
    ppermute x8, starting transfers between devices, over_z(): return lax.ppermute(v, 'col', [(i, i ^ d) for i in range(8)])  11.4 us
    ppermute x6, starting transfers between devices, over_x(): return lax.ppermute(v, 'blk', blk_perm(lambda y, x, k: (y, x ^ d, k)))  9.57 us
    ppermute x6, starting transfers between devices, over_first(): lax.ppermute(v, 'blk', blk_perm(lambda y, x, k: (y, x ^ d, k) if k == 0 e...  9.18 us
  transfers between devices with their start and end apart: 49, of which 34 were waited for; matrix products, arithmetic and copies ran while one was open for 2% of the time, Pallas kernels for 1%

profile of v1, /device:TPU:2, one launch (start us, length us, event | category | flops | bytes accessed | tf_op | source)
XLA Modules:
  0.0 174.8 jit_solution(7044875558571777434)
XLA Ops:
  4.0 2.8 %collective-permute-start.6 = (bf16[2,128,256]{2,1,0:T(8,128)(2,1)S(1)}, bf16[2,128,256]{2,1,0:T(8,128)(2,1)S(1)}, u32[]{:S(2)}, u32[]{:S(2)}) collective-permute-start(bf16[2,128,256]{2,1,0:T(8,128)(2,1)S(1)} %maximum_select_fusion.2), channel_id=1, source_target_pairs={{0,32},{8,136},{16,48},{24,152},{32,0},{40,168},{48,16},{56,184},{... | collective-permute-start | bytes 393224 | tf_op jit(solution)/shard_map/ppermute | solution.py:45
  7.4 3.0 %collective-permute-done.6 = bf16[2,128,256]{2,1,0:T(8,128)(2,1)S(1)} collective-permute-done((bf16[2,128,256]{2,1,0:T(8,128)(2,1)S(1)}, bf16[2,128,256]{2,1,0:T(8,128)(2,1)S(1)}, u32[]{:S(2)}, u32[]{:S(2)}) %collective-permute-start.6) | collective-permute-done | bytes 131104 | tf_op jit(solution)/shard_map/ppermute | solution.py:45
  12.6 2.9 %collective-permute-start.9 = (bf16[8,128,256]{2,1,0:T(8,128)(2,1)S(1)}, bf16[8,128,256]{2,1,0:T(8,128)(2,1)S(1)}, u32[]{:S(2)}, u32[]{:S(2)}) collective-permute-start(bf16[8,128,256]{2,1,0:T(8,128)(2,1)S(1)} %pad_maximum_fusion.refs_7_), channel_id=1, source_target_pairs={{0,128},{8,40},{16,144},{24,56},{32,160},{40,8},{48,176},{56,24},{... | collective-permute-start | bytes 1572872 | tf_op jit(solution)/shard_map/ppermute | solution.py:51
  17.7 4.1 %collective-permute-done = bf16[2,128,256]{2,1,0:T(8,128)(2,1)S(1)} collective-permute-done((bf16[2,128,256]{2,1,0:T(8,128)(2,1)}, bf16[2,128,256]{2,1,0:T(8,128)(2,1)S(1)}, u32[]{:S(2)}, u32[]{:S(2)}) %collective-permute-start) | collective-permute-done | bytes 131104 | tf_op jit(solution)/shard_map/ppermute | solution.py:65
  21.8 5.1 %collective-permute-start.1 = (bf16[2,2,128,256]{3,2,1,0:T(8,128)(2,1)S(1)}, bf16[2,2,128,256]{3,2,1,0:T(8,128)(2,1)S(1)}, u32[]{:S(2)}, u32[]{:S(2)}) collective-permute-start(bf16[2,2,128,256]{3,2,1,0:T(8,128)(2,1)S(1)} %maximum_select_fusion.refs_3_), channel_id=1, source_target_pairs={{0,7},{1,2},{2,1},{3,4},{4,3},{5,6},{6,5},{7,0},{8,9},{9,8},{10,11... | collective-permute-start | bytes 786440 | tf_op jit(solution)/shard_map/ppermute | solution.py:65
  26.9 4.4 %collective-permute-done.1.refs_4_ = bf16[2,2,128,256]{3,2,1,0:T(8,128)(2,1)S(1)} collective-permute-done((bf16[2,2,128,256]{3,2,1,0:T(8,128)(2,1)S(1)}, bf16[2,2,128,256]{3,2,1,0:T(8,128)(2,1)S(1)}, u32[]{:S(2)}, u32[]{:S(2)}) %collective-permute-start.1) | collective-permute-done | bytes 262176 | tf_op jit(solution)/shard_map/ppermute | solution.py:65
  31.9 6.8 %collective-permute-done.2.refs_5_ = bf16[2,2,128,256]{3,2,1,0:T(8,128)(2,1)S(1)} collective-permute-done((bf16[2,2,128,256]{3,2,1,0:T(8,128)(2,1)S(1)}, bf16[2,2,128,256]{3,2,1,0:T(8,128)(2,1)S(1)}, u32[]{:S(2)}, u32[]{:S(2)}) %collective-permute-start.2) | collective-permute-done | bytes 262176 | tf_op jit(solution)/shard_map/ppermute | solution.py:65
  38.7 3.5 %collective-permute-start.3 = (bf16[2,2,128,256]{3,2,1,0:T(8,128)(2,1)S(1)}, bf16[2,2,128,256]{3,2,1,0:T(8,128)(2,1)S(1)}, u32[]{:S(2)}, u32[]{:S(2)}) collective-permute-start(bf16[2,2,128,256]{3,2,1,0:T(8,128)(2,1)S(1)} %collective-permute-done.2.refs_5_), channel_id=1, source_target_pairs={{0,7},{1,2},{2,1},{3,4},{4,3},{5,6},{6,5},{7,0},{8,9},{9,8},{10,11... | collective-permute-start | bytes 786440 | tf_op jit(solution)/shard_map/ppermute | solution.py:65
  42.2 4.3 %collective-permute-done.3.refs_6_ = bf16[2,2,128,256]{3,2,1,0:T(8,128)(2,1)S(1)} collective-permute-done((bf16[2,2,128,256]{3,2,1,0:T(8,128)(2,1)S(1)}, bf16[2,2,128,256]{3,2,1,0:T(8,128)(2,1)S(1)}, u32[]{:S(2)}, u32[]{:S(2)}) %collective-permute-start.3) | collective-permute-done | bytes 262176 | tf_op jit(solution)/shard_map/ppermute | solution.py:65
  46.6 3.2 %shard_map.86 = (bf16[12,128,1024]{2,1,0:T(8,128)(2,1)S(1)}, bf16[12,128,256]{2,1,0:T(8,128)(2,1)S(1)}, bf16[2,1024,256]{2,1,0:T(8,128)(2,1)S(1)}, f32[4,1024]{1,0:T(4,128)S(1)}) custom-call(s32[2]{0:T(128)S(1)} %copy-done.1, s32[2,8]{1,0:T(2,128)S(1)} %copy-done, s32[64]{0:T(128)S(1)} %copy-done.2, bf16[2,2,128,256]{3,2,1,0:T(8,128)(2,1)S(1)} %maximum_select_fusion.refs_3_, ...), custom_call_target="tpu_custom_call" | custom-call | flops 800000000 | bytes 7000000 | tf_op jit(solution)/shard_map/pallas_call | solution.py:341
  50.0 3.8 %collective-permute-done.15 = f32[4,1024]{1,0:T(4,128)S(1)} collective-permute-done((f32[4,1024]{1,0:T(4,128)S(1)}, f32[4,1024]{1,0:T(4,128)S(1)}, u32[]{:S(2)}, u32[]{:S(2)}) %collective-permute-start.15) | collective-permute-done | bytes 16416 | tf_op jit(solution)/shard_map/ppermute | solution.py:57
  53.7 3.1 %collective-permute-start.16 = (f32[4,1024]{1,0:T(4,128)S(1)}, f32[4,1024]{1,0:T(4,128)S(1)}, u32[]{:S(2)}, u32[]{:S(2)}) collective-permute-start(f32[4,1024]{1,0:T(4,128)S(1)} %add.76.refs_4_), channel_id=1, source_target_pairs={{0,5},{1,4},{2,7},{3,6},{4,1},{5,0},{6,3},{7,2},{8,13},{9,12},{10,... | collective-permute-start | bytes 49160 | tf_op jit(solution)/shard_map/ppermute | solution.py:57
  61.4 3.7 %collective-permute-done.18.refs_7_ = f32[4,1024]{1,0:T(4,128)S(1)} collective-permute-done((f32[4,1024]{1,0:T(4,128)S(1)}, f32[4,1024]{1,0:T(4,128)S(1)}, u32[]{:S(2)}, u32[]{:S(2)}) %collective-permute-start.18) | collective-permute-done | bytes 16416 | tf_op jit(solution)/shard_map/ppermute | solution.py:57
  69.7 3.0 %collective-permute-start.20 = (bf16[128,128]{1,0:T(8,128)(2,1)S(1)}, bf16[128,128]{1,0:T(8,128)(2,1)S(1)}, u32[]{:S(2)}, u32[]{:S(2)}) collective-permute-start(bf16[128,128]{1,0:T(8,128)(2,1)S(1)} %fusion.7), channel_id=1, source_target_pairs={{0,16},{8,24},{16,0},{24,8},{32,48},{40,56},{48,32},{56,40},{64,80... | collective-permute-start | bytes 98312 | tf_op jit(solution)/shard_map/ppermute | solution.py:37
  84.7 3.3 %collective-permute-done.26 = f32[2,1024]{1,0:T(2,128)S(1)} collective-permute-done((f32[2,1024]{1,0:T(2,128)S(1)}, f32[2,1024]{1,0:T(2,128)S(1)}, u32[]{:S(2)}, u32[]{:S(2)}) %collective-permute-start.26) | collective-permute-done | bytes 8224 | tf_op jit(solution)/shard_map/ppermute | solution.py:57
  90.6 2.8 %collective-permute-start.29 = (f32[2,1024]{1,0:T(2,128)S(1)}, f32[2,1024]{1,0:T(2,128)S(1)}, u32[]{:S(2)}, u32[]{:S(2)}) collective-permute-start(f32[2,1024]{1,0:T(2,128)S(1)} %add.81.refs_4_), channel_id=1, source_target_pairs={{0,6},{1,7},{2,4},{3,5},{4,2},{5,3},{6,0},{7,1},{8,14},{9,15},{10,... | collective-permute-start | bytes 24584 | tf_op jit(solution)/shard_map/ppermute | solution.py:57
  100.1 3.7 %collective-permute-done.30 = bf16[64,128]{1,0:T(8,128)(2,1)S(1)} collective-permute-done((bf16[64,128]{1,0:T(8,128)(2,1)S(1)}, bf16[64,128]{1,0:T(8,128)(2,1)S(1)}, u32[]{:S(2)}, u32[]{:S(2)}) %collective-permute-start.30) | collective-permute-done | bytes 16416 | tf_op jit(solution)/shard_map/ppermute | solution.py:33
  115.1 2.8 %collective-permute-done.35.refs_8_ = bf16[64,128]{1,0:T(8,128)(2,1)S(1)} collective-permute-done((bf16[64,128]{1,0:T(8,128)(2,1)S(1)}, bf16[64,128]{1,0:T(8,128)(2,1)S(1)}, u32[]{:S(2)}, u32[]{:S(2)}) %collective-permute-start.35) | collective-permute-done | bytes 16416 | tf_op jit(solution)/shard_map/ppermute | solution.py:41
  121.5 3.3 %collective-permute-start.37 = (bf16[2,2,128,256]{3,2,1,0:T(8,128)(2,1)S(1)}, bf16[2,2,128,256]{3,2,1,0:T(8,128)(2,1)S(1)}, u32[]{:S(2)}, u32[]{:S(2)}) collective-permute-start(bf16[2,2,128,256]{3,2,1,0:T(8,128)(2,1)S(1)} %get-tuple-element.31), channel_id=1, source_target_pairs={{0,7},{1,2},{2,1},{3,4},{4,3},{5,6},{6,5},{7,0},{8,9},{9,8},{10,11... | collective-permute-start | bytes 786440 | tf_op jit(solution)/shard_map/ppermute | solution.py:65
  124.8 5.4 %collective-permute-done.37 = bf16[2,2,128,256]{3,2,1,0:T(8,128)(2,1)S(1)} collective-permute-done((bf16[2,2,128,256]{3,2,1,0:T(8,128)(2,1)S(1)}, bf16[2,2,128,256]{3,2,1,0:T(8,128)(2,1)S(1)}, u32[]{:S(2)}, u32[]{:S(2)}) %collective-permute-start.37) | collective-permute-done | bytes 262176 | tf_op jit(solution)/shard_map/ppermute | solution.py:65
  130.6 8.7 %collective-permute-done.38 = bf16[2,2,128,256]{3,2,1,0:T(8,128)(2,1)S(1)} collective-permute-done((bf16[2,2,128,256]{3,2,1,0:T(8,128)(2,1)S(1)}, bf16[2,2,128,256]{3,2,1,0:T(8,128)(2,1)S(1)}, u32[]{:S(2)}, u32[]{:S(2)}) %collective-permute-start.38) | collective-permute-done | bytes 262176 | tf_op jit(solution)/shard_map/ppermute | solution.py:65
  139.3 3.8 %collective-permute-start.39 = (bf16[2,2,128,256]{3,2,1,0:T(8,128)(2,1)S(1)}, bf16[2,2,128,256]{3,2,1,0:T(8,128)(2,1)S(1)}, u32[]{:S(2)}, u32[]{:S(2)}) collective-permute-start(bf16[2,2,128,256]{3,2,1,0:T(8,128)(2,1)S(1)} %add_convert_fusion.2), channel_id=1, source_target_pairs={{0,7},{1,2},{2,1},{3,4},{4,3},{5,6},{6,5},{7,0},{8,9},{9,8},{10,11... | collective-permute-start | bytes 786440 | tf_op jit(solution)/shard_map/ppermute | solution.py:65
  149.1 7.8 %collective-permute-done.44 = bf16[8,128,256]{2,1,0:T(8,128)(2,1)S(1)} collective-permute-done((bf16[8,128,256]{2,1,0:T(8,128)(2,1)S(1)}, bf16[8,128,256]{2,1,0:T(8,128)(2,1)S(1)}, u32[]{:S(2)}, u32[]{:S(2)}) %collective-permute-start.44) | collective-permute-done | bytes 524320 | tf_op jit(solution)/shard_map/ppermute | solution.py:45
  156.9 6.4 %collective-permute-done.43 = bf16[8,128,256]{2,1,0:T(8,128)(2,1)S(1)} collective-permute-done((bf16[8,128,256]{2,1,0:T(8,128)(2,1)S(1)}, bf16[8,128,256]{2,1,0:T(8,128)(2,1)S(1)}, u32[]{:S(2)}, u32[]{:S(2)}) %collective-permute-start.43) | collective-permute-done | bytes 524320 | tf_op jit(solution)/shard_map/ppermute | solution.py:45
  (121 shorter events, 72.2 us)
Async XLA Ops:
  4.0 6.5 %collective-permute-start.6 = (bf16[2,128,256]{2,1,0:T(8,128)(2,1)S(1)}, bf16[2,128,256]{2,1,0:T(8,128)(2,1)S(1)}, u32[]{:S(2)}, u32[]{:S(2)}) collective-permute-start(bf16[2,128,256]{2,1,0:T(8,128)(2,1)S(1)} %maximum_select_fusion.2), channel_id=1, source_target_pairs={{0,32},{8,136},{16,48},{24,152},{32,0},{40,168},{48,16},{56,184},{... | collective-permute-start | bytes 393224 | tf_op jit(solution)/shard_map/ppermute | solution.py:45
  11.8 19.5 %collective-permute-start.8 = (bf16[8,128,256]{2,1,0:T(8,128)(2,1)S(1)}, bf16[8,128,256]{2,1,0:T(8,128)(2,1)S(1)}, u32[]{:S(2)}, u32[]{:S(2)}) collective-permute-start(bf16[8,128,256]{2,1,0:T(8,128)(2,1)S(1)} %pad_maximum_fusion.refs_7_), channel_id=1, source_target_pairs={{0,64},{8,24},{16,80},{24,8},{32,96},{40,56},{48,112},{56,40},{64,... | collective-permute-start | bytes 1572872 | tf_op jit(solution)/shard_map/ppermute | solution.py:51
  12.6 18.7 %collective-permute-start.9 = (bf16[8,128,256]{2,1,0:T(8,128)(2,1)S(1)}, bf16[8,128,256]{2,1,0:T(8,128)(2,1)S(1)}, u32[]{:S(2)}, u32[]{:S(2)}) collective-permute-start(bf16[8,128,256]{2,1,0:T(8,128)(2,1)S(1)} %pad_maximum_fusion.refs_7_), channel_id=1, source_target_pairs={{0,128},{8,40},{16,144},{24,56},{32,160},{40,8},{48,176},{56,24},{... | collective-permute-start | bytes 1572872 | tf_op jit(solution)/shard_map/ppermute | solution.py:51
  15.5 16.3 %collective-permute-start.10 = (bf16[8,128,256]{2,1,0:T(8,128)(2,1)S(1)}, bf16[8,128,256]{2,1,0:T(8,128)(2,1)S(1)}, u32[]{:S(2)}, u32[]{:S(2)}) collective-permute-start(bf16[8,128,256]{2,1,0:T(8,128)(2,1)S(1)} %pad_maximum_fusion.refs_7_), channel_id=1, source_target_pairs={{0,192},{8,56},{16,208},{24,40},{32,224},{40,24},{48,240},{56,8},{... | collective-permute-start | bytes 1572872 | tf_op jit(solution)/shard_map/ppermute | solution.py:51
  21.8 9.5 %collective-permute-start.1 = (bf16[2,2,128,256]{3,2,1,0:T(8,128)(2,1)S(1)}, bf16[2,2,128,256]{3,2,1,0:T(8,128)(2,1)S(1)}, u32[]{:S(2)}, u32[]{:S(2)}) collective-permute-start(bf16[2,2,128,256]{3,2,1,0:T(8,128)(2,1)S(1)} %maximum_select_fusion.refs_3_), channel_id=1, source_target_pairs={{0,7},{1,2},{2,1},{3,4},{4,3},{5,6},{6,5},{7,0},{8,9},{9,8},{10,11... | collective-permute-start | bytes 786440 | tf_op jit(solution)/shard_map/ppermute | solution.py:65
  26.9 15.3 %collective-permute-start.11 = (bf16[8,128,256]{2,1,0:T(8,128)(2,1)S(1)}, bf16[8,128,256]{2,1,0:T(8,128)(2,1)S(1)}, u32[]{:S(2)}, u32[]{:S(2)}) collective-permute-start(bf16[8,128,256]{2,1,0:T(8,128)(2,1)S(1)} %pad_maximum_fusion.refs_7_), channel_id=1, source_target_pairs={{0,8},{8,0},{16,24},{24,16},{32,40},{40,32},{48,56},{56,48},{64,72... | collective-permute-start | bytes 1572872 | tf_op jit(solution)/shard_map/ppermute | solution.py:33
  31.3 7.4 %collective-permute-start.2 = (bf16[2,2,128,256]{3,2,1,0:T(8,128)(2,1)S(1)}, bf16[2,2,128,256]{3,2,1,0:T(8,128)(2,1)S(1)}, u32[]{:S(2)}, u32[]{:S(2)}) collective-permute-start(bf16[2,2,128,256]{3,2,1,0:T(8,128)(2,1)S(1)} %collective-permute-done.1.refs_4_), channel_id=1, source_target_pairs={{0,1},{1,0},{2,3},{3,2},{4,5},{5,4},{6,7},{7,6},{8,15},{9,10},{10,... | collective-permute-start | bytes 786440 | tf_op jit(solution)/shard_map/ppermute | solution.py:65
  31.3 15.3 %collective-permute-start.12 = (bf16[8,128,256]{2,1,0:T(8,128)(2,1)S(1)}, bf16[8,128,256]{2,1,0:T(8,128)(2,1)S(1)}, u32[]{:S(2)}, u32[]{:S(2)}) collective-permute-start(bf16[8,128,256]{2,1,0:T(8,128)(2,1)S(1)} %collective-permute-done.8.refs_8_), channel_id=1, source_target_pairs={{0,8},{8,0},{16,24},{24,16},{32,40},{40,32},{48,56},{56,48},{64,72... | collective-permute-start | bytes 1572872 | tf_op jit(solution)/shard_map/ppermute | solution.py:33
  31.3 15.2 %collective-permute-start.13 = (bf16[8,128,256]{2,1,0:T(8,128)(2,1)S(1)}, bf16[8,128,256]{2,1,0:T(8,128)(2,1)S(1)}, u32[]{:S(2)}, u32[]{:S(2)}) collective-permute-start(bf16[8,128,256]{2,1,0:T(8,128)(2,1)S(1)} %collective-permute-done.9.refs_9_), channel_id=1, source_target_pairs={{0,8},{8,0},{16,24},{24,16},{32,40},{40,32},{48,56},{56,48},{64,72... | collective-permute-start | bytes 1572872 | tf_op jit(solution)/shard_map/ppermute | solution.py:33
  31.8 14.7 %collective-permute-start.14 = (bf16[8,128,256]{2,1,0:T(8,128)(2,1)S(1)}, bf16[8,128,256]{2,1,0:T(8,128)(2,1)S(1)}, u32[]{:S(2)}, u32[]{:S(2)}) collective-permute-start(bf16[8,128,256]{2,1,0:T(8,128)(2,1)S(1)} %collective-permute-done.10.refs_10_), channel_id=1, source_target_pairs={{0,8},{8,0},{16,24},{24,16},{32,40},{40,32},{48,56},{56,48},{64,72... | collective-permute-start | bytes 1572872 | tf_op jit(solution)/shard_map/ppermute | solution.py:33
  38.7 7.8 %collective-permute-start.3 = (bf16[2,2,128,256]{3,2,1,0:T(8,128)(2,1)S(1)}, bf16[2,2,128,256]{3,2,1,0:T(8,128)(2,1)S(1)}, u32[]{:S(2)}, u32[]{:S(2)}) collective-permute-start(bf16[2,2,128,256]{3,2,1,0:T(8,128)(2,1)S(1)} %collective-permute-done.2.refs_5_), channel_id=1, source_target_pairs={{0,7},{1,2},{2,1},{3,4},{4,3},{5,6},{6,5},{7,0},{8,9},{9,8},{10,11... | collective-permute-start | bytes 786440 | tf_op jit(solution)/shard_map/ppermute | solution.py:65
  53.7 6.7 %collective-permute-start.16 = (f32[4,1024]{1,0:T(4,128)S(1)}, f32[4,1024]{1,0:T(4,128)S(1)}, u32[]{:S(2)}, u32[]{:S(2)}) collective-permute-start(f32[4,1024]{1,0:T(4,128)S(1)} %add.76.refs_4_), channel_id=1, source_target_pairs={{0,5},{1,4},{2,7},{3,6},{4,1},{5,0},{6,3},{7,2},{8,13},{9,12},{10,... | collective-permute-start | bytes 49160 | tf_op jit(solution)/shard_map/ppermute | solution.py:57
  88.0 6.7 %collective-permute-start.27 = (f32[2,1024]{1,0:T(2,128)S(1)}, f32[2,1024]{1,0:T(2,128)S(1)}, u32[]{:S(2)}, u32[]{:S(2)}) collective-permute-start(f32[2,1024]{1,0:T(2,128)S(1)} %add.81.refs_4_), channel_id=1, source_target_pairs={{0,5},{1,4},{2,7},{3,6},{4,1},{5,0},{6,3},{7,2},{8,13},{9,12},{10,... | collective-permute-start | bytes 24584 | tf_op jit(solution)/shard_map/ppermute | solution.py:57
  88.4 6.3 %collective-permute-start.28 = (f32[2,1024]{1,0:T(2,128)S(1)}, f32[2,1024]{1,0:T(2,128)S(1)}, u32[]{:S(2)}, u32[]{:S(2)}) collective-permute-start(f32[2,1024]{1,0:T(2,128)S(1)} %add.81.refs_4_), channel_id=1, source_target_pairs={{0,2},{1,3},{2,0},{3,1},{4,6},{5,7},{6,4},{7,5},{8,10},{9,11},{10,... | collective-permute-start | bytes 24584 | tf_op jit(solution)/shard_map/ppermute | solution.py:57
  99.5 43.6 %collective-permute-start.41 = (bf16[32,128,256]{2,1,0:T(8,128)(2,1)S(1)}, bf16[32,128,256]{2,1,0:T(8,128)(2,1)S(1)}, u32[]{:S(2)}, u32[]{:S(2)}) collective-permute-start(bf16[32,128,256]{2,1,0:T(8,128)(2,1)S(1)} %get-tuple-element.34), channel_id=1, source_target_pairs={{0,8},{8,0},{16,24},{24,16},{32,40},{40,32},{48,56},{56,48},{64,72... | collective-permute-start | bytes 6291464 | tf_op jit(solution)/shard_map/ppermute | solution.py:33
  121.5 8.7 %collective-permute-start.37 = (bf16[2,2,128,256]{3,2,1,0:T(8,128)(2,1)S(1)}, bf16[2,2,128,256]{3,2,1,0:T(8,128)(2,1)S(1)}, u32[]{:S(2)}, u32[]{:S(2)}) collective-permute-start(bf16[2,2,128,256]{3,2,1,0:T(8,128)(2,1)S(1)} %get-tuple-element.31), channel_id=1, source_target_pairs={{0,7},{1,2},{2,1},{3,4},{4,3},{5,6},{6,5},{7,0},{8,9},{9,8},{10,11... | collective-permute-start | bytes 786440 | tf_op jit(solution)/shard_map/ppermute | solution.py:65
  130.2 9.0 %collective-permute-start.38 = (bf16[2,2,128,256]{3,2,1,0:T(8,128)(2,1)S(1)}, bf16[2,2,128,256]{3,2,1,0:T(8,128)(2,1)S(1)}, u32[]{:S(2)}, u32[]{:S(2)}) collective-permute-start(bf16[2,2,128,256]{3,2,1,0:T(8,128)(2,1)S(1)} %add_convert_fusion.3), channel_id=1, source_target_pairs={{0,1},{1,0},{2,3},{3,2},{4,5},{5,4},{6,7},{7,6},{8,15},{9,10},{10,... | collective-permute-start | bytes 786440 | tf_op jit(solution)/shard_map/ppermute | solution.py:65
  139.3 9.6 %collective-permute-start.39 = (bf16[2,2,128,256]{3,2,1,0:T(8,128)(2,1)S(1)}, bf16[2,2,128,256]{3,2,1,0:T(8,128)(2,1)S(1)}, u32[]{:S(2)}, u32[]{:S(2)}) collective-permute-start(bf16[2,2,128,256]{3,2,1,0:T(8,128)(2,1)S(1)} %add_convert_fusion.2), channel_id=1, source_target_pairs={{0,7},{1,2},{2,1},{3,4},{4,3},{5,6},{6,5},{7,0},{8,9},{9,8},{10,11... | collective-permute-start | bytes 786440 | tf_op jit(solution)/shard_map/ppermute | solution.py:65
  144.1 12.8 %collective-permute-start.44 = (bf16[8,128,256]{2,1,0:T(8,128)(2,1)S(1)}, bf16[8,128,256]{2,1,0:T(8,128)(2,1)S(1)}, u32[]{:S(2)}, u32[]{:S(2)}) collective-permute-start(bf16[8,128,256]{2,1,0:T(8,128)(2,1)S(1)} %get-tuple-element.41), channel_id=1, source_target_pairs={{0,32},{8,136},{16,48},{24,152},{32,0},{40,168},{48,16},{56,184},{... | collective-permute-start | bytes 1572872 | tf_op jit(solution)/shard_map/ppermute | solution.py:45
  145.7 17.5 %collective-permute-start.43 = (bf16[8,128,256]{2,1,0:T(8,128)(2,1)S(1)}, bf16[8,128,256]{2,1,0:T(8,128)(2,1)S(1)}, u32[]{:S(2)}, u32[]{:S(2)}) collective-permute-start(bf16[8,128,256]{2,1,0:T(8,128)(2,1)S(1)} %get-tuple-element.42), channel_id=1, source_target_pairs={{0,48},{8,200},{16,32},{24,216},{32,16},{40,232},{48,0},{56,248},{... | collective-permute-start | bytes 1572872 | tf_op jit(solution)/shard_map/ppermute | solution.py:45
  146.7 17.6 %collective-permute-start.42 = (bf16[8,128,256]{2,1,0:T(8,128)(2,1)S(1)}, bf16[8,128,256]{2,1,0:T(8,128)(2,1)S(1)}, u32[]{:S(2)}, u32[]{:S(2)}) collective-permute-start(bf16[8,128,256]{2,1,0:T(8,128)(2,1)S(1)} %get-tuple-element.40), channel_id=1, source_target_pairs={{0,16},{8,72},{16,0},{24,88},{32,48},{40,104},{48,32},{56,120},{64... | collective-permute-start | bytes 1572872 | tf_op jit(solution)/shard_map/ppermute | solution.py:45
  149.0 19.2 %collective-permute-start.40 = (bf16[2,128,256]{2,1,0:T(8,128)(2,1)S(1)}, bf16[2,128,256]{2,1,0:T(8,128)(2,1)S(1)}, u32[]{:S(2)}, u32[]{:S(2)}) collective-permute-start(bf16[2,128,256]{2,1,0:T(8,128)(2,1)S(1)} %fusion.5), channel_id=1, source_target_pairs={{0,1},{1,0},{2,3},{3,2},{4,5},{5,4},{6,7},{7,6},{8,15},{9,10},{10,... | collective-permute-start | bytes 393224 | tf_op jit(solution)/shard_map/ppermute | solution.py:65
  164.6 6.7 %collective-permute-start.47 = (bf16[2,128,256]{2,1,0:T(8,128)(2,1)S(1)}, bf16[2,128,256]{2,1,0:T(8,128)(2,1)S(1)}, u32[]{:S(2)}, u32[]{:S(2)}) collective-permute-start(bf16[2,128,256]{2,1,0:T(8,128)(2,1)S(1)} %get-tuple-element.44), channel_id=1, source_target_pairs={{0,128},{8,40},{16,144},{24,56},{32,160},{40,8},{48,176},{56,24},{... | collective-permute-start | bytes 393224 | tf_op jit(solution)/shard_map/ppermute | solution.py:51
  165.1 7.5 %collective-permute-start.46 = (bf16[2,128,256]{2,1,0:T(8,128)(2,1)S(1)}, bf16[2,128,256]{2,1,0:T(8,128)(2,1)S(1)}, u32[]{:S(2)}, u32[]{:S(2)}) collective-permute-start(bf16[2,128,256]{2,1,0:T(8,128)(2,1)S(1)} %get-tuple-element.45), channel_id=1, source_target_pairs={{0,192},{8,56},{16,208},{24,40},{32,224},{40,24},{48,240},{56,8},{... | collective-permute-start | bytes 393224 | tf_op jit(solution)/shard_map/ppermute | solution.py:51
  (31 other events, 359.7 us)

commit v2 on v1

--- a/solution.py
+++ b/solution.py
@@ -9,7 +9,7 @@
 from jax.sharding import PartitionSpec as P
 
 
-PAIRS = 12
+GROUPS = 7
 TEMP = 0.02
 OFFSET = 0.3
 EPS = 1e-06
@@ -93,14 +93,16 @@
 
 
 def col_sum_parts(v):
-    v = v + over_z(v, 1)
-    return (v,) + tuple(over_z(v, d) for d in (5, 2, 6))
+    v = v + over_z(v.astype(BF16), 1).astype(F32)
+    low = v.astype(BF16)
+    return (v,) + tuple(over_z(low, d) for d in (5, 2, 6))
 
 
 def blk_sum_parts(v):
     v = v + swap(v.astype(BF16)).astype(F32)
     low = v.astype(BF16)
-    v = v + sum(over_x(low, d).astype(F32) for d in (1, 3, 2))
+    for d in (1, 3, 2):
+        v = v + over_x(low, d).astype(F32)
     low = v.astype(BF16)
     parts = [v]
     for d in (1, 3, 2):
@@ -116,7 +118,8 @@
     s = s.astype(BF16).reshape(4, 2, 128, 256)
     t = s[0].astype(F32)
     for d in (1, 3, 2):
-        t = t + over_second(s[d], d).astype(F32)
+        came = over_second(s[d], d)
+        t = t + came.astype(F32)
     keep = pick(core, t[0], t[1])
     came = swap(pick(core, t[1], t[0]).astype(BF16)).astype(F32)
     return pick(core, jnp.stack([keep, came]), jnp.stack([came, keep]))
@@ -131,15 +134,18 @@
     return jnp.where(even, pair[0], pair[1]) + came.astype(F32)
 
 
-def slot_of(meta, s):
+def group_of(meta, g):
     counts, candidates, home = meta
-    first = counts[0]
-    p = jnp.where(s >= first, 1, 0)
-    return p, home[candidates[p, s - first * p]]
+    first = lax.shift_right_logical(counts[0] + 1, 1)
+    p = jnp.where(g >= first, 1, 0)
+    k = jnp.minimum(2 * (g - first * p), 6)
+    both = k + 1 < counts[p]
+    return p, (home[candidates[p, k]], home[candidates[p, jnp.where(both, k + 1, k)]]), both
 
 
 def live(meta):
-    return meta[0][0] + meta[0][1]
+    counts = meta[0]
+    return lax.shift_right_logical(counts[0] + 1, 1) + lax.shift_right_logical(counts[1] + 1, 1)
 
 
 def place():
@@ -169,55 +175,73 @@
     return jnp.where(row == 0, high, jnp.where(row == 1, v - high, 0.0)).astype(BF16)
 
 
-def build_kernel(*refs):
-    meta, refs = refs[:3], refs[3:]
-    src = refs[:4]
-    tgt = refs[4:12]
-    mass, kt, tiles, raw, rows, unit_src, acc, sems = refs[12:]
-    n = live(meta)
-    b, z, my_y, my_x, my_k = place()
-
-    def fetch(s, _):
-        _, j = slot_of(meta, s)
-        i, owner = j % 2, j // 2
-        dy, dx = (owner // 8) ^ my_y, ((owner // 2) % 4) ^ my_x
-        first, second = jnp.where(i == 0, dx, dy), jnp.where(i == 0, dy, dx)
-        array = second + jnp.where(i == my_k, 0, 4)
-        at = first * 2 + owner % 2
-        for a in range(8):
-
-            @pl.when(array == a)
-            def _():
-                pltpu.make_async_copy(tgt[a].at[at], tiles.at[s], sems.at[s]).start()
-
-        return 0
-
-    lax.fori_loop(0, n, fetch, 0)
-    for ref, places in zip(src, chunk_places(b, z)):
+def unit_kernel(s0, s1, s2, s3, raw, unit_src):
+    b, z = place()[:2]
+    for ref, places in zip((s0, s1, s2, s3), chunk_places(b, z)):
         for h, at in enumerate(places):
             for p in range(2):
                 chunk = ref[h, p]
                 raw[p, pl.ds(at, 128), :] = chunk
                 unit_src[p, pl.ds(at, 128), :] = unit(chunk)
+
+
+def build_kernel(*refs):
+    meta, refs = refs[:3], refs[3:]
+    tgt = refs[:8]
+    unit_src, mass, kt, tiles, rows, acc, sems = refs[8:]
+    n = live(meta)
+    _, z, my_y, my_x, my_k = place()
+
+    def fetch(g, _):
+        _, targets, _ = group_of(meta, g)
+        for h, j in enumerate(targets):
+            i, owner = j % 2, j // 2
+            dy, dx = (owner // 8) ^ my_y, ((owner // 2) % 4) ^ my_x
+            first, second = jnp.where(i == 0, dx, dy), jnp.where(i == 0, dy, dx)
+            array = second + jnp.where(i == my_k, 0, 4)
+            at = first * 2 + owner % 2
+            for a in range(8):
+
+                @pl.when(array == a)
+                def _():
+                    pltpu.make_async_copy(
+                        tgt[a].at[at], tiles.at[g, pl.ds(h * 128, 128), :], sems.at[g, h]
+                    ).start()
+
+        return 0
+
+    lax.fori_loop(0, n, fetch, 0)
     acc[...] = jnp.zeros_like(acc)
     scale = math.log2(math.e) / (256 * TEMP)
     shift = OFFSET / TEMP * math.log2(math.e)
 
-    def step(s, _):
-        p, _ = slot_of(meta, s)
-        pltpu.make_async_copy(tgt[0].at[0], tiles.at[s], sems.at[s]).wait()
-        tile = unit(tiles[s])
+    def step(g, _):
+        p, _, both = group_of(meta, g)
+        for h in range(2):
+            pltpu.make_async_copy(
+                tgt[0].at[0], tiles.at[g, pl.ds(h * 128, 128), :], sems.at[g, h]
+            ).wait()
+        tile = unit(tiles[g])
+        keep = jnp.where(both, 1.0, 0.0)
         for c in range(4):
             cols = slice(c * 256, (c + 1) * 256)
             score = lax.dot_general(
                 tile, unit_src[p, cols, :], (((1,), (1,)), ((), ())), preferred_element_type=F32
             )
             k = jnp.exp2(score * scale - shift)
-            kt[s, :, cols] = k.astype(BF16)
-            acc[p, :, cols] += k.reshape(16, 8, 256).sum(axis=0)
+            upper, lower = k[:128], k[128:] * keep
+            kt[g, :128, cols] = upper.astype(BF16)
+            kt[g, 128:, cols] = lower.astype(BF16)
+            acc[p, :, cols] += (upper + lower).reshape(16, 8, 256).sum(axis=0)
         return 0
 
     lax.fori_loop(0, n, step, 0)
+
+    def clear(g, _):
+        kt[g] = jnp.zeros_like(kt[g])
+        return 0
+
+    lax.fori_loop(n, GROUPS, clear, 0)
     lane = lax.broadcasted_iota(jnp.int32, (1, 1024), 1) // 128
     for p in range(2):
         rows[p : p + 1, :] = jnp.sum(acc[p], axis=0, keepdims=True)
@@ -229,12 +253,12 @@
     meta, refs = refs[:3], refs[3:]
     if first:
         kt, r0, r1, r2, r3, tgt_mass, out, mass_out, u_rows = refs
-        total = (r0[...] + r1[...]) + (r2[...] + r3[...])
+        total = r0[...] + r1[...].astype(F32) + r2[...].astype(F32) + r3[...].astype(F32)
         mass = total[2:4]
         mass_out[...] = mass
     else:
         kt, r0, r1, r2, r3, mass_in, out, u_out, u_rows = refs
-        total = (r0[...] + r1[...]) + (r2[...] + r3[...])
+        total = r0[...] + r1[...].astype(F32) + r2[...].astype(F32) + r3[...].astype(F32)
         mass = mass_in[...]
     u = mass / total[0:2]
     if not first:
@@ -243,15 +267,16 @@
         u_rows[p] = two_rows(u[p : p + 1])
     out[...] = jnp.zeros_like(out)
 
-    def step(s, _):
-        p, j = slot_of(meta, s)
+    found = []
+    for g in range(GROUPS):
+        p, targets, _ = group_of(meta, g)
         part = lax.dot_general(
-            u_rows[p], kt[s], (((1,), (1,)), ((), ())), preferred_element_type=F32
+            u_rows[p], kt[g], (((1,), (1,)), ((), ())), preferred_element_type=F32
         )
-        out[pl.ds(j, 1), :] += part[0:1] + part[1:2]
-        return 0
-
-    lax.fori_loop(0, live(meta), step, 0)
+        found.append((targets, part[0:1] + part[1:2]))
+    for targets, part in found:
+        for h, j in enumerate(targets):
+            out[pl.ds(j, 1), :] += part[:, h * 128 : (h + 1) * 128]
     if first:
         b = place()[0]
         out[pl.ds(64 + 2 * b, 1), :] = tgt_mass[0:1, :].astype(F32)
@@ -266,13 +291,13 @@
     v_all[...] = total[64:] / total[:64]
     acc[...] = jnp.zeros_like(acc)
 
-    def step(s, _):
-        p, j = slot_of(meta, s)
-        v = two_rows(v_all[pl.ds(j, 1), :])
-        acc[p] += jnp.dot(v, kt[s], preferred_element_type=F32)[:8]
-        return 0
-
-    lax.fori_loop(0, live(meta), step, 0)
+    found = []
+    for g in range(GROUPS):
+        p, targets, _ = group_of(meta, g)
+        v = two_rows(jnp.concatenate([v_all[pl.ds(j, 1), :] for j in targets], axis=1))
+        found.append((p, jnp.dot(v, kt[g], preferred_element_type=F32)[:8]))
+    for p, part in found:
+        acc[p] += part
     for p in range(2):
         out[p : p + 1, :] = acc[p, 0:1, :] + acc[p, 1:2, :]
 
@@ -284,22 +309,24 @@
     mine[...] = jnp.zeros_like(mine)
     other[...] = jnp.zeros_like(other)
 
-    def step(s, _):
-        p, j = slot_of(meta, s)
+    def step(g, _):
+        p, targets, _ = group_of(meta, g)
         row = jnp.where(p == 0, u[0:1, :], u[1:2, :])
-        plan = (kt[s].astype(F32) * row).astype(BF16)
-        back = jnp.dot(plan, raw[p], preferred_element_type=F32)
-        i, owner = j % 2, j // 2
-        dy, dx = (owner // 8) ^ my_y, ((owner // 2) % 4) ^ my_x
-        at = jnp.where(i == 0, dx * 8 + dy * 2, dy * 8 + dx * 2) + owner % 2
-
-        @pl.when(i == my_k)
-        def _():
-            mine[at] = (mine[at].astype(F32) + back).astype(BF16)
-
-        @pl.when(i != my_k)
-        def _():
-            other[at] = (other[at].astype(F32) + back).astype(BF16)
+        plan = (kt[g].astype(F32) * row).astype(BF16)
+        both = jnp.dot(plan, raw[p], preferred_element_type=F32)
+        for h, j in enumerate(targets):
+            back = both[h * 128 : (h + 1) * 128]
+            i, owner = j % 2, j // 2
+            dy, dx = (owner // 8) ^ my_y, ((owner // 2) % 4) ^ my_x
+            at = jnp.where(i == 0, dx * 8 + dy * 2, dy * 8 + dx * 2) + owner % 2
+
+            @pl.when(i == my_k)
+            def _():
+                mine[at] = (mine[at].astype(F32) + back).astype(BF16)
+
+            @pl.when(i != my_k)
+            def _():
+                other[at] = (other[at].astype(F32) + back).astype(BF16)
 
         return 0
 
@@ -316,25 +343,28 @@
     v_out[1:2, :] = v_all[pl.ds(2 * b + 1, 1), :]
     acc[...] = jnp.zeros_like(acc)
 
-    def step(s, _):
-        p, j = slot_of(meta, s)
-        v = jnp.broadcast_to(v_all[pl.ds(j, 1), :], (128, 128)).T
+    def step(g, _):
+        p, targets, _ = group_of(meta, g)
+        v = [jnp.broadcast_to(v_all[pl.ds(j, 1), :], (128, 128)).T for j in targets]
+        v = jnp.concatenate(v, axis=0)
         row = jnp.where(p == 0, u[0:1, :], u[1:2, :])
-        plan = []
-        for c in range(8):
-            cols = slice(c * 128, (c + 1) * 128)
-            plan.append((kt[s, :, cols].astype(F32) * row[:, cols] * v).astype(BF16))
-        plan = jnp.concatenate(plan, axis=1)
-        acc[p] += lax.dot_general(
-            plan, tiles[s], (((0,), (0,)), ((), ())), preferred_element_type=F32
-        )
+        tile = tiles[g].T
+        for c in range(4):
+            plan = []
+            for d in range(2):
+                cols = slice(c * 256 + d * 128, c * 256 + (d + 1) * 128)
+                plan.append((kt[g, :, cols].astype(F32) * row[:, cols] * v).astype(BF16))
+            cols = slice(c * 256, (c + 1) * 256)
+            acc[p, :, cols] += jnp.dot(
+                tile, jnp.concatenate(plan, axis=1), preferred_element_type=F32
+            )
         return 0
 
     lax.fori_loop(0, live(meta), step, 0)
     for ref, places in zip((out1, out2, out3, out4), chunk_places(b, z)):
         for h, at in enumerate(places):
             for p in range(2):
-                ref[h, p] = acc[p, pl.ds(at, 128), :].astype(BF16)
+                ref[h, p] = acc[p, :, pl.ds(at, 128)].astype(BF16).T
 
 
 def call(kernel, out_shape, in_specs, scratch, args, flops, nbytes):
@@ -356,21 +386,15 @@
     sources = gather_sources(src_feat, even)
     targets = gather_targets(tgt_feat, core)
     S = jax.ShapeDtypeStruct
-    kt, tiles, raw, rows = call(
+    raw, unit_src = call(
+        unit_kernel, [S((2, 1024, 256), BF16)] * 2, [VMEM] * 4, [], sources, 2_000_000, 3_000_000
+    )
+    kt, tiles, rows = call(
         build_kernel,
-        [
-            S((PAIRS, 128, 1024), BF16),
-            S((PAIRS, 128, 256), BF16),
-            S((2, 1024, 256), BF16),
-            S((4, 1024), F32),
-        ],
-        [SMEM] * 3 + [VMEM] * 4 + [ANY] * 8 + [VMEM],
-        [
-            pltpu.VMEM((2, 1024, 256), BF16),
-            pltpu.VMEM((2, 8, 1024), F32),
-            pltpu.SemaphoreType.DMA((PAIRS,)),
-        ],
-        (*meta, *sources, *targets, src_mass),
+        [S((GROUPS, 256, 1024), BF16), S((GROUPS, 256, 256), BF16), S((4, 1024), F32)],
+        [SMEM] * 3 + [ANY] * 8 + [VMEM] * 2,
+        [pltpu.VMEM((2, 8, 1024), F32), pltpu.SemaphoreType.DMA((GROUPS, 2))],
+        (*meta, *targets, unit_src, src_mass),
         800_000_000,
         7_000_000,
     )
@@ -417,7 +441,7 @@
         toward_kernel,
         [S((2, 2, 128, 256), BF16)] * 4 + [S((2, 128), F32)],
         [SMEM] * 3 + [VMEM] * 8,
-        [pltpu.VMEM((64, 128), F32), pltpu.VMEM((2, 1024, 256), F32)],
+        [pltpu.VMEM((64, 128), F32), pltpu.VMEM((2, 256, 1024), F32)],
         (*meta, kt, u, tiles, *parts, mass_tgt),
         800_000_000,
         6_000_000,

time: 176 us -> 177 us (level)
    pallas_call x6 -> x7, Pallas kernels: 11.5 us -> 12.2 us  [call(): pl.pallas_call(kernel, out_shape=out_shape, in_specs=in_specs, out_specs=...]
  transfers between devices with their start and end apart: 49 -> 49, of which waited for: 34 -> 34; matrix products, arithmetic and copies ran while one was open for 2% -> 2% of each run, Pallas kernels for 1% -> 2%
where the time goes in v2:
time: 177 us; the launch traced here: 175 us
  waiting for transfers between devices  90.5 us (51%)
  starting transfers between devices  66.7 us (38%)
  Pallas kernels  12.2 us (7%)
  other arithmetic  3.18 us (2%)
    ppermute x8, waiting for transfers between devices, along_z(): return lax.ppermute(v, ('blk', 'col'), pairs)  34 us
    ppermute x6, waiting for transfers between devices, over_first(): lax.ppermute(v, 'blk', blk_perm(lambda y, x, k: (y, x ^ d, k) if k == 0 e...  19.5 us
    ppermute x8, starting transfers between devices, along_z(): return lax.ppermute(v, ('blk', 'col'), pairs)  16.8 us
    ppermute x8, waiting for transfers between devices, over_z(): return lax.ppermute(v, 'col', [(i, i ^ d) for i in range(8)])  15.3 us
    pallas_call x7, Pallas kernels, call(): pl.pallas_call(kernel, out_shape=out_shape, in_specs=in_specs, out_specs=...  12.2 us
    ppermute x8, starting transfers between devices, over_z(): return lax.ppermute(v, 'col', [(i, i ^ d) for i in range(8)])  11.8 us
    ppermute x6, starting transfers between devices, over_x(): return lax.ppermute(v, 'blk', blk_perm(lambda y, x, k: (y, x ^ d, k)))  9.56 us
    ppermute x6, starting transfers between devices, over_first(): lax.ppermute(v, 'blk', blk_perm(lambda y, x, k: (y, x ^ d, k) if k == 0 e...  9.18 us
  transfers between devices with their start and end apart: 49, of which 34 were waited for; matrix products, arithmetic and copies ran while one was open for 2% of the time, Pallas kernels for 2%

profile of v2, /device:TPU:2, one launch (start us, length us, event | category | flops | bytes accessed | tf_op | source)
XLA Modules:
  0.0 174.8 jit_solution(3734994136414798355)
XLA Ops:
  7.4 3.0 %collective-permute-done.2 = bf16[2,128,256]{2,1,0:T(8,128)(2,1)S(1)} collective-permute-done((bf16[2,128,256]{2,1,0:T(8,128)(2,1)S(1)}, bf16[2,128,256]{2,1,0:T(8,128)(2,1)S(1)}, u32[]{:S(2)}, u32[]{:S(2)}) %collective-permute-start.2) | collective-permute-done | bytes 131104 | tf_op jit(solution)/shard_map/ppermute | solution.py:45
  12.6 2.9 %collective-permute-start.5 = (bf16[8,128,256]{2,1,0:T(8,128)(2,1)S(1)}, bf16[8,128,256]{2,1,0:T(8,128)(2,1)S(1)}, u32[]{:S(2)}, u32[]{:S(2)}) collective-permute-start(bf16[8,128,256]{2,1,0:T(8,128)(2,1)S(1)} %pad_maximum_fusion.refs_3_), channel_id=1, source_target_pairs={{0,128},{8,40},{16,144},{24,56},{32,160},{40,8},{48,176},{56,24},{... | collective-permute-start | bytes 1572872 | tf_op jit(solution)/shard_map/ppermute | solution.py:51
  17.7 4.1 %collective-permute-done.11 = bf16[2,128,256]{2,1,0:T(8,128)(2,1)S(1)} collective-permute-done((bf16[2,128,256]{2,1,0:T(8,128)(2,1)}, bf16[2,128,256]{2,1,0:T(8,128)(2,1)S(1)}, u32[]{:S(2)}, u32[]{:S(2)}) %collective-permute-start.11) | collective-permute-done | bytes 131104 | tf_op jit(solution)/shard_map/ppermute | solution.py:65
  21.8 5.1 %collective-permute-start.12 = (bf16[2,2,128,256]{3,2,1,0:T(8,128)(2,1)S(1)}, bf16[2,2,128,256]{3,2,1,0:T(8,128)(2,1)S(1)}, u32[]{:S(2)}, u32[]{:S(2)}) collective-permute-start(bf16[2,2,128,256]{3,2,1,0:T(8,128)(2,1)S(1)} %maximum_select_fusion.s0), channel_id=1, source_target_pairs={{0,7},{1,2},{2,1},{3,4},{4,3},{5,6},{6,5},{7,0},{8,9},{9,8},{10,11... | collective-permute-start | bytes 786440 | tf_op jit(solution)/shard_map/ppermute | solution.py:65
  26.9 4.4 %collective-permute-done.12.s1 = bf16[2,2,128,256]{3,2,1,0:T(8,128)(2,1)S(1)} collective-permute-done((bf16[2,2,128,256]{3,2,1,0:T(8,128)(2,1)S(1)}, bf16[2,2,128,256]{3,2,1,0:T(8,128)(2,1)S(1)}, u32[]{:S(2)}, u32[]{:S(2)}) %collective-permute-start.12) | collective-permute-done | bytes 262176 | tf_op jit(solution)/shard_map/ppermute | solution.py:65
  32.3 6.4 %collective-permute-done.13.s2 = bf16[2,2,128,256]{3,2,1,0:T(8,128)(2,1)S(1)} collective-permute-done((bf16[2,2,128,256]{3,2,1,0:T(8,128)(2,1)S(1)}, bf16[2,2,128,256]{3,2,1,0:T(8,128)(2,1)S(1)}, u32[]{:S(2)}, u32[]{:S(2)}) %collective-permute-start.13) | collective-permute-done | bytes 262176 | tf_op jit(solution)/shard_map/ppermute | solution.py:65
  38.7 3.5 %collective-permute-start.14 = (bf16[2,2,128,256]{3,2,1,0:T(8,128)(2,1)S(1)}, bf16[2,2,128,256]{3,2,1,0:T(8,128)(2,1)S(1)}, u32[]{:S(2)}, u32[]{:S(2)}) collective-permute-start(bf16[2,2,128,256]{3,2,1,0:T(8,128)(2,1)S(1)} %collective-permute-done.13.s2), channel_id=1, source_target_pairs={{0,7},{1,2},{2,1},{3,4},{4,3},{5,6},{6,5},{7,0},{8,9},{9,8},{10,11... | collective-permute-start | bytes 786440 | tf_op jit(solution)/shard_map/ppermute | solution.py:65
  42.2 4.3 %collective-permute-done.14.s3 = bf16[2,2,128,256]{3,2,1,0:T(8,128)(2,1)S(1)} collective-permute-done((bf16[2,2,128,256]{3,2,1,0:T(8,128)(2,1)S(1)}, bf16[2,2,128,256]{3,2,1,0:T(8,128)(2,1)S(1)}, u32[]{:S(2)}, u32[]{:S(2)}) %collective-permute-start.14) | collective-permute-done | bytes 262176 | tf_op jit(solution)/shard_map/ppermute | solution.py:65
  47.1 3.2 %shard_map.87 = (bf16[7,256,1024]{2,1,0:T(8,128)(2,1)S(1)}, bf16[7,256,256]{2,1,0:T(8,128)(2,1)S(1)}, f32[4,1024]{1,0:T(4,128)S(1)}) custom-call(s32[2]{0:T(128)S(1)} %copy-done.1, s32[2,8]{1,0:T(2,128)S(1)} %copy-done, s32[64]{0:T(128)S(1)} %copy-done.2, bf16[8,128,256]{2,1,0:T(8,128)(2,1)S(1)} %pad_maximum_fusion.refs_3_, ...), custom_call_target="tpu_custom_call" | custom-call | flops 800000000 | bytes 7000000 | tf_op jit(solution)/shard_map/pallas_call | solution.py:371
  50.3 3.6 %collective-permute-done.15 = bf16[4,1024]{1,0:T(4,128)(2,1)S(1)} collective-permute-done((bf16[4,1024]{1,0:T(4,128)(2,1)S(1)}, bf16[4,1024]{1,0:T(4,128)(2,1)S(1)}, u32[]{:S(2)}, u32[]{:S(2)}) %collective-permute-start.15) | collective-permute-done | bytes 8224 | tf_op jit(solution)/shard_map/ppermute | solution.py:57
  54.0 3.2 %collective-permute-start.16 = (bf16[4,1024]{1,0:T(4,128)(2,1)S(1)}, bf16[4,1024]{1,0:T(4,128)(2,1)S(1)}, u32[]{:S(2)}, u32[]{:S(2)}) collective-permute-start(bf16[4,1024]{1,0:T(4,128)(2,1)S(1)} %get-tuple-element.44), channel_id=1, source_target_pairs={{0,5},{1,4},{2,7},{3,6},{4,1},{5,0},{6,3},{7,2},{8,13},{9,12},{10,... | collective-permute-start | bytes 24584 | tf_op jit(solution)/shard_map/ppermute | solution.py:57
  61.8 3.7 %collective-permute-done.18.refs_7_ = bf16[4,1024]{1,0:T(4,128)(2,1)S(1)} collective-permute-done((bf16[4,1024]{1,0:T(4,128)(2,1)S(1)}, bf16[4,1024]{1,0:T(4,128)(2,1)S(1)}, u32[]{:S(2)}, u32[]{:S(2)}) %collective-permute-start.18) | collective-permute-done | bytes 8224 | tf_op jit(solution)/shard_map/ppermute | solution.py:57
  70.1 3.1 %collective-permute-start.20 = (bf16[128,128]{1,0:T(8,128)(2,1)S(1)}, bf16[128,128]{1,0:T(8,128)(2,1)S(1)}, u32[]{:S(2)}, u32[]{:S(2)}) collective-permute-start(bf16[128,128]{1,0:T(8,128)(2,1)S(1)} %fusion.7), channel_id=1, source_target_pairs={{0,16},{8,24},{16,0},{24,8},{32,48},{40,56},{48,32},{56,40},{64,80... | collective-permute-start | bytes 98312 | tf_op jit(solution)/shard_map/ppermute | solution.py:37
  75.5 3.2 %collective-permute-start.24 = (bf16[128,128]{1,0:T(8,128)(2,1)S(1)}, bf16[128,128]{1,0:T(8,128)(2,1)S(1)}, u32[]{:S(2)}, u32[]{:S(2)}) collective-permute-start(bf16[128,128]{1,0:T(8,128)(2,1)S(1)} %get-tuple-element.42), channel_id=1, source_target_pairs={{0,192},{8,200},{16,208},{24,216},{32,224},{40,232},{48,240},{56,2... | collective-permute-start | bytes 98312 | tf_op jit(solution)/shard_map/ppermute | solution.py:41
  80.7 3.4 %collective-permute-done.25.refs_7_ = bf16[128,128]{1,0:T(8,128)(2,1)S(1)} collective-permute-done((bf16[128,128]{1,0:T(8,128)(2,1)S(1)}, bf16[128,128]{1,0:T(8,128)(2,1)S(1)}, u32[]{:S(2)}, u32[]{:S(2)}) %collective-permute-start.25) | collective-permute-done | bytes 32800 | tf_op jit(solution)/shard_map/ppermute | solution.py:41
  85.8 3.2 %collective-permute-done.26 = bf16[2,1024]{1,0:T(2,128)(2,1)S(1)} collective-permute-done((bf16[2,1024]{1,0:T(2,128)(2,1)S(1)}, bf16[2,1024]{1,0:T(2,128)(2,1)S(1)}, u32[]{:S(2)}, u32[]{:S(2)}) %collective-permute-start.26) | collective-permute-done | bytes 4128 | tf_op jit(solution)/shard_map/ppermute | solution.py:57
  91.5 3.0 %collective-permute-start.29 = (bf16[2,1024]{1,0:T(2,128)(2,1)S(1)}, bf16[2,1024]{1,0:T(2,128)(2,1)S(1)}, u32[]{:S(2)}, u32[]{:S(2)}) collective-permute-start(bf16[2,1024]{1,0:T(2,128)(2,1)S(1)} %get-tuple-element.40), channel_id=1, source_target_pairs={{0,6},{1,7},{2,4},{3,5},{4,2},{5,3},{6,0},{7,1},{8,14},{9,15},{10,... | collective-permute-start | bytes 12296 | tf_op jit(solution)/shard_map/ppermute | solution.py:57
  101.5 3.7 %collective-permute-done.30 = bf16[64,128]{1,0:T(8,128)(2,1)S(1)} collective-permute-done((bf16[64,128]{1,0:T(8,128)(2,1)S(1)}, bf16[64,128]{1,0:T(8,128)(2,1)S(1)}, u32[]{:S(2)}, u32[]{:S(2)}) %collective-permute-start.30) | collective-permute-done | bytes 16416 | tf_op jit(solution)/shard_map/ppermute | solution.py:33
  121.7 3.3 %collective-permute-start.37 = (bf16[2,2,128,256]{3,2,1,0:T(8,128)(2,1)S(1)}, bf16[2,2,128,256]{3,2,1,0:T(8,128)(2,1)S(1)}, u32[]{:S(2)}, u32[]{:S(2)}) collective-permute-start(bf16[2,2,128,256]{3,2,1,0:T(8,128)(2,1)S(1)} %get-tuple-element.33), channel_id=1, source_target_pairs={{0,7},{1,2},{2,1},{3,4},{4,3},{5,6},{6,5},{7,0},{8,9},{9,8},{10,11... | collective-permute-start | bytes 786440 | tf_op jit(solution)/shard_map/ppermute | solution.py:65
  125.0 5.8 %collective-permute-done.37 = bf16[2,2,128,256]{3,2,1,0:T(8,128)(2,1)S(1)} collective-permute-done((bf16[2,2,128,256]{3,2,1,0:T(8,128)(2,1)S(1)}, bf16[2,2,128,256]{3,2,1,0:T(8,128)(2,1)S(1)}, u32[]{:S(2)}, u32[]{:S(2)}) %collective-permute-start.37) | collective-permute-done | bytes 262176 | tf_op jit(solution)/shard_map/ppermute | solution.py:65
  131.0 9.0 %collective-permute-done.38 = bf16[2,2,128,256]{3,2,1,0:T(8,128)(2,1)S(1)} collective-permute-done((bf16[2,2,128,256]{3,2,1,0:T(8,128)(2,1)S(1)}, bf16[2,2,128,256]{3,2,1,0:T(8,128)(2,1)S(1)}, u32[]{:S(2)}, u32[]{:S(2)}) %collective-permute-start.38) | collective-permute-done | bytes 262176 | tf_op jit(solution)/shard_map/ppermute | solution.py:65
  140.0 3.7 %collective-permute-start.39 = (bf16[2,2,128,256]{3,2,1,0:T(8,128)(2,1)S(1)}, bf16[2,2,128,256]{3,2,1,0:T(8,128)(2,1)S(1)}, u32[]{:S(2)}, u32[]{:S(2)}) collective-permute-start(bf16[2,2,128,256]{3,2,1,0:T(8,128)(2,1)S(1)} %add_convert_fusion.2), channel_id=1, source_target_pairs={{0,7},{1,2},{2,1},{3,4},{4,3},{5,6},{6,5},{7,0},{8,9},{9,8},{10,11... | collective-permute-start | bytes 786440 | tf_op jit(solution)/shard_map/ppermute | solution.py:65
  149.7 8.1 %collective-permute-done.44 = bf16[8,128,256]{2,1,0:T(8,128)(2,1)S(1)} collective-permute-done((bf16[8,128,256]{2,1,0:T(8,128)(2,1)S(1)}, bf16[8,128,256]{2,1,0:T(8,128)(2,1)S(1)}, u32[]{:S(2)}, u32[]{:S(2)}) %collective-permute-start.44) | collective-permute-done | bytes 524320 | tf_op jit(solution)/shard_map/ppermute | solution.py:45
  157.8 5.6 %collective-permute-done.43 = bf16[8,128,256]{2,1,0:T(8,128)(2,1)S(1)} collective-permute-done((bf16[8,128,256]{2,1,0:T(8,128)(2,1)S(1)}, bf16[8,128,256]{2,1,0:T(8,128)(2,1)S(1)}, u32[]{:S(2)}, u32[]{:S(2)}) %collective-permute-start.43) | collective-permute-done | bytes 524320 | tf_op jit(solution)/shard_map/ppermute | solution.py:45
  (124 shorter events, 71.2 us)
Async XLA Ops:
  4.0 6.5 %collective-permute-start.2 = (bf16[2,128,256]{2,1,0:T(8,128)(2,1)S(1)}, bf16[2,128,256]{2,1,0:T(8,128)(2,1)S(1)}, u32[]{:S(2)}, u32[]{:S(2)}) collective-permute-start(bf16[2,128,256]{2,1,0:T(8,128)(2,1)S(1)} %maximum_select_fusion.2), channel_id=1, source_target_pairs={{0,32},{8,136},{16,48},{24,152},{32,0},{40,168},{48,16},{56,184},{... | collective-permute-start | bytes 393224 | tf_op jit(solution)/shard_map/ppermute | solution.py:45
  11.8 19.5 %collective-permute-start.4 = (bf16[8,128,256]{2,1,0:T(8,128)(2,1)S(1)}, bf16[8,128,256]{2,1,0:T(8,128)(2,1)S(1)}, u32[]{:S(2)}, u32[]{:S(2)}) collective-permute-start(bf16[8,128,256]{2,1,0:T(8,128)(2,1)S(1)} %pad_maximum_fusion.refs_3_), channel_id=1, source_target_pairs={{0,64},{8,24},{16,80},{24,8},{32,96},{40,56},{48,112},{56,40},{64,... | collective-permute-start | bytes 1572872 | tf_op jit(solution)/shard_map/ppermute | solution.py:51
  12.6 19.2 %collective-permute-start.5 = (bf16[8,128,256]{2,1,0:T(8,128)(2,1)S(1)}, bf16[8,128,256]{2,1,0:T(8,128)(2,1)S(1)}, u32[]{:S(2)}, u32[]{:S(2)}) collective-permute-start(bf16[8,128,256]{2,1,0:T(8,128)(2,1)S(1)} %pad_maximum_fusion.refs_3_), channel_id=1, source_target_pairs={{0,128},{8,40},{16,144},{24,56},{32,160},{40,8},{48,176},{56,24},{... | collective-permute-start | bytes 1572872 | tf_op jit(solution)/shard_map/ppermute | solution.py:51
  15.5 16.4 %collective-permute-start.6 = (bf16[8,128,256]{2,1,0:T(8,128)(2,1)S(1)}, bf16[8,128,256]{2,1,0:T(8,128)(2,1)S(1)}, u32[]{:S(2)}, u32[]{:S(2)}) collective-permute-start(bf16[8,128,256]{2,1,0:T(8,128)(2,1)S(1)} %pad_maximum_fusion.refs_3_), channel_id=1, source_target_pairs={{0,192},{8,56},{16,208},{24,40},{32,224},{40,24},{48,240},{56,8},{... | collective-permute-start | bytes 1572872 | tf_op jit(solution)/shard_map/ppermute | solution.py:51
  21.8 9.5 %collective-permute-start.12 = (bf16[2,2,128,256]{3,2,1,0:T(8,128)(2,1)S(1)}, bf16[2,2,128,256]{3,2,1,0:T(8,128)(2,1)S(1)}, u32[]{:S(2)}, u32[]{:S(2)}) collective-permute-start(bf16[2,2,128,256]{3,2,1,0:T(8,128)(2,1)S(1)} %maximum_select_fusion.s0), channel_id=1, source_target_pairs={{0,7},{1,2},{2,1},{3,4},{4,3},{5,6},{6,5},{7,0},{8,9},{9,8},{10,11... | collective-permute-start | bytes 786440 | tf_op jit(solution)/shard_map/ppermute | solution.py:65
  31.3 7.4 %collective-permute-start.13 = (bf16[2,2,128,256]{3,2,1,0:T(8,128)(2,1)S(1)}, bf16[2,2,128,256]{3,2,1,0:T(8,128)(2,1)S(1)}, u32[]{:S(2)}, u32[]{:S(2)}) collective-permute-start(bf16[2,2,128,256]{3,2,1,0:T(8,128)(2,1)S(1)} %collective-permute-done.12.s1), channel_id=1, source_target_pairs={{0,1},{1,0},{2,3},{3,2},{4,5},{5,4},{6,7},{7,6},{8,15},{9,10},{10,... | collective-permute-start | bytes 786440 | tf_op jit(solution)/shard_map/ppermute | solution.py:65
  31.3 15.7 %collective-permute-start.7 = (bf16[8,128,256]{2,1,0:T(8,128)(2,1)S(1)}, bf16[8,128,256]{2,1,0:T(8,128)(2,1)S(1)}, u32[]{:S(2)}, u32[]{:S(2)}) collective-permute-start(bf16[8,128,256]{2,1,0:T(8,128)(2,1)S(1)} %pad_maximum_fusion.refs_3_), channel_id=1, source_target_pairs={{0,8},{8,0},{16,24},{24,16},{32,40},{40,32},{48,56},{56,48},{64,72... | collective-permute-start | bytes 1572872 | tf_op jit(solution)/shard_map/ppermute | solution.py:33
  31.3 15.7 %collective-permute-start.8 = (bf16[8,128,256]{2,1,0:T(8,128)(2,1)S(1)}, bf16[8,128,256]{2,1,0:T(8,128)(2,1)S(1)}, u32[]{:S(2)}, u32[]{:S(2)}) collective-permute-start(bf16[8,128,256]{2,1,0:T(8,128)(2,1)S(1)} %collective-permute-done.4.refs_4_), channel_id=1, source_target_pairs={{0,8},{8,0},{16,24},{24,16},{32,40},{40,32},{48,56},{56,48},{64,72... | collective-permute-start | bytes 1572872 | tf_op jit(solution)/shard_map/ppermute | solution.py:33
  31.8 15.2 %collective-permute-start.9 = (bf16[8,128,256]{2,1,0:T(8,128)(2,1)S(1)}, bf16[8,128,256]{2,1,0:T(8,128)(2,1)S(1)}, u32[]{:S(2)}, u32[]{:S(2)}) collective-permute-start(bf16[8,128,256]{2,1,0:T(8,128)(2,1)S(1)} %collective-permute-done.5.refs_5_), channel_id=1, source_target_pairs={{0,8},{8,0},{16,24},{24,16},{32,40},{40,32},{48,56},{56,48},{64,72... | collective-permute-start | bytes 1572872 | tf_op jit(solution)/shard_map/ppermute | solution.py:33
  31.9 15.1 %collective-permute-start.10 = (bf16[8,128,256]{2,1,0:T(8,128)(2,1)S(1)}, bf16[8,128,256]{2,1,0:T(8,128)(2,1)S(1)}, u32[]{:S(2)}, u32[]{:S(2)}) collective-permute-start(bf16[8,128,256]{2,1,0:T(8,128)(2,1)S(1)} %collective-permute-done.6.refs_6_), channel_id=1, source_target_pairs={{0,8},{8,0},{16,24},{24,16},{32,40},{40,32},{48,56},{56,48},{64,72... | collective-permute-start | bytes 1572872 | tf_op jit(solution)/shard_map/ppermute | solution.py:33
  38.7 7.8 %collective-permute-start.14 = (bf16[2,2,128,256]{3,2,1,0:T(8,128)(2,1)S(1)}, bf16[2,2,128,256]{3,2,1,0:T(8,128)(2,1)S(1)}, u32[]{:S(2)}, u32[]{:S(2)}) collective-permute-start(bf16[2,2,128,256]{3,2,1,0:T(8,128)(2,1)S(1)} %collective-permute-done.13.s2), channel_id=1, source_target_pairs={{0,7},{1,2},{2,1},{3,4},{4,3},{5,6},{6,5},{7,0},{8,9},{9,8},{10,11... | collective-permute-start | bytes 786440 | tf_op jit(solution)/shard_map/ppermute | solution.py:65
  54.0 6.7 %collective-permute-start.16 = (bf16[4,1024]{1,0:T(4,128)(2,1)S(1)}, bf16[4,1024]{1,0:T(4,128)(2,1)S(1)}, u32[]{:S(2)}, u32[]{:S(2)}) collective-permute-start(bf16[4,1024]{1,0:T(4,128)(2,1)S(1)} %get-tuple-element.44), channel_id=1, source_target_pairs={{0,5},{1,4},{2,7},{3,6},{4,1},{5,0},{6,3},{7,2},{8,13},{9,12},{10,... | collective-permute-start | bytes 24584 | tf_op jit(solution)/shard_map/ppermute | solution.py:57
  89.0 6.7 %collective-permute-start.27 = (bf16[2,1024]{1,0:T(2,128)(2,1)S(1)}, bf16[2,1024]{1,0:T(2,128)(2,1)S(1)}, u32[]{:S(2)}, u32[]{:S(2)}) collective-permute-start(bf16[2,1024]{1,0:T(2,128)(2,1)S(1)} %get-tuple-element.40), channel_id=1, source_target_pairs={{0,5},{1,4},{2,7},{3,6},{4,1},{5,0},{6,3},{7,2},{8,13},{9,12},{10,... | collective-permute-start | bytes 12296 | tf_op jit(solution)/shard_map/ppermute | solution.py:57
  89.5 6.2 %collective-permute-start.28 = (bf16[2,1024]{1,0:T(2,128)(2,1)S(1)}, bf16[2,1024]{1,0:T(2,128)(2,1)S(1)}, u32[]{:S(2)}, u32[]{:S(2)}) collective-permute-start(bf16[2,1024]{1,0:T(2,128)(2,1)S(1)} %get-tuple-element.40), channel_id=1, source_target_pairs={{0,2},{1,3},{2,0},{3,1},{4,6},{5,7},{6,4},{7,5},{8,10},{9,11},{10,... | collective-permute-start | bytes 12296 | tf_op jit(solution)/shard_map/ppermute | solution.py:57
  100.9 42.9 %collective-permute-start.41 = (bf16[32,128,256]{2,1,0:T(8,128)(2,1)S(1)}, bf16[32,128,256]{2,1,0:T(8,128)(2,1)S(1)}, u32[]{:S(2)}, u32[]{:S(2)}) collective-permute-start(bf16[32,128,256]{2,1,0:T(8,128)(2,1)S(1)} %get-tuple-element.36), channel_id=1, source_target_pairs={{0,8},{8,0},{16,24},{24,16},{32,40},{40,32},{48,56},{56,48},{64,72... | collective-permute-start | bytes 6291464 | tf_op jit(solution)/shard_map/ppermute | solution.py:33
  121.7 9.1 %collective-permute-start.37 = (bf16[2,2,128,256]{3,2,1,0:T(8,128)(2,1)S(1)}, bf16[2,2,128,256]{3,2,1,0:T(8,128)(2,1)S(1)}, u32[]{:S(2)}, u32[]{:S(2)}) collective-permute-start(bf16[2,2,128,256]{3,2,1,0:T(8,128)(2,1)S(1)} %get-tuple-element.33), channel_id=1, source_target_pairs={{0,7},{1,2},{2,1},{3,4},{4,3},{5,6},{6,5},{7,0},{8,9},{9,8},{10,11... | collective-permute-start | bytes 786440 | tf_op jit(solution)/shard_map/ppermute | solution.py:65
  130.9 9.1 %collective-permute-start.38 = (bf16[2,2,128,256]{3,2,1,0:T(8,128)(2,1)S(1)}, bf16[2,2,128,256]{3,2,1,0:T(8,128)(2,1)S(1)}, u32[]{:S(2)}, u32[]{:S(2)}) collective-permute-start(bf16[2,2,128,256]{3,2,1,0:T(8,128)(2,1)S(1)} %add_convert_fusion.3), channel_id=1, source_target_pairs={{0,1},{1,0},{2,3},{3,2},{4,5},{5,4},{6,7},{7,6},{8,15},{9,10},{10,... | collective-permute-start | bytes 786440 | tf_op jit(solution)/shard_map/ppermute | solution.py:65
  140.0 9.4 %collective-permute-start.39 = (bf16[2,2,128,256]{3,2,1,0:T(8,128)(2,1)S(1)}, bf16[2,2,128,256]{3,2,1,0:T(8,128)(2,1)S(1)}, u32[]{:S(2)}, u32[]{:S(2)}) collective-permute-start(bf16[2,2,128,256]{3,2,1,0:T(8,128)(2,1)S(1)} %add_convert_fusion.2), channel_id=1, source_target_pairs={{0,7},{1,2},{2,1},{3,4},{4,3},{5,6},{6,5},{7,0},{8,9},{9,8},{10,11... | collective-permute-start | bytes 786440 | tf_op jit(solution)/shard_map/ppermute | solution.py:65
  144.7 13.1 %collective-permute-start.44 = (bf16[8,128,256]{2,1,0:T(8,128)(2,1)S(1)}, bf16[8,128,256]{2,1,0:T(8,128)(2,1)S(1)}, u32[]{:S(2)}, u32[]{:S(2)}) collective-permute-start(bf16[8,128,256]{2,1,0:T(8,128)(2,1)S(1)} %get-tuple-element.47), channel_id=1, source_target_pairs={{0,32},{8,136},{16,48},{24,152},{32,0},{40,168},{48,16},{56,184},{... | collective-permute-start | bytes 1572872 | tf_op jit(solution)/shard_map/ppermute | solution.py:45
  145.8 17.6 %collective-permute-start.43 = (bf16[8,128,256]{2,1,0:T(8,128)(2,1)S(1)}, bf16[8,128,256]{2,1,0:T(8,128)(2,1)S(1)}, u32[]{:S(2)}, u32[]{:S(2)}) collective-permute-start(bf16[8,128,256]{2,1,0:T(8,128)(2,1)S(1)} %get-tuple-element.48), channel_id=1, source_target_pairs={{0,48},{8,200},{16,32},{24,216},{32,16},{40,232},{48,0},{56,248},{... | collective-permute-start | bytes 1572872 | tf_op jit(solution)/shard_map/ppermute | solution.py:45
  146.7 17.6 %collective-permute-start.42 = (bf16[8,128,256]{2,1,0:T(8,128)(2,1)S(1)}, bf16[8,128,256]{2,1,0:T(8,128)(2,1)S(1)}, u32[]{:S(2)}, u32[]{:S(2)}) collective-permute-start(bf16[8,128,256]{2,1,0:T(8,128)(2,1)S(1)} %get-tuple-element.46), channel_id=1, source_target_pairs={{0,16},{8,72},{16,0},{24,88},{32,48},{40,104},{48,32},{56,120},{64... | collective-permute-start | bytes 1572872 | tf_op jit(solution)/shard_map/ppermute | solution.py:45
  149.6 18.6 %collective-permute-start.40 = (bf16[2,128,256]{2,1,0:T(8,128)(2,1)S(1)}, bf16[2,128,256]{2,1,0:T(8,128)(2,1)S(1)}, u32[]{:S(2)}, u32[]{:S(2)}) collective-permute-start(bf16[2,128,256]{2,1,0:T(8,128)(2,1)S(1)} %fusion.5), channel_id=1, source_target_pairs={{0,1},{1,0},{2,3},{3,2},{4,5},{5,4},{6,7},{7,6},{8,15},{9,10},{10,... | collective-permute-start | bytes 393224 | tf_op jit(solution)/shard_map/ppermute | solution.py:65
  164.6 6.6 %collective-permute-start.47 = (bf16[2,128,256]{2,1,0:T(8,128)(2,1)S(1)}, bf16[2,128,256]{2,1,0:T(8,128)(2,1)S(1)}, u32[]{:S(2)}, u32[]{:S(2)}) collective-permute-start(bf16[2,128,256]{2,1,0:T(8,128)(2,1)S(1)} %get-tuple-element.50), channel_id=1, source_target_pairs={{0,128},{8,40},{16,144},{24,56},{32,160},{40,8},{48,176},{56,24},{... | collective-permute-start | bytes 393224 | tf_op jit(solution)/shard_map/ppermute | solution.py:51
  166.1 6.5 %collective-permute-start.46 = (bf16[2,128,256]{2,1,0:T(8,128)(2,1)S(1)}, bf16[2,128,256]{2,1,0:T(8,128)(2,1)S(1)}, u32[]{:S(2)}, u32[]{:S(2)}) collective-permute-start(bf16[2,128,256]{2,1,0:T(8,128)(2,1)S(1)} %get-tuple-element.51), channel_id=1, source_target_pairs={{0,192},{8,56},{16,208},{24,40},{32,224},{40,24},{48,240},{56,8},{... | collective-permute-start | bytes 393224 | tf_op jit(solution)/shard_map/ppermute | solution.py:51
  (31 other events, 335.6 us)

commit v3 on v2

--- a/solution.py
+++ b/solution.py
@@ -17,7 +17,6 @@
 BF16 = jnp.bfloat16
 SMEM = pl.BlockSpec(memory_space=pltpu.SMEM)
 VMEM = pl.BlockSpec(memory_space=pltpu.VMEM)
-ANY = pl.BlockSpec(memory_space=pl.ANY)
 LIMIT = 16 * 1024 * 1024
 
 
@@ -188,39 +187,33 @@
 def build_kernel(*refs):
     meta, refs = refs[:3], refs[3:]
     tgt = refs[:8]
-    unit_src, mass, kt, tiles, rows, acc, sems = refs[8:]
+    unit_src, mass, kt, tiles, rows, acc = refs[8:]
     n = live(meta)
     _, z, my_y, my_x, my_k = place()
 
-    def fetch(g, _):
-        _, targets, _ = group_of(meta, g)
+    def fetch(g, targets):
         for h, j in enumerate(targets):
             i, owner = j % 2, j // 2
             dy, dx = (owner // 8) ^ my_y, ((owner // 2) % 4) ^ my_x
             first, second = jnp.where(i == 0, dx, dy), jnp.where(i == 0, dy, dx)
-            array = second + jnp.where(i == my_k, 0, 4)
             at = first * 2 + owner % 2
-            for a in range(8):
-
-                @pl.when(array == a)
+            for near in (0, 1):
+
+                @pl.when((i == my_k) == (near == 0))
                 def _():
-                    pltpu.make_async_copy(
-                        tgt[a].at[at], tiles.at[g, pl.ds(h * 128, 128), :], sems.at[g, h]
-                    ).start()
-
-        return 0
-
-    lax.fori_loop(0, n, fetch, 0)
+                    for a in range(4):
+
+                        @pl.when(second == a)
+                        def _():
+                            tiles[g, h * 128 : (h + 1) * 128, :] = tgt[4 * near + a][at]
+
     acc[...] = jnp.zeros_like(acc)
     scale = math.log2(math.e) / (256 * TEMP)
     shift = OFFSET / TEMP * math.log2(math.e)
 
     def step(g, _):
-        p, _, both = group_of(meta, g)
-        for h in range(2):
-            pltpu.make_async_copy(
-                tgt[0].at[0], tiles.at[g, pl.ds(h * 128, 128), :], sems.at[g, h]
-            ).wait()
+        p, targets, both = group_of(meta, g)
+        fetch(g, targets)
         tile = unit(tiles[g])
         keep = jnp.where(both, 1.0, 0.0)
         for c in range(4):
@@ -392,8 +385,8 @@
     kt, tiles, rows = call(
         build_kernel,
         [S((GROUPS, 256, 1024), BF16), S((GROUPS, 256, 256), BF16), S((4, 1024), F32)],
-        [SMEM] * 3 + [ANY] * 8 + [VMEM] * 2,
-        [pltpu.VMEM((2, 8, 1024), F32), pltpu.SemaphoreType.DMA((GROUPS, 2))],
+        [SMEM] * 3 + [VMEM] * 10,
+        [pltpu.VMEM((2, 8, 1024), F32)],
         (*meta, *targets, unit_src, src_mass),
         800_000_000,
         7_000_000,

time: 177 us -> 176 us (level)
  no operation moved by 1% of the time
where the time goes in v3:
time: 176 us; the launch traced here: 174 us
  waiting for transfers between devices  90.6 us (51%)
  starting transfers between devices  66.8 us (38%)
  Pallas kernels  11.5 us (7%)
  other arithmetic  3.18 us (2%)
    ppermute x8, waiting for transfers between devices, along_z(): return lax.ppermute(v, ('blk', 'col'), pairs)  34.1 us
    ppermute x6, waiting for transfers between devices, over_first(): lax.ppermute(v, 'blk', blk_perm(lambda y, x, k: (y, x ^ d, k) if k == 0 e...  19.5 us
    ppermute x8, starting transfers between devices, along_z(): return lax.ppermute(v, ('blk', 'col'), pairs)  16.7 us
    ppermute x8, waiting for transfers between devices, over_z(): return lax.ppermute(v, 'col', [(i, i ^ d) for i in range(8)])  15.3 us
    ppermute x8, starting transfers between devices, over_z(): return lax.ppermute(v, 'col', [(i, i ^ d) for i in range(8)])  11.8 us
    pallas_call x7, Pallas kernels, call(): pl.pallas_call(kernel, out_shape=out_shape, in_specs=in_specs, out_specs=...  11.5 us
    ppermute x6, starting transfers between devices, over_x(): return lax.ppermute(v, 'blk', blk_perm(lambda y, x, k: (y, x ^ d, k)))  9.56 us
    ppermute x6, starting transfers between devices, over_y(): return lax.ppermute(v, 'blk', blk_perm(lambda y, x, k: (y ^ d, x, k)))  9.31 us
  transfers between devices with their start and end apart: 49, of which 34 were waited for; matrix products, arithmetic and copies ran while one was open for 2% of the time, Pallas kernels for 2%

profile of v3, /device:TPU:2, one launch (start us, length us, event | category | flops | bytes accessed | tf_op | source)
XLA Modules:
  0.0 174.2 jit_solution(16658717979220126623)
XLA Ops:
  4.0 2.8 %collective-permute-start.2 = (bf16[2,128,256]{2,1,0:T(8,128)(2,1)S(1)}, bf16[2,128,256]{2,1,0:T(8,128)(2,1)S(1)}, u32[]{:S(2)}, u32[]{:S(2)}) collective-permute-start(bf16[2,128,256]{2,1,0:T(8,128)(2,1)S(1)} %maximum_select_fusion.2), channel_id=1, source_target_pairs={{0,32},{8,136},{16,48},{24,152},{32,0},{40,168},{48,16},{56,184},{... | collective-permute-start | bytes 393224 | tf_op jit(solution)/shard_map/ppermute | solution.py:44
  7.4 3.0 %collective-permute-done.2 = bf16[2,128,256]{2,1,0:T(8,128)(2,1)S(1)} collective-permute-done((bf16[2,128,256]{2,1,0:T(8,128)(2,1)S(1)}, bf16[2,128,256]{2,1,0:T(8,128)(2,1)S(1)}, u32[]{:S(2)}, u32[]{:S(2)}) %collective-permute-start.2) | collective-permute-done | bytes 131104 | tf_op jit(solution)/shard_map/ppermute | solution.py:44
  12.6 2.9 %collective-permute-start.5 = (bf16[8,128,256]{2,1,0:T(8,128)(2,1)S(1)}, bf16[8,128,256]{2,1,0:T(8,128)(2,1)S(1)}, u32[]{:S(2)}, u32[]{:S(2)}) collective-permute-start(bf16[8,128,256]{2,1,0:T(8,128)(2,1)S(1)} %pad_maximum_fusion.refs_3_), channel_id=1, source_target_pairs={{0,128},{8,40},{16,144},{24,56},{32,160},{40,8},{48,176},{56,24},{... | collective-permute-start | bytes 1572872 | tf_op jit(solution)/shard_map/ppermute | solution.py:50
  17.7 4.1 %collective-permute-done.11 = bf16[2,128,256]{2,1,0:T(8,128)(2,1)S(1)} collective-permute-done((bf16[2,128,256]{2,1,0:T(8,128)(2,1)}, bf16[2,128,256]{2,1,0:T(8,128)(2,1)S(1)}, u32[]{:S(2)}, u32[]{:S(2)}) %collective-permute-start.11) | collective-permute-done | bytes 131104 | tf_op jit(solution)/shard_map/ppermute | solution.py:64
  21.8 5.1 %collective-permute-start.12 = (bf16[2,2,128,256]{3,2,1,0:T(8,128)(2,1)S(1)}, bf16[2,2,128,256]{3,2,1,0:T(8,128)(2,1)S(1)}, u32[]{:S(2)}, u32[]{:S(2)}) collective-permute-start(bf16[2,2,128,256]{3,2,1,0:T(8,128)(2,1)S(1)} %maximum_select_fusion.s0), channel_id=1, source_target_pairs={{0,7},{1,2},{2,1},{3,4},{4,3},{5,6},{6,5},{7,0},{8,9},{9,8},{10,11... | collective-permute-start | bytes 786440 | tf_op jit(solution)/shard_map/ppermute | solution.py:64
  26.9 4.4 %collective-permute-done.12.s1 = bf16[2,2,128,256]{3,2,1,0:T(8,128)(2,1)S(1)} collective-permute-done((bf16[2,2,128,256]{3,2,1,0:T(8,128)(2,1)S(1)}, bf16[2,2,128,256]{3,2,1,0:T(8,128)(2,1)S(1)}, u32[]{:S(2)}, u32[]{:S(2)}) %collective-permute-start.12) | collective-permute-done | bytes 262176 | tf_op jit(solution)/shard_map/ppermute | solution.py:64
  32.3 6.4 %collective-permute-done.13.s2 = bf16[2,2,128,256]{3,2,1,0:T(8,128)(2,1)S(1)} collective-permute-done((bf16[2,2,128,256]{3,2,1,0:T(8,128)(2,1)S(1)}, bf16[2,2,128,256]{3,2,1,0:T(8,128)(2,1)S(1)}, u32[]{:S(2)}, u32[]{:S(2)}) %collective-permute-start.13) | collective-permute-done | bytes 262176 | tf_op jit(solution)/shard_map/ppermute | solution.py:64
  38.7 3.5 %collective-permute-start.14 = (bf16[2,2,128,256]{3,2,1,0:T(8,128)(2,1)S(1)}, bf16[2,2,128,256]{3,2,1,0:T(8,128)(2,1)S(1)}, u32[]{:S(2)}, u32[]{:S(2)}) collective-permute-start(bf16[2,2,128,256]{3,2,1,0:T(8,128)(2,1)S(1)} %collective-permute-done.13.s2), channel_id=1, source_target_pairs={{0,7},{1,2},{2,1},{3,4},{4,3},{5,6},{6,5},{7,0},{8,9},{9,8},{10,11... | collective-permute-start | bytes 786440 | tf_op jit(solution)/shard_map/ppermute | solution.py:64
  42.2 4.3 %collective-permute-done.14.s3 = bf16[2,2,128,256]{3,2,1,0:T(8,128)(2,1)S(1)} collective-permute-done((bf16[2,2,128,256]{3,2,1,0:T(8,128)(2,1)S(1)}, bf16[2,2,128,256]{3,2,1,0:T(8,128)(2,1)S(1)}, u32[]{:S(2)}, u32[]{:S(2)}) %collective-permute-start.14) | collective-permute-done | bytes 262176 | tf_op jit(solution)/shard_map/ppermute | solution.py:64
  49.6 3.6 %collective-permute-done.15 = bf16[4,1024]{1,0:T(4,128)(2,1)S(1)} collective-permute-done((bf16[4,1024]{1,0:T(4,128)(2,1)S(1)}, bf16[4,1024]{1,0:T(4,128)(2,1)S(1)}, u32[]{:S(2)}, u32[]{:S(2)}) %collective-permute-start.15) | collective-permute-done | bytes 8224 | tf_op jit(solution)/shard_map/ppermute | solution.py:56
  53.2 3.2 %collective-permute-start.16 = (bf16[4,1024]{1,0:T(4,128)(2,1)S(1)}, bf16[4,1024]{1,0:T(4,128)(2,1)S(1)}, u32[]{:S(2)}, u32[]{:S(2)}) collective-permute-start(bf16[4,1024]{1,0:T(4,128)(2,1)S(1)} %get-tuple-element.44), channel_id=1, source_target_pairs={{0,5},{1,4},{2,7},{3,6},{4,1},{5,0},{6,3},{7,2},{8,13},{9,12},{10,... | collective-permute-start | bytes 24584 | tf_op jit(solution)/shard_map/ppermute | solution.py:56
  61.0 3.7 %collective-permute-done.18.refs_7_ = bf16[4,1024]{1,0:T(4,128)(2,1)S(1)} collective-permute-done((bf16[4,1024]{1,0:T(4,128)(2,1)S(1)}, bf16[4,1024]{1,0:T(4,128)(2,1)S(1)}, u32[]{:S(2)}, u32[]{:S(2)}) %collective-permute-start.18) | collective-permute-done | bytes 8224 | tf_op jit(solution)/shard_map/ppermute | solution.py:56
  69.3 3.1 %collective-permute-start.20 = (bf16[128,128]{1,0:T(8,128)(2,1)S(1)}, bf16[128,128]{1,0:T(8,128)(2,1)S(1)}, u32[]{:S(2)}, u32[]{:S(2)}) collective-permute-start(bf16[128,128]{1,0:T(8,128)(2,1)S(1)} %fusion.7), channel_id=1, source_target_pairs={{0,16},{8,24},{16,0},{24,8},{32,48},{40,56},{48,32},{56,40},{64,80... | collective-permute-start | bytes 98312 | tf_op jit(solution)/shard_map/ppermute | solution.py:36
  74.7 3.4 %collective-permute-start.24 = (bf16[128,128]{1,0:T(8,128)(2,1)S(1)}, bf16[128,128]{1,0:T(8,128)(2,1)S(1)}, u32[]{:S(2)}, u32[]{:S(2)}) collective-permute-start(bf16[128,128]{1,0:T(8,128)(2,1)S(1)} %get-tuple-element.42), channel_id=1, source_target_pairs={{0,192},{8,200},{16,208},{24,216},{32,224},{40,232},{48,240},{56,2... | collective-permute-start | bytes 98312 | tf_op jit(solution)/shard_map/ppermute | solution.py:40
  80.0 3.5 %collective-permute-done.25.refs_7_ = bf16[128,128]{1,0:T(8,128)(2,1)S(1)} collective-permute-done((bf16[128,128]{1,0:T(8,128)(2,1)S(1)}, bf16[128,128]{1,0:T(8,128)(2,1)S(1)}, u32[]{:S(2)}, u32[]{:S(2)}) %collective-permute-start.25) | collective-permute-done | bytes 32800 | tf_op jit(solution)/shard_map/ppermute | solution.py:40
  85.2 3.2 %collective-permute-done.26 = bf16[2,1024]{1,0:T(2,128)(2,1)S(1)} collective-permute-done((bf16[2,1024]{1,0:T(2,128)(2,1)S(1)}, bf16[2,1024]{1,0:T(2,128)(2,1)S(1)}, u32[]{:S(2)}, u32[]{:S(2)}) %collective-permute-start.26) | collective-permute-done | bytes 4128 | tf_op jit(solution)/shard_map/ppermute | solution.py:56
  91.0 3.0 %collective-permute-start.29 = (bf16[2,1024]{1,0:T(2,128)(2,1)S(1)}, bf16[2,1024]{1,0:T(2,128)(2,1)S(1)}, u32[]{:S(2)}, u32[]{:S(2)}) collective-permute-start(bf16[2,1024]{1,0:T(2,128)(2,1)S(1)} %get-tuple-element.40), channel_id=1, source_target_pairs={{0,6},{1,7},{2,4},{3,5},{4,2},{5,3},{6,0},{7,1},{8,14},{9,15},{10,... | collective-permute-start | bytes 12296 | tf_op jit(solution)/shard_map/ppermute | solution.py:56
  100.9 3.7 %collective-permute-done.30 = bf16[64,128]{1,0:T(8,128)(2,1)S(1)} collective-permute-done((bf16[64,128]{1,0:T(8,128)(2,1)S(1)}, bf16[64,128]{1,0:T(8,128)(2,1)S(1)}, u32[]{:S(2)}, u32[]{:S(2)}) %collective-permute-start.30) | collective-permute-done | bytes 16416 | tf_op jit(solution)/shard_map/ppermute | solution.py:32
  121.2 3.3 %collective-permute-start.37 = (bf16[2,2,128,256]{3,2,1,0:T(8,128)(2,1)S(1)}, bf16[2,2,128,256]{3,2,1,0:T(8,128)(2,1)S(1)}, u32[]{:S(2)}, u32[]{:S(2)}) collective-permute-start(bf16[2,2,128,256]{3,2,1,0:T(8,128)(2,1)S(1)} %get-tuple-element.33), channel_id=1, source_target_pairs={{0,7},{1,2},{2,1},{3,4},{4,3},{5,6},{6,5},{7,0},{8,9},{9,8},{10,11... | collective-permute-start | bytes 786440 | tf_op jit(solution)/shard_map/ppermute | solution.py:64
  124.5 5.9 %collective-permute-done.37 = bf16[2,2,128,256]{3,2,1,0:T(8,128)(2,1)S(1)} collective-permute-done((bf16[2,2,128,256]{3,2,1,0:T(8,128)(2,1)S(1)}, bf16[2,2,128,256]{3,2,1,0:T(8,128)(2,1)S(1)}, u32[]{:S(2)}, u32[]{:S(2)}) %collective-permute-start.37) | collective-permute-done | bytes 262176 | tf_op jit(solution)/shard_map/ppermute | solution.py:64
  130.5 9.0 %collective-permute-done.38 = bf16[2,2,128,256]{3,2,1,0:T(8,128)(2,1)S(1)} collective-permute-done((bf16[2,2,128,256]{3,2,1,0:T(8,128)(2,1)S(1)}, bf16[2,2,128,256]{3,2,1,0:T(8,128)(2,1)S(1)}, u32[]{:S(2)}, u32[]{:S(2)}) %collective-permute-start.38) | collective-permute-done | bytes 262176 | tf_op jit(solution)/shard_map/ppermute | solution.py:64
  139.5 3.7 %collective-permute-start.39 = (bf16[2,2,128,256]{3,2,1,0:T(8,128)(2,1)S(1)}, bf16[2,2,128,256]{3,2,1,0:T(8,128)(2,1)S(1)}, u32[]{:S(2)}, u32[]{:S(2)}) collective-permute-start(bf16[2,2,128,256]{3,2,1,0:T(8,128)(2,1)S(1)} %add_convert_fusion.2), channel_id=1, source_target_pairs={{0,7},{1,2},{2,1},{3,4},{4,3},{5,6},{6,5},{7,0},{8,9},{9,8},{10,11... | collective-permute-start | bytes 786440 | tf_op jit(solution)/shard_map/ppermute | solution.py:64
  149.1 8.1 %collective-permute-done.44 = bf16[8,128,256]{2,1,0:T(8,128)(2,1)S(1)} collective-permute-done((bf16[8,128,256]{2,1,0:T(8,128)(2,1)S(1)}, bf16[8,128,256]{2,1,0:T(8,128)(2,1)S(1)}, u32[]{:S(2)}, u32[]{:S(2)}) %collective-permute-start.44) | collective-permute-done | bytes 524320 | tf_op jit(solution)/shard_map/ppermute | solution.py:44
  157.2 5.7 %collective-permute-done.43 = bf16[8,128,256]{2,1,0:T(8,128)(2,1)S(1)} collective-permute-done((bf16[8,128,256]{2,1,0:T(8,128)(2,1)S(1)}, bf16[8,128,256]{2,1,0:T(8,128)(2,1)S(1)}, u32[]{:S(2)}, u32[]{:S(2)}) %collective-permute-start.43) | collective-permute-done | bytes 524320 | tf_op jit(solution)/shard_map/ppermute | solution.py:44
  (124 shorter events, 70.7 us)
Async XLA Ops:
  4.0 6.5 %collective-permute-start.2 = (bf16[2,128,256]{2,1,0:T(8,128)(2,1)S(1)}, bf16[2,128,256]{2,1,0:T(8,128)(2,1)S(1)}, u32[]{:S(2)}, u32[]{:S(2)}) collective-permute-start(bf16[2,128,256]{2,1,0:T(8,128)(2,1)S(1)} %maximum_select_fusion.2), channel_id=1, source_target_pairs={{0,32},{8,136},{16,48},{24,152},{32,0},{40,168},{48,16},{56,184},{... | collective-permute-start | bytes 393224 | tf_op jit(solution)/shard_map/ppermute | solution.py:44
  11.8 19.5 %collective-permute-start.4 = (bf16[8,128,256]{2,1,0:T(8,128)(2,1)S(1)}, bf16[8,128,256]{2,1,0:T(8,128)(2,1)S(1)}, u32[]{:S(2)}, u32[]{:S(2)}) collective-permute-start(bf16[8,128,256]{2,1,0:T(8,128)(2,1)S(1)} %pad_maximum_fusion.refs_3_), channel_id=1, source_target_pairs={{0,64},{8,24},{16,80},{24,8},{32,96},{40,56},{48,112},{56,40},{64,... | collective-permute-start | bytes 1572872 | tf_op jit(solution)/shard_map/ppermute | solution.py:50
  12.6 19.2 %collective-permute-start.5 = (bf16[8,128,256]{2,1,0:T(8,128)(2,1)S(1)}, bf16[8,128,256]{2,1,0:T(8,128)(2,1)S(1)}, u32[]{:S(2)}, u32[]{:S(2)}) collective-permute-start(bf16[8,128,256]{2,1,0:T(8,128)(2,1)S(1)} %pad_maximum_fusion.refs_3_), channel_id=1, source_target_pairs={{0,128},{8,40},{16,144},{24,56},{32,160},{40,8},{48,176},{56,24},{... | collective-permute-start | bytes 1572872 | tf_op jit(solution)/shard_map/ppermute | solution.py:50
  15.5 16.4 %collective-permute-start.6 = (bf16[8,128,256]{2,1,0:T(8,128)(2,1)S(1)}, bf16[8,128,256]{2,1,0:T(8,128)(2,1)S(1)}, u32[]{:S(2)}, u32[]{:S(2)}) collective-permute-start(bf16[8,128,256]{2,1,0:T(8,128)(2,1)S(1)} %pad_maximum_fusion.refs_3_), channel_id=1, source_target_pairs={{0,192},{8,56},{16,208},{24,40},{32,224},{40,24},{48,240},{56,8},{... | collective-permute-start | bytes 1572872 | tf_op jit(solution)/shard_map/ppermute | solution.py:50
  21.8 9.5 %collective-permute-start.12 = (bf16[2,2,128,256]{3,2,1,0:T(8,128)(2,1)S(1)}, bf16[2,2,128,256]{3,2,1,0:T(8,128)(2,1)S(1)}, u32[]{:S(2)}, u32[]{:S(2)}) collective-permute-start(bf16[2,2,128,256]{3,2,1,0:T(8,128)(2,1)S(1)} %maximum_select_fusion.s0), channel_id=1, source_target_pairs={{0,7},{1,2},{2,1},{3,4},{4,3},{5,6},{6,5},{7,0},{8,9},{9,8},{10,11... | collective-permute-start | bytes 786440 | tf_op jit(solution)/shard_map/ppermute | solution.py:64
  31.3 7.4 %collective-permute-start.13 = (bf16[2,2,128,256]{3,2,1,0:T(8,128)(2,1)S(1)}, bf16[2,2,128,256]{3,2,1,0:T(8,128)(2,1)S(1)}, u32[]{:S(2)}, u32[]{:S(2)}) collective-permute-start(bf16[2,2,128,256]{3,2,1,0:T(8,128)(2,1)S(1)} %collective-permute-done.12.s1), channel_id=1, source_target_pairs={{0,1},{1,0},{2,3},{3,2},{4,5},{5,4},{6,7},{7,6},{8,15},{9,10},{10,... | collective-permute-start | bytes 786440 | tf_op jit(solution)/shard_map/ppermute | solution.py:64
  31.3 15.7 %collective-permute-start.7 = (bf16[8,128,256]{2,1,0:T(8,128)(2,1)S(1)}, bf16[8,128,256]{2,1,0:T(8,128)(2,1)S(1)}, u32[]{:S(2)}, u32[]{:S(2)}) collective-permute-start(bf16[8,128,256]{2,1,0:T(8,128)(2,1)S(1)} %pad_maximum_fusion.refs_3_), channel_id=1, source_target_pairs={{0,8},{8,0},{16,24},{24,16},{32,40},{40,32},{48,56},{56,48},{64,72... | collective-permute-start | bytes 1572872 | tf_op jit(solution)/shard_map/ppermute | solution.py:32
  31.3 15.7 %collective-permute-start.8 = (bf16[8,128,256]{2,1,0:T(8,128)(2,1)S(1)}, bf16[8,128,256]{2,1,0:T(8,128)(2,1)S(1)}, u32[]{:S(2)}, u32[]{:S(2)}) collective-permute-start(bf16[8,128,256]{2,1,0:T(8,128)(2,1)S(1)} %collective-permute-done.4.refs_4_), channel_id=1, source_target_pairs={{0,8},{8,0},{16,24},{24,16},{32,40},{40,32},{48,56},{56,48},{64,72... | collective-permute-start | bytes 1572872 | tf_op jit(solution)/shard_map/ppermute | solution.py:32
  31.8 15.2 %collective-permute-start.9 = (bf16[8,128,256]{2,1,0:T(8,128)(2,1)S(1)}, bf16[8,128,256]{2,1,0:T(8,128)(2,1)S(1)}, u32[]{:S(2)}, u32[]{:S(2)}) collective-permute-start(bf16[8,128,256]{2,1,0:T(8,128)(2,1)S(1)} %collective-permute-done.5.refs_5_), channel_id=1, source_target_pairs={{0,8},{8,0},{16,24},{24,16},{32,40},{40,32},{48,56},{56,48},{64,72... | collective-permute-start | bytes 1572872 | tf_op jit(solution)/shard_map/ppermute | solution.py:32
  31.9 15.1 %collective-permute-start.10 = (bf16[8,128,256]{2,1,0:T(8,128)(2,1)S(1)}, bf16[8,128,256]{2,1,0:T(8,128)(2,1)S(1)}, u32[]{:S(2)}, u32[]{:S(2)}) collective-permute-start(bf16[8,128,256]{2,1,0:T(8,128)(2,1)S(1)} %collective-permute-done.6.refs_6_), channel_id=1, source_target_pairs={{0,8},{8,0},{16,24},{24,16},{32,40},{40,32},{48,56},{56,48},{64,72... | collective-permute-start | bytes 1572872 | tf_op jit(solution)/shard_map/ppermute | solution.py:32
  38.7 7.8 %collective-permute-start.14 = (bf16[2,2,128,256]{3,2,1,0:T(8,128)(2,1)S(1)}, bf16[2,2,128,256]{3,2,1,0:T(8,128)(2,1)S(1)}, u32[]{:S(2)}, u32[]{:S(2)}) collective-permute-start(bf16[2,2,128,256]{3,2,1,0:T(8,128)(2,1)S(1)} %collective-permute-done.13.s2), channel_id=1, source_target_pairs={{0,7},{1,2},{2,1},{3,4},{4,3},{5,6},{6,5},{7,0},{8,9},{9,8},{10,11... | collective-permute-start | bytes 786440 | tf_op jit(solution)/shard_map/ppermute | solution.py:64
  53.2 6.7 %collective-permute-start.16 = (bf16[4,1024]{1,0:T(4,128)(2,1)S(1)}, bf16[4,1024]{1,0:T(4,128)(2,1)S(1)}, u32[]{:S(2)}, u32[]{:S(2)}) collective-permute-start(bf16[4,1024]{1,0:T(4,128)(2,1)S(1)} %get-tuple-element.44), channel_id=1, source_target_pairs={{0,5},{1,4},{2,7},{3,6},{4,1},{5,0},{6,3},{7,2},{8,13},{9,12},{10,... | collective-permute-start | bytes 24584 | tf_op jit(solution)/shard_map/ppermute | solution.py:56
  88.4 6.7 %collective-permute-start.27 = (bf16[2,1024]{1,0:T(2,128)(2,1)S(1)}, bf16[2,1024]{1,0:T(2,128)(2,1)S(1)}, u32[]{:S(2)}, u32[]{:S(2)}) collective-permute-start(bf16[2,1024]{1,0:T(2,128)(2,1)S(1)} %get-tuple-element.40), channel_id=1, source_target_pairs={{0,5},{1,4},{2,7},{3,6},{4,1},{5,0},{6,3},{7,2},{8,13},{9,12},{10,... | collective-permute-start | bytes 12296 | tf_op jit(solution)/shard_map/ppermute | solution.py:56
  88.9 6.2 %collective-permute-start.28 = (bf16[2,1024]{1,0:T(2,128)(2,1)S(1)}, bf16[2,1024]{1,0:T(2,128)(2,1)S(1)}, u32[]{:S(2)}, u32[]{:S(2)}) collective-permute-start(bf16[2,1024]{1,0:T(2,128)(2,1)S(1)} %get-tuple-element.40), channel_id=1, source_target_pairs={{0,2},{1,3},{2,0},{3,1},{4,6},{5,7},{6,4},{7,5},{8,10},{9,11},{10,... | collective-permute-start | bytes 12296 | tf_op jit(solution)/shard_map/ppermute | solution.py:56
  100.3 42.9 %collective-permute-start.41 = (bf16[32,128,256]{2,1,0:T(8,128)(2,1)S(1)}, bf16[32,128,256]{2,1,0:T(8,128)(2,1)S(1)}, u32[]{:S(2)}, u32[]{:S(2)}) collective-permute-start(bf16[32,128,256]{2,1,0:T(8,128)(2,1)S(1)} %get-tuple-element.36), channel_id=1, source_target_pairs={{0,8},{8,0},{16,24},{24,16},{32,40},{40,32},{48,56},{56,48},{64,72... | collective-permute-start | bytes 6291464 | tf_op jit(solution)/shard_map/ppermute | solution.py:32
  121.2 9.1 %collective-permute-start.37 = (bf16[2,2,128,256]{3,2,1,0:T(8,128)(2,1)S(1)}, bf16[2,2,128,256]{3,2,1,0:T(8,128)(2,1)S(1)}, u32[]{:S(2)}, u32[]{:S(2)}) collective-permute-start(bf16[2,2,128,256]{3,2,1,0:T(8,128)(2,1)S(1)} %get-tuple-element.33), channel_id=1, source_target_pairs={{0,7},{1,2},{2,1},{3,4},{4,3},{5,6},{6,5},{7,0},{8,9},{9,8},{10,11... | collective-permute-start | bytes 786440 | tf_op jit(solution)/shard_map/ppermute | solution.py:64
  130.4 9.1 %collective-permute-start.38 = (bf16[2,2,128,256]{3,2,1,0:T(8,128)(2,1)S(1)}, bf16[2,2,128,256]{3,2,1,0:T(8,128)(2,1)S(1)}, u32[]{:S(2)}, u32[]{:S(2)}) collective-permute-start(bf16[2,2,128,256]{3,2,1,0:T(8,128)(2,1)S(1)} %add_convert_fusion.3), channel_id=1, source_target_pairs={{0,1},{1,0},{2,3},{3,2},{4,5},{5,4},{6,7},{7,6},{8,15},{9,10},{10,... | collective-permute-start | bytes 786440 | tf_op jit(solution)/shard_map/ppermute | solution.py:64
  139.5 9.4 %collective-permute-start.39 = (bf16[2,2,128,256]{3,2,1,0:T(8,128)(2,1)S(1)}, bf16[2,2,128,256]{3,2,1,0:T(8,128)(2,1)S(1)}, u32[]{:S(2)}, u32[]{:S(2)}) collective-permute-start(bf16[2,2,128,256]{3,2,1,0:T(8,128)(2,1)S(1)} %add_convert_fusion.2), channel_id=1, source_target_pairs={{0,7},{1,2},{2,1},{3,4},{4,3},{5,6},{6,5},{7,0},{8,9},{9,8},{10,11... | collective-permute-start | bytes 786440 | tf_op jit(solution)/shard_map/ppermute | solution.py:64
  144.1 13.1 %collective-permute-start.44 = (bf16[8,128,256]{2,1,0:T(8,128)(2,1)S(1)}, bf16[8,128,256]{2,1,0:T(8,128)(2,1)S(1)}, u32[]{:S(2)}, u32[]{:S(2)}) collective-permute-start(bf16[8,128,256]{2,1,0:T(8,128)(2,1)S(1)} %get-tuple-element.47), channel_id=1, source_target_pairs={{0,32},{8,136},{16,48},{24,152},{32,0},{40,168},{48,16},{56,184},{... | collective-permute-start | bytes 1572872 | tf_op jit(solution)/shard_map/ppermute | solution.py:44
  145.3 17.6 %collective-permute-start.43 = (bf16[8,128,256]{2,1,0:T(8,128)(2,1)S(1)}, bf16[8,128,256]{2,1,0:T(8,128)(2,1)S(1)}, u32[]{:S(2)}, u32[]{:S(2)}) collective-permute-start(bf16[8,128,256]{2,1,0:T(8,128)(2,1)S(1)} %get-tuple-element.48), channel_id=1, source_target_pairs={{0,48},{8,200},{16,32},{24,216},{32,16},{40,232},{48,0},{56,248},{... | collective-permute-start | bytes 1572872 | tf_op jit(solution)/shard_map/ppermute | solution.py:44
  146.1 17.6 %collective-permute-start.42 = (bf16[8,128,256]{2,1,0:T(8,128)(2,1)S(1)}, bf16[8,128,256]{2,1,0:T(8,128)(2,1)S(1)}, u32[]{:S(2)}, u32[]{:S(2)}) collective-permute-start(bf16[8,128,256]{2,1,0:T(8,128)(2,1)S(1)} %get-tuple-element.46), channel_id=1, source_target_pairs={{0,16},{8,72},{16,0},{24,88},{32,48},{40,104},{48,32},{56,120},{64... | collective-permute-start | bytes 1572872 | tf_op jit(solution)/shard_map/ppermute | solution.py:44
  149.0 18.6 %collective-permute-start.40 = (bf16[2,128,256]{2,1,0:T(8,128)(2,1)S(1)}, bf16[2,128,256]{2,1,0:T(8,128)(2,1)S(1)}, u32[]{:S(2)}, u32[]{:S(2)}) collective-permute-start(bf16[2,128,256]{2,1,0:T(8,128)(2,1)S(1)} %fusion.5), channel_id=1, source_target_pairs={{0,1},{1,0},{2,3},{3,2},{4,5},{5,4},{6,7},{7,6},{8,15},{9,10},{10,... | collective-permute-start | bytes 393224 | tf_op jit(solution)/shard_map/ppermute | solution.py:64
  164.0 6.6 %collective-permute-start.47 = (bf16[2,128,256]{2,1,0:T(8,128)(2,1)S(1)}, bf16[2,128,256]{2,1,0:T(8,128)(2,1)S(1)}, u32[]{:S(2)}, u32[]{:S(2)}) collective-permute-start(bf16[2,128,256]{2,1,0:T(8,128)(2,1)S(1)} %get-tuple-element.50), channel_id=1, source_target_pairs={{0,128},{8,40},{16,144},{24,56},{32,160},{40,8},{48,176},{56,24},{... | collective-permute-start | bytes 393224 | tf_op jit(solution)/shard_map/ppermute | solution.py:50
  165.5 6.5 %collective-permute-start.46 = (bf16[2,128,256]{2,1,0:T(8,128)(2,1)S(1)}, bf16[2,128,256]{2,1,0:T(8,128)(2,1)S(1)}, u32[]{:S(2)}, u32[]{:S(2)}) collective-permute-start(bf16[2,128,256]{2,1,0:T(8,128)(2,1)S(1)} %get-tuple-element.51), channel_id=1, source_target_pairs={{0,192},{8,56},{16,208},{24,40},{32,224},{40,24},{48,240},{56,8},{... | collective-permute-start | bytes 393224 | tf_op jit(solution)/shard_map/ppermute | solution.py:50
  (31 other events, 335.1 us)

commit v4 on v3

--- a/solution.py
+++ b/solution.py
@@ -326,38 +326,37 @@
     lax.fori_loop(0, live(meta), step, 0)
 
 
-def toward_kernel(*refs):
+def toward_kernel(which, *refs):
     meta, refs = refs[:3], refs[3:]
-    kt, u, tiles, c0, c1, c2, c3, mass, out1, out2, out3, out4, v_out, v_all, acc = refs
+    kt, u, tiles, c0, c1, c2, c3, mass = refs[:8]
+    outs = refs[8 : 8 + len(which)]
+    v_out, v_all, acc = refs[8 + len(which) :]
     total = c0[...] + c1[...].astype(F32) + c2[...].astype(F32) + c3[...].astype(F32)
     v_all[...] = mass[...] / total
     b, z = place()[:2]
     v_out[0:1, :] = v_all[pl.ds(2 * b, 1), :]
     v_out[1:2, :] = v_all[pl.ds(2 * b + 1, 1), :]
+    places = chunk_places(b, z)
     acc[...] = jnp.zeros_like(acc)
 
     def step(g, _):
         p, targets, _ = group_of(meta, g)
         v = [jnp.broadcast_to(v_all[pl.ds(j, 1), :], (128, 128)).T for j in targets]
         v = jnp.concatenate(v, axis=0)
-        row = jnp.where(p == 0, u[0:1, :], u[1:2, :])
         tile = tiles[g].T
-        for c in range(4):
+        for n, pair in enumerate(which):
             plan = []
-            for d in range(2):
-                cols = slice(c * 256 + d * 128, c * 256 + (d + 1) * 128)
-                plan.append((kt[g, :, cols].astype(F32) * row[:, cols] * v).astype(BF16))
-            cols = slice(c * 256, (c + 1) * 256)
-            acc[p, :, cols] += jnp.dot(
-                tile, jnp.concatenate(plan, axis=1), preferred_element_type=F32
-            )
+            for at in places[pair]:
+                row = jnp.where(p == 0, u[0:1, pl.ds(at, 128)], u[1:2, pl.ds(at, 128)])
+                plan.append((kt[g, :, pl.ds(at, 128)].astype(F32) * row * v).astype(BF16))
+            acc[p, n] += jnp.dot(tile, jnp.concatenate(plan, axis=1), preferred_element_type=F32)
         return 0
 
     lax.fori_loop(0, live(meta), step, 0)
-    for ref, places in zip((out1, out2, out3, out4), chunk_places(b, z)):
-        for h, at in enumerate(places):
+    for n, ref in enumerate(outs):
+        for h in range(2):
             for p in range(2):
-                ref[h, p] = acc[p, :, pl.ds(at, 128)].astype(BF16).T
+                ref[h, p] = acc[p, n, :, h * 128 : (h + 1) * 128].astype(BF16).T
 
 
 def call(kernel, out_shape, in_specs, scratch, args, flops, nbytes):
@@ -430,16 +429,19 @@
     came = swap(other)
     parts = blk_sum_parts(sums)
     tgt_own = reduce_targets(mine, came, core)
-    *parts, v = call(
-        toward_kernel,
-        [S((2, 2, 128, 256), BF16)] * 4 + [S((2, 128), F32)],
-        [SMEM] * 3 + [VMEM] * 8,
-        [pltpu.VMEM((64, 128), F32), pltpu.VMEM((2, 256, 1024), F32)],
-        (*meta, kt, u, tiles, *parts, mass_tgt),
-        800_000_000,
-        6_000_000,
-    )
-    src_own = reduce_sources(parts, even)
+    rows = []
+    for which in ((3,), (0, 1, 2)):
+        *found, v = call(
+            functools.partial(toward_kernel, which),
+            [S((2, 2, 128, 256), BF16)] * len(which) + [S((2, 128), F32)],
+            [SMEM] * 3 + [VMEM] * 8,
+            [pltpu.VMEM((64, 128), F32), pltpu.VMEM((2, len(which), 256, 256), F32)],
+            (*meta, kt, u, tiles, *parts, mass_tgt),
+            200_000_000 * len(which),
+            4_000_000,
+        )
+        rows = found + rows
+    src_own = reduce_sources(rows, even)
     src_aligned = (src_own / src_mass.astype(F32)[:, :, None]).astype(BF16)
     tgt_aligned = (tgt_own * v[:, :, None] / tgt_mass.astype(F32)[:, :, None]).astype(BF16)
     return (src_aligned, tgt_aligned)

time: 176 us -> 176 us (level)
  waiting for transfers between devices: 90.6 us -> 88.5 us
  Pallas kernels: 11.5 us -> 13.4 us
    ppermute x8, waiting for transfers between devices: 34.1 us -> 31.9 us  [along_z(): return lax.ppermute(v, ('blk', 'col'), pairs)]
    pallas_call x7 -> x8, Pallas kernels: 11.5 us -> 13.4 us  [call(): pl.pallas_call(kernel, out_shape=out_shape, in_specs=in_specs, out_specs=...]
  transfers between devices with their start and end apart: 49 -> 49, of which waited for: 34 -> 34; matrix products, arithmetic and copies ran while one was open for 2% -> 2% of each run, Pallas kernels for 2% -> 3%
where the time goes in v4:
time: 176 us; the launch traced here: 174 us
  waiting for transfers between devices  88.5 us (50%)
  starting transfers between devices  66.7 us (38%)
  Pallas kernels  13.4 us (8%)
  other arithmetic  3.17 us (2%)
    ppermute x8, waiting for transfers between devices, along_z(): return lax.ppermute(v, ('blk', 'col'), pairs)  31.9 us
    ppermute x6, waiting for transfers between devices, over_first(): lax.ppermute(v, 'blk', blk_perm(lambda y, x, k: (y, x ^ d, k) if k == 0 e...  19.5 us
    ppermute x8, starting transfers between devices, along_z(): return lax.ppermute(v, ('blk', 'col'), pairs)  16.6 us
    ppermute x8, waiting for transfers between devices, over_z(): return lax.ppermute(v, 'col', [(i, i ^ d) for i in range(8)])  15.4 us
    pallas_call x8, Pallas kernels, call(): pl.pallas_call(kernel, out_shape=out_shape, in_specs=in_specs, out_specs=...  13.4 us
    ppermute x8, starting transfers between devices, over_z(): return lax.ppermute(v, 'col', [(i, i ^ d) for i in range(8)])  11.8 us
    ppermute x6, starting transfers between devices, over_x(): return lax.ppermute(v, 'blk', blk_perm(lambda y, x, k: (y, x ^ d, k)))  9.56 us
    ppermute x6, starting transfers between devices, over_y(): return lax.ppermute(v, 'blk', blk_perm(lambda y, x, k: (y ^ d, x, k)))  9.31 us
  transfers between devices with their start and end apart: 49, of which 34 were waited for; matrix products, arithmetic and copies ran while one was open for 2% of the time, Pallas kernels for 3%

profile of v4, /device:TPU:2, one launch (start us, length us, event | category | flops | bytes accessed | tf_op | source)
XLA Modules:
  0.0 173.9 jit_solution(3283376404989016484)
XLA Ops:
  4.0 2.8 %collective-permute-start.2 = (bf16[2,128,256]{2,1,0:T(8,128)(2,1)S(1)}, bf16[2,128,256]{2,1,0:T(8,128)(2,1)S(1)}, u32[]{:S(2)}, u32[]{:S(2)}) collective-permute-start(bf16[2,128,256]{2,1,0:T(8,128)(2,1)S(1)} %maximum_select_fusion.2), channel_id=1, source_target_pairs={{0,32},{8,136},{16,48},{24,152},{32,0},{40,168},{48,16},{56,184},{... | collective-permute-start | bytes 393224 | tf_op jit(solution)/shard_map/ppermute | solution.py:44
  7.4 3.0 %collective-permute-done.2 = bf16[2,128,256]{2,1,0:T(8,128)(2,1)S(1)} collective-permute-done((bf16[2,128,256]{2,1,0:T(8,128)(2,1)S(1)}, bf16[2,128,256]{2,1,0:T(8,128)(2,1)S(1)}, u32[]{:S(2)}, u32[]{:S(2)}) %collective-permute-start.2) | collective-permute-done | bytes 131104 | tf_op jit(solution)/shard_map/ppermute | solution.py:44
  12.6 2.9 %collective-permute-start.5 = (bf16[8,128,256]{2,1,0:T(8,128)(2,1)S(1)}, bf16[8,128,256]{2,1,0:T(8,128)(2,1)S(1)}, u32[]{:S(2)}, u32[]{:S(2)}) collective-permute-start(bf16[8,128,256]{2,1,0:T(8,128)(2,1)S(1)} %pad_maximum_fusion.refs_3_), channel_id=1, source_target_pairs={{0,128},{8,40},{16,144},{24,56},{32,160},{40,8},{48,176},{56,24},{... | collective-permute-start | bytes 1572872 | tf_op jit(solution)/shard_map/ppermute | solution.py:50
  17.7 4.1 %collective-permute-done.11 = bf16[2,128,256]{2,1,0:T(8,128)(2,1)S(1)} collective-permute-done((bf16[2,128,256]{2,1,0:T(8,128)(2,1)}, bf16[2,128,256]{2,1,0:T(8,128)(2,1)S(1)}, u32[]{:S(2)}, u32[]{:S(2)}) %collective-permute-start.11) | collective-permute-done | bytes 131104 | tf_op jit(solution)/shard_map/ppermute | solution.py:64
  21.8 5.1 %collective-permute-start.12 = (bf16[2,2,128,256]{3,2,1,0:T(8,128)(2,1)S(1)}, bf16[2,2,128,256]{3,2,1,0:T(8,128)(2,1)S(1)}, u32[]{:S(2)}, u32[]{:S(2)}) collective-permute-start(bf16[2,2,128,256]{3,2,1,0:T(8,128)(2,1)S(1)} %maximum_select_fusion.s0), channel_id=1, source_target_pairs={{0,7},{1,2},{2,1},{3,4},{4,3},{5,6},{6,5},{7,0},{8,9},{9,8},{10,11... | collective-permute-start | bytes 786440 | tf_op jit(solution)/shard_map/ppermute | solution.py:64
  26.9 4.4 %collective-permute-done.12.s1 = bf16[2,2,128,256]{3,2,1,0:T(8,128)(2,1)S(1)} collective-permute-done((bf16[2,2,128,256]{3,2,1,0:T(8,128)(2,1)S(1)}, bf16[2,2,128,256]{3,2,1,0:T(8,128)(2,1)S(1)}, u32[]{:S(2)}, u32[]{:S(2)}) %collective-permute-start.12) | collective-permute-done | bytes 262176 | tf_op jit(solution)/shard_map/ppermute | solution.py:64
  32.3 6.4 %collective-permute-done.13.s2 = bf16[2,2,128,256]{3,2,1,0:T(8,128)(2,1)S(1)} collective-permute-done((bf16[2,2,128,256]{3,2,1,0:T(8,128)(2,1)S(1)}, bf16[2,2,128,256]{3,2,1,0:T(8,128)(2,1)S(1)}, u32[]{:S(2)}, u32[]{:S(2)}) %collective-permute-start.13) | collective-permute-done | bytes 262176 | tf_op jit(solution)/shard_map/ppermute | solution.py:64
  38.7 3.5 %collective-permute-start.14 = (bf16[2,2,128,256]{3,2,1,0:T(8,128)(2,1)S(1)}, bf16[2,2,128,256]{3,2,1,0:T(8,128)(2,1)S(1)}, u32[]{:S(2)}, u32[]{:S(2)}) collective-permute-start(bf16[2,2,128,256]{3,2,1,0:T(8,128)(2,1)S(1)} %collective-permute-done.13.s2), channel_id=1, source_target_pairs={{0,7},{1,2},{2,1},{3,4},{4,3},{5,6},{6,5},{7,0},{8,9},{9,8},{10,11... | collective-permute-start | bytes 786440 | tf_op jit(solution)/shard_map/ppermute | solution.py:64
  42.2 4.3 %collective-permute-done.14.s3 = bf16[2,2,128,256]{3,2,1,0:T(8,128)(2,1)S(1)} collective-permute-done((bf16[2,2,128,256]{3,2,1,0:T(8,128)(2,1)S(1)}, bf16[2,2,128,256]{3,2,1,0:T(8,128)(2,1)S(1)}, u32[]{:S(2)}, u32[]{:S(2)}) %collective-permute-start.14) | collective-permute-done | bytes 262176 | tf_op jit(solution)/shard_map/ppermute | solution.py:64
  49.6 3.6 %collective-permute-done.15 = bf16[4,1024]{1,0:T(4,128)(2,1)S(1)} collective-permute-done((bf16[4,1024]{1,0:T(4,128)(2,1)S(1)}, bf16[4,1024]{1,0:T(4,128)(2,1)S(1)}, u32[]{:S(2)}, u32[]{:S(2)}) %collective-permute-start.15) | collective-permute-done | bytes 8224 | tf_op jit(solution)/shard_map/ppermute | solution.py:56
  53.2 3.2 %collective-permute-start.16 = (bf16[4,1024]{1,0:T(4,128)(2,1)S(1)}, bf16[4,1024]{1,0:T(4,128)(2,1)S(1)}, u32[]{:S(2)}, u32[]{:S(2)}) collective-permute-start(bf16[4,1024]{1,0:T(4,128)(2,1)S(1)} %get-tuple-element.44), channel_id=1, source_target_pairs={{0,5},{1,4},{2,7},{3,6},{4,1},{5,0},{6,3},{7,2},{8,13},{9,12},{10,... | collective-permute-start | bytes 24584 | tf_op jit(solution)/shard_map/ppermute | solution.py:56
  61.0 3.7 %collective-permute-done.18.refs_7_ = bf16[4,1024]{1,0:T(4,128)(2,1)S(1)} collective-permute-done((bf16[4,1024]{1,0:T(4,128)(2,1)S(1)}, bf16[4,1024]{1,0:T(4,128)(2,1)S(1)}, u32[]{:S(2)}, u32[]{:S(2)}) %collective-permute-start.18) | collective-permute-done | bytes 8224 | tf_op jit(solution)/shard_map/ppermute | solution.py:56
  69.3 3.1 %collective-permute-start.20 = (bf16[128,128]{1,0:T(8,128)(2,1)S(1)}, bf16[128,128]{1,0:T(8,128)(2,1)S(1)}, u32[]{:S(2)}, u32[]{:S(2)}) collective-permute-start(bf16[128,128]{1,0:T(8,128)(2,1)S(1)} %fusion.7), channel_id=1, source_target_pairs={{0,16},{8,24},{16,0},{24,8},{32,48},{40,56},{48,32},{56,40},{64,80... | collective-permute-start | bytes 98312 | tf_op jit(solution)/shard_map/ppermute | solution.py:36
  74.7 3.4 %collective-permute-start.24 = (bf16[128,128]{1,0:T(8,128)(2,1)S(1)}, bf16[128,128]{1,0:T(8,128)(2,1)S(1)}, u32[]{:S(2)}, u32[]{:S(2)}) collective-permute-start(bf16[128,128]{1,0:T(8,128)(2,1)S(1)} %get-tuple-element.42), channel_id=1, source_target_pairs={{0,192},{8,200},{16,208},{24,216},{32,224},{40,232},{48,240},{56,2... | collective-permute-start | bytes 98312 | tf_op jit(solution)/shard_map/ppermute | solution.py:40
  80.0 3.5 %collective-permute-done.25.refs_7_ = bf16[128,128]{1,0:T(8,128)(2,1)S(1)} collective-permute-done((bf16[128,128]{1,0:T(8,128)(2,1)S(1)}, bf16[128,128]{1,0:T(8,128)(2,1)S(1)}, u32[]{:S(2)}, u32[]{:S(2)}) %collective-permute-start.25) | collective-permute-done | bytes 32800 | tf_op jit(solution)/shard_map/ppermute | solution.py:40
  85.2 3.2 %collective-permute-done.26 = bf16[2,1024]{1,0:T(2,128)(2,1)S(1)} collective-permute-done((bf16[2,1024]{1,0:T(2,128)(2,1)S(1)}, bf16[2,1024]{1,0:T(2,128)(2,1)S(1)}, u32[]{:S(2)}, u32[]{:S(2)}) %collective-permute-start.26) | collective-permute-done | bytes 4128 | tf_op jit(solution)/shard_map/ppermute | solution.py:56
  91.0 3.0 %collective-permute-start.29 = (bf16[2,1024]{1,0:T(2,128)(2,1)S(1)}, bf16[2,1024]{1,0:T(2,128)(2,1)S(1)}, u32[]{:S(2)}, u32[]{:S(2)}) collective-permute-start(bf16[2,1024]{1,0:T(2,128)(2,1)S(1)} %get-tuple-element.40), channel_id=1, source_target_pairs={{0,6},{1,7},{2,4},{3,5},{4,2},{5,3},{6,0},{7,1},{8,14},{9,15},{10,... | collective-permute-start | bytes 12296 | tf_op jit(solution)/shard_map/ppermute | solution.py:56
  100.9 3.7 %collective-permute-done.30 = bf16[64,128]{1,0:T(8,128)(2,1)S(1)} collective-permute-done((bf16[64,128]{1,0:T(8,128)(2,1)S(1)}, bf16[64,128]{1,0:T(8,128)(2,1)S(1)}, u32[]{:S(2)}, u32[]{:S(2)}) %collective-permute-start.30) | collective-permute-done | bytes 16416 | tf_op jit(solution)/shard_map/ppermute | solution.py:32
  121.0 3.2 %collective-permute-start.37 = (bf16[2,2,128,256]{3,2,1,0:T(8,128)(2,1)S(1)}, bf16[2,2,128,256]{3,2,1,0:T(8,128)(2,1)S(1)}, u32[]{:S(2)}, u32[]{:S(2)}) collective-permute-start(bf16[2,2,128,256]{3,2,1,0:T(8,128)(2,1)S(1)} %get-tuple-element.33), channel_id=1, source_target_pairs={{0,7},{1,2},{2,1},{3,4},{4,3},{5,6},{6,5},{7,0},{8,9},{9,8},{10,11... | collective-permute-start | bytes 786440 | tf_op jit(solution)/shard_map/ppermute | solution.py:64
  126.3 3.7 %collective-permute-done.37 = bf16[2,2,128,256]{3,2,1,0:T(8,128)(2,1)S(1)} collective-permute-done((bf16[2,2,128,256]{3,2,1,0:T(8,128)(2,1)S(1)}, bf16[2,2,128,256]{3,2,1,0:T(8,128)(2,1)S(1)}, u32[]{:S(2)}, u32[]{:S(2)}) %collective-permute-start.37) | collective-permute-done | bytes 262176 | tf_op jit(solution)/shard_map/ppermute | solution.py:64
  130.2 9.0 %collective-permute-done.38 = bf16[2,2,128,256]{3,2,1,0:T(8,128)(2,1)S(1)} collective-permute-done((bf16[2,2,128,256]{3,2,1,0:T(8,128)(2,1)S(1)}, bf16[2,2,128,256]{3,2,1,0:T(8,128)(2,1)S(1)}, u32[]{:S(2)}, u32[]{:S(2)}) %collective-permute-start.38) | collective-permute-done | bytes 262176 | tf_op jit(solution)/shard_map/ppermute | solution.py:64
  139.2 3.6 %collective-permute-start.39 = (bf16[2,2,128,256]{3,2,1,0:T(8,128)(2,1)S(1)}, bf16[2,2,128,256]{3,2,1,0:T(8,128)(2,1)S(1)}, u32[]{:S(2)}, u32[]{:S(2)}) collective-permute-start(bf16[2,2,128,256]{3,2,1,0:T(8,128)(2,1)S(1)} %add_convert_fusion.2), channel_id=1, source_target_pairs={{0,7},{1,2},{2,1},{3,4},{4,3},{5,6},{6,5},{7,0},{8,9},{9,8},{10,11... | collective-permute-start | bytes 786440 | tf_op jit(solution)/shard_map/ppermute | solution.py:64
  148.8 8.1 %collective-permute-done.44 = bf16[8,128,256]{2,1,0:T(8,128)(2,1)S(1)} collective-permute-done((bf16[8,128,256]{2,1,0:T(8,128)(2,1)S(1)}, bf16[8,128,256]{2,1,0:T(8,128)(2,1)S(1)}, u32[]{:S(2)}, u32[]{:S(2)}) %collective-permute-start.44) | collective-permute-done | bytes 524320 | tf_op jit(solution)/shard_map/ppermute | solution.py:44
  156.9 5.8 %collective-permute-done.43 = bf16[8,128,256]{2,1,0:T(8,128)(2,1)S(1)} collective-permute-done((bf16[8,128,256]{2,1,0:T(8,128)(2,1)S(1)}, bf16[8,128,256]{2,1,0:T(8,128)(2,1)S(1)}, u32[]{:S(2)}, u32[]{:S(2)}) %collective-permute-start.43) | collective-permute-done | bytes 524320 | tf_op jit(solution)/shard_map/ppermute | solution.py:44
  (125 shorter events, 72.5 us)
Async XLA Ops:
  4.0 6.5 %collective-permute-start.2 = (bf16[2,128,256]{2,1,0:T(8,128)(2,1)S(1)}, bf16[2,128,256]{2,1,0:T(8,128)(2,1)S(1)}, u32[]{:S(2)}, u32[]{:S(2)}) collective-permute-start(bf16[2,128,256]{2,1,0:T(8,128)(2,1)S(1)} %maximum_select_fusion.2), channel_id=1, source_target_pairs={{0,32},{8,136},{16,48},{24,152},{32,0},{40,168},{48,16},{56,184},{... | collective-permute-start | bytes 393224 | tf_op jit(solution)/shard_map/ppermute | solution.py:44
  11.8 19.5 %collective-permute-start.4 = (bf16[8,128,256]{2,1,0:T(8,128)(2,1)S(1)}, bf16[8,128,256]{2,1,0:T(8,128)(2,1)S(1)}, u32[]{:S(2)}, u32[]{:S(2)}) collective-permute-start(bf16[8,128,256]{2,1,0:T(8,128)(2,1)S(1)} %pad_maximum_fusion.refs_3_), channel_id=1, source_target_pairs={{0,64},{8,24},{16,80},{24,8},{32,96},{40,56},{48,112},{56,40},{64,... | collective-permute-start | bytes 1572872 | tf_op jit(solution)/shard_map/ppermute | solution.py:50
  12.6 19.2 %collective-permute-start.5 = (bf16[8,128,256]{2,1,0:T(8,128)(2,1)S(1)}, bf16[8,128,256]{2,1,0:T(8,128)(2,1)S(1)}, u32[]{:S(2)}, u32[]{:S(2)}) collective-permute-start(bf16[8,128,256]{2,1,0:T(8,128)(2,1)S(1)} %pad_maximum_fusion.refs_3_), channel_id=1, source_target_pairs={{0,128},{8,40},{16,144},{24,56},{32,160},{40,8},{48,176},{56,24},{... | collective-permute-start | bytes 1572872 | tf_op jit(solution)/shard_map/ppermute | solution.py:50
  15.5 16.4 %collective-permute-start.6 = (bf16[8,128,256]{2,1,0:T(8,128)(2,1)S(1)}, bf16[8,128,256]{2,1,0:T(8,128)(2,1)S(1)}, u32[]{:S(2)}, u32[]{:S(2)}) collective-permute-start(bf16[8,128,256]{2,1,0:T(8,128)(2,1)S(1)} %pad_maximum_fusion.refs_3_), channel_id=1, source_target_pairs={{0,192},{8,56},{16,208},{24,40},{32,224},{40,24},{48,240},{56,8},{... | collective-permute-start | bytes 1572872 | tf_op jit(solution)/shard_map/ppermute | solution.py:50
  21.8 9.5 %collective-permute-start.12 = (bf16[2,2,128,256]{3,2,1,0:T(8,128)(2,1)S(1)}, bf16[2,2,128,256]{3,2,1,0:T(8,128)(2,1)S(1)}, u32[]{:S(2)}, u32[]{:S(2)}) collective-permute-start(bf16[2,2,128,256]{3,2,1,0:T(8,128)(2,1)S(1)} %maximum_select_fusion.s0), channel_id=1, source_target_pairs={{0,7},{1,2},{2,1},{3,4},{4,3},{5,6},{6,5},{7,0},{8,9},{9,8},{10,11... | collective-permute-start | bytes 786440 | tf_op jit(solution)/shard_map/ppermute | solution.py:64
  31.3 7.4 %collective-permute-start.13 = (bf16[2,2,128,256]{3,2,1,0:T(8,128)(2,1)S(1)}, bf16[2,2,128,256]{3,2,1,0:T(8,128)(2,1)S(1)}, u32[]{:S(2)}, u32[]{:S(2)}) collective-permute-start(bf16[2,2,128,256]{3,2,1,0:T(8,128)(2,1)S(1)} %collective-permute-done.12.s1), channel_id=1, source_target_pairs={{0,1},{1,0},{2,3},{3,2},{4,5},{5,4},{6,7},{7,6},{8,15},{9,10},{10,... | collective-permute-start | bytes 786440 | tf_op jit(solution)/shard_map/ppermute | solution.py:64
  31.3 15.7 %collective-permute-start.7 = (bf16[8,128,256]{2,1,0:T(8,128)(2,1)S(1)}, bf16[8,128,256]{2,1,0:T(8,128)(2,1)S(1)}, u32[]{:S(2)}, u32[]{:S(2)}) collective-permute-start(bf16[8,128,256]{2,1,0:T(8,128)(2,1)S(1)} %pad_maximum_fusion.refs_3_), channel_id=1, source_target_pairs={{0,8},{8,0},{16,24},{24,16},{32,40},{40,32},{48,56},{56,48},{64,72... | collective-permute-start | bytes 1572872 | tf_op jit(solution)/shard_map/ppermute | solution.py:32
  31.3 15.7 %collective-permute-start.8 = (bf16[8,128,256]{2,1,0:T(8,128)(2,1)S(1)}, bf16[8,128,256]{2,1,0:T(8,128)(2,1)S(1)}, u32[]{:S(2)}, u32[]{:S(2)}) collective-permute-start(bf16[8,128,256]{2,1,0:T(8,128)(2,1)S(1)} %collective-permute-done.4.refs_4_), channel_id=1, source_target_pairs={{0,8},{8,0},{16,24},{24,16},{32,40},{40,32},{48,56},{56,48},{64,72... | collective-permute-start | bytes 1572872 | tf_op jit(solution)/shard_map/ppermute | solution.py:32
  31.8 15.2 %collective-permute-start.9 = (bf16[8,128,256]{2,1,0:T(8,128)(2,1)S(1)}, bf16[8,128,256]{2,1,0:T(8,128)(2,1)S(1)}, u32[]{:S(2)}, u32[]{:S(2)}) collective-permute-start(bf16[8,128,256]{2,1,0:T(8,128)(2,1)S(1)} %collective-permute-done.5.refs_5_), channel_id=1, source_target_pairs={{0,8},{8,0},{16,24},{24,16},{32,40},{40,32},{48,56},{56,48},{64,72... | collective-permute-start | bytes 1572872 | tf_op jit(solution)/shard_map/ppermute | solution.py:32
  31.9 15.1 %collective-permute-start.10 = (bf16[8,128,256]{2,1,0:T(8,128)(2,1)S(1)}, bf16[8,128,256]{2,1,0:T(8,128)(2,1)S(1)}, u32[]{:S(2)}, u32[]{:S(2)}) collective-permute-start(bf16[8,128,256]{2,1,0:T(8,128)(2,1)S(1)} %collective-permute-done.6.refs_6_), channel_id=1, source_target_pairs={{0,8},{8,0},{16,24},{24,16},{32,40},{40,32},{48,56},{56,48},{64,72... | collective-permute-start | bytes 1572872 | tf_op jit(solution)/shard_map/ppermute | solution.py:32
  38.7 7.8 %collective-permute-start.14 = (bf16[2,2,128,256]{3,2,1,0:T(8,128)(2,1)S(1)}, bf16[2,2,128,256]{3,2,1,0:T(8,128)(2,1)S(1)}, u32[]{:S(2)}, u32[]{:S(2)}) collective-permute-start(bf16[2,2,128,256]{3,2,1,0:T(8,128)(2,1)S(1)} %collective-permute-done.13.s2), channel_id=1, source_target_pairs={{0,7},{1,2},{2,1},{3,4},{4,3},{5,6},{6,5},{7,0},{8,9},{9,8},{10,11... | collective-permute-start | bytes 786440 | tf_op jit(solution)/shard_map/ppermute | solution.py:64
  53.2 6.7 %collective-permute-start.16 = (bf16[4,1024]{1,0:T(4,128)(2,1)S(1)}, bf16[4,1024]{1,0:T(4,128)(2,1)S(1)}, u32[]{:S(2)}, u32[]{:S(2)}) collective-permute-start(bf16[4,1024]{1,0:T(4,128)(2,1)S(1)} %get-tuple-element.44), channel_id=1, source_target_pairs={{0,5},{1,4},{2,7},{3,6},{4,1},{5,0},{6,3},{7,2},{8,13},{9,12},{10,... | collective-permute-start | bytes 24584 | tf_op jit(solution)/shard_map/ppermute | solution.py:56
  88.5 6.7 %collective-permute-start.27 = (bf16[2,1024]{1,0:T(2,128)(2,1)S(1)}, bf16[2,1024]{1,0:T(2,128)(2,1)S(1)}, u32[]{:S(2)}, u32[]{:S(2)}) collective-permute-start(bf16[2,1024]{1,0:T(2,128)(2,1)S(1)} %get-tuple-element.40), channel_id=1, source_target_pairs={{0,5},{1,4},{2,7},{3,6},{4,1},{5,0},{6,3},{7,2},{8,13},{9,12},{10,... | collective-permute-start | bytes 12296 | tf_op jit(solution)/shard_map/ppermute | solution.py:56
  88.9 6.2 %collective-permute-start.28 = (bf16[2,1024]{1,0:T(2,128)(2,1)S(1)}, bf16[2,1024]{1,0:T(2,128)(2,1)S(1)}, u32[]{:S(2)}, u32[]{:S(2)}) collective-permute-start(bf16[2,1024]{1,0:T(2,128)(2,1)S(1)} %get-tuple-element.40), channel_id=1, source_target_pairs={{0,2},{1,3},{2,0},{3,1},{4,6},{5,7},{6,4},{7,5},{8,10},{9,11},{10,... | collective-permute-start | bytes 12296 | tf_op jit(solution)/shard_map/ppermute | solution.py:56
  100.3 42.6 %collective-permute-start.41 = (bf16[32,128,256]{2,1,0:T(8,128)(2,1)S(1)}, bf16[32,128,256]{2,1,0:T(8,128)(2,1)S(1)}, u32[]{:S(2)}, u32[]{:S(2)}) collective-permute-start(bf16[32,128,256]{2,1,0:T(8,128)(2,1)S(1)} %get-tuple-element.36), channel_id=1, source_target_pairs={{0,8},{8,0},{16,24},{24,16},{32,40},{40,32},{48,56},{56,48},{64,72... | collective-permute-start | bytes 6291464 | tf_op jit(solution)/shard_map/ppermute | solution.py:32
  121.0 9.1 %collective-permute-start.37 = (bf16[2,2,128,256]{3,2,1,0:T(8,128)(2,1)S(1)}, bf16[2,2,128,256]{3,2,1,0:T(8,128)(2,1)S(1)}, u32[]{:S(2)}, u32[]{:S(2)}) collective-permute-start(bf16[2,2,128,256]{3,2,1,0:T(8,128)(2,1)S(1)} %get-tuple-element.33), channel_id=1, source_target_pairs={{0,7},{1,2},{2,1},{3,4},{4,3},{5,6},{6,5},{7,0},{8,9},{9,8},{10,11... | collective-permute-start | bytes 786440 | tf_op jit(solution)/shard_map/ppermute | solution.py:64
  130.1 9.1 %collective-permute-start.38 = (bf16[2,2,128,256]{3,2,1,0:T(8,128)(2,1)S(1)}, bf16[2,2,128,256]{3,2,1,0:T(8,128)(2,1)S(1)}, u32[]{:S(2)}, u32[]{:S(2)}) collective-permute-start(bf16[2,2,128,256]{3,2,1,0:T(8,128)(2,1)S(1)} %add_convert_fusion.3), channel_id=1, source_target_pairs={{0,1},{1,0},{2,3},{3,2},{4,5},{5,4},{6,7},{7,6},{8,15},{9,10},{10,... | collective-permute-start | bytes 786440 | tf_op jit(solution)/shard_map/ppermute | solution.py:64
  139.2 9.4 %collective-permute-start.39 = (bf16[2,2,128,256]{3,2,1,0:T(8,128)(2,1)S(1)}, bf16[2,2,128,256]{3,2,1,0:T(8,128)(2,1)S(1)}, u32[]{:S(2)}, u32[]{:S(2)}) collective-permute-start(bf16[2,2,128,256]{3,2,1,0:T(8,128)(2,1)S(1)} %add_convert_fusion.2), channel_id=1, source_target_pairs={{0,7},{1,2},{2,1},{3,4},{4,3},{5,6},{6,5},{7,0},{8,9},{9,8},{10,11... | collective-permute-start | bytes 786440 | tf_op jit(solution)/shard_map/ppermute | solution.py:64
  143.8 13.1 %collective-permute-start.44 = (bf16[8,128,256]{2,1,0:T(8,128)(2,1)S(1)}, bf16[8,128,256]{2,1,0:T(8,128)(2,1)S(1)}, u32[]{:S(2)}, u32[]{:S(2)}) collective-permute-start(bf16[8,128,256]{2,1,0:T(8,128)(2,1)S(1)} %get-tuple-element.47), channel_id=1, source_target_pairs={{0,32},{8,136},{16,48},{24,152},{32,0},{40,168},{48,16},{56,184},{... | collective-permute-start | bytes 1572872 | tf_op jit(solution)/shard_map/ppermute | solution.py:44
  145.1 17.6 %collective-permute-start.43 = (bf16[8,128,256]{2,1,0:T(8,128)(2,1)S(1)}, bf16[8,128,256]{2,1,0:T(8,128)(2,1)S(1)}, u32[]{:S(2)}, u32[]{:S(2)}) collective-permute-start(bf16[8,128,256]{2,1,0:T(8,128)(2,1)S(1)} %get-tuple-element.48), channel_id=1, source_target_pairs={{0,48},{8,200},{16,32},{24,216},{32,16},{40,232},{48,0},{56,248},{... | collective-permute-start | bytes 1572872 | tf_op jit(solution)/shard_map/ppermute | solution.py:44
  145.8 17.6 %collective-permute-start.42 = (bf16[8,128,256]{2,1,0:T(8,128)(2,1)S(1)}, bf16[8,128,256]{2,1,0:T(8,128)(2,1)S(1)}, u32[]{:S(2)}, u32[]{:S(2)}) collective-permute-start(bf16[8,128,256]{2,1,0:T(8,128)(2,1)S(1)} %get-tuple-element.46), channel_id=1, source_target_pairs={{0,16},{8,72},{16,0},{24,88},{32,48},{40,104},{48,32},{56,120},{64... | collective-permute-start | bytes 1572872 | tf_op jit(solution)/shard_map/ppermute | solution.py:44
  148.7 18.6 %collective-permute-start.40 = (bf16[2,128,256]{2,1,0:T(8,128)(2,1)S(1)}, bf16[2,128,256]{2,1,0:T(8,128)(2,1)S(1)}, u32[]{:S(2)}, u32[]{:S(2)}) collective-permute-start(bf16[2,128,256]{2,1,0:T(8,128)(2,1)S(1)} %fusion.5), channel_id=1, source_target_pairs={{0,1},{1,0},{2,3},{3,2},{4,5},{5,4},{6,7},{7,6},{8,15},{9,10},{10,... | collective-permute-start | bytes 393224 | tf_op jit(solution)/shard_map/ppermute | solution.py:64
  163.7 6.6 %collective-permute-start.47 = (bf16[2,128,256]{2,1,0:T(8,128)(2,1)S(1)}, bf16[2,128,256]{2,1,0:T(8,128)(2,1)S(1)}, u32[]{:S(2)}, u32[]{:S(2)}) collective-permute-start(bf16[2,128,256]{2,1,0:T(8,128)(2,1)S(1)} %get-tuple-element.50), channel_id=1, source_target_pairs={{0,128},{8,40},{16,144},{24,56},{32,160},{40,8},{48,176},{56,24},{... | collective-permute-start | bytes 393224 | tf_op jit(solution)/shard_map/ppermute | solution.py:50
  165.3 6.4 %collective-permute-start.46 = (bf16[2,128,256]{2,1,0:T(8,128)(2,1)S(1)}, bf16[2,128,256]{2,1,0:T(8,128)(2,1)S(1)}, u32[]{:S(2)}, u32[]{:S(2)}) collective-permute-start(bf16[2,128,256]{2,1,0:T(8,128)(2,1)S(1)} %get-tuple-element.51), channel_id=1, source_target_pairs={{0,192},{8,56},{16,208},{24,40},{32,224},{40,24},{48,240},{56,8},{... | collective-permute-start | bytes 393224 | tf_op jit(solution)/shard_map/ppermute | solution.py:50
  (31 other events, 335.2 us)
